TPU v7x, 32 devices: a whole 2x2x4 slice. The times are simulated.
32 devices in a mesh: dp: 4 (over y, x), ctx: 8 (over z, core).
Axes of the slice: x: 2, y: 2, z: 4, core: 2. Of those that a mesh axis runs over, the one named last changes fastest.
Arguments:
- query_rows: bfloat16 [4096, 4096], P(('dp', 'ctx')), may hold values from -32 to 32
- key_rows: bfloat16 [4096, 512], P(('dp', 'ctx')), may hold values from -8 to 8
- value_rows: bfloat16 [4096, 512], P(('dp', 'ctx')), may hold values from -6 to 6
- out_grad: bfloat16 [4096, 4096], P(('dp', 'ctx')), may hold values from -6 to 6
- destination: int32 [4, 1024], P('dp'), may hold values from 0 to 1023, as said below
- group_first: int32 [4, 8], P('dp', 'ctx'), may hold values from 0 to 7, as said below
Outputs:
- attended: bfloat16 [4096, 4096], P(('dp', 'ctx'))
- grad_query: bfloat16 [4096, 4096], P(('dp', 'ctx'))
- grad_key: bfloat16 [4096, 512], P(('dp', 'ctx'))
- grad_value: bfloat16 [4096, 512], P(('dp', 'ctx'))
- bias_grad: float32 [4608], replicated
Inputs may be any that keep to these rules, and one draw needn't show every extreme that they name: For each replica r, destination[r] is a permutation of 0 to 1023. Of the 128 tokens of one index of ctx, at most 32 take slots in any one block, and in every replica some index and block reach 32. group_first[r, b] equals b where a sequence group begins (always at b = 0) and group_first[r, b - 1] otherwise.
All inputs are finite; a program needn't handle non-finite values.
Results may differ from a plain program's by a relative error of at most 0.008.
Values may be sent and summed in bfloat16 or wider, within the bound.
No kernel may reach another device: no remote copies, remote signals or barrier semaphores. Data moves between devices by JAX's collectives and lax.ppermute only.
A program may use at most 64 MiB of HBM per device.

v0:
```python
import functools
import math

import jax
import jax.numpy as jnp
from jax import lax
from jax.experimental import pallas as pl
from jax.experimental.pallas import tpu as pltpu
from jax.sharding import PartitionSpec as P

HD = 128
GROUP = 8
CORES = 2
EXTRA = 8
BIAS_ROWS = 16
NEG = -1e30
LOG2E = math.log2(math.e)


def nn(left, right):
    return lax.dot_general(
        left, right, (((1,), (0,)), ((), ())), preferred_element_type=jnp.float32
    )


def attention_kernel(
    core_ref,
    slot_query,
    slot_key,
    query_own,
    grad_own,
    far_in,
    pairs,
    *refs,
    carried,
):
    if carried:
        refs = refs[2:]
    attended, grad_query, far_out, parts, bias, key_t, value_t, mask, key_sum, value_sum = refs
    count = pairs.shape[0]
    length = query_own.shape[0]
    keys_total = count * length
    scaling = HD ** (-0.5)
    keys = pairs[:, :length, :].reshape(keys_total, HD)
    values = pairs[:, length : 2 * length, :].reshape(keys_total, HD)
    key_t[...] = keys.T
    value_t[...] = values.T
    slot = slot_query[...]
    block = slot // length
    reach = jnp.zeros_like(slot)
    for b in range(count):
        flag = pairs[b, 2 * length : 2 * length + 1, 0:1].astype(jnp.float32)
        linked = (flag > 0.5).astype(jnp.int32)
        reach = reach + jnp.where(block == b, 1, 0) * linked
    first = (block - reach) * length
    key_slot = slot_key[...]
    mask[...] = jnp.where((key_slot <= slot) & (key_slot >= first), 0.0, NEG)
    key_sum[...] = jnp.zeros_like(key_sum)
    value_sum[...] = jnp.zeros_like(value_sum)
    bias[...] = jnp.zeros_like(bias)

    def one_head(g, _):
        at = pl.ds(pl.multiple_of(g * HD, HD), HD)
        query = jnp.concatenate([query_own[:, at], far_in[0, :, at]], axis=0)
        grad = jnp.concatenate([grad_own[:, at], far_in[1, :, at]], axis=0)
        score = nn(query, key_t[...]) * (scaling * LOG2E) + mask[...]
        raw = jnp.exp2(score - jnp.max(score, axis=1, keepdims=True))
        inverse = 1.0 / jnp.sum(raw, axis=1, keepdims=True)
        press = nn(grad, value_t[...])
        prob = raw * inverse
        centred = jnp.sum(prob * press, axis=1, keepdims=True)
        slope = (prob * (press - centred)).astype(jnp.bfloat16)
        weight = prob.astype(jnp.bfloat16)
        out = nn(weight, pairs[:, length : 2 * length, :].reshape(keys_total, HD)).astype(
            jnp.bfloat16
        )
        into = (nn(slope, pairs[:, :length, :].reshape(keys_total, HD)) * scaling).astype(
            jnp.bfloat16
        )
        attended[:, at] = out[:length]
        grad_query[:, at] = into[:length]
        far_out[0, :, at] = out[length:]
        far_out[1, :, at] = into[length:]
        bias[pl.ds(g, 1), :] = jnp.sum(into.astype(jnp.float32), axis=0, keepdims=True)
        key_sum[...] += nn(query.T, slope)
        value_sum[...] += nn(grad.T, weight)
        return 0

    lax.fori_loop(0, GROUP, one_head, 0)
    from_keys = key_sum[...].T * scaling
    from_values = value_sum[...].T
    bias[GROUP : GROUP + 1, :] = jnp.sum(from_values, axis=0, keepdims=True)
    parts[:, :length, :] = from_keys.astype(jnp.bfloat16).reshape(count, length, HD)
    parts[:, length:, :] = from_values.astype(jnp.bfloat16).reshape(count, length, HD)


def attention(core, chunk, chunks, slot_query, slot_key, query, grad, far_in, pairs, carried):
    count = pairs.shape[0]
    length = query.shape[0]
    wide = GROUP * HD
    whole = lambda *shape: pl.BlockSpec(shape, lambda i, c: (0,) * len(shape))
    mine = pl.BlockSpec((length, wide), lambda i, c: (0, chunks * c[0] + chunk))
    out_shape = [
        jax.ShapeDtypeStruct(query.shape, jnp.bfloat16),
        jax.ShapeDtypeStruct(query.shape, jnp.bfloat16),
        jax.ShapeDtypeStruct((2, length, wide), jnp.bfloat16),
        jax.ShapeDtypeStruct((count, 2 * length, HD), jnp.bfloat16),
        jax.ShapeDtypeStruct((BIAS_ROWS, HD), jnp.float32),
    ]
    rows = CORES * length
    cols = count * length
    in_specs = [
        whole(rows, 1),
        whole(1, cols),
        mine,
        mine,
        whole(2, length, wide),
        whole(*pairs.shape),
    ]
    operands = [slot_query, slot_key, query, grad, far_in, pairs]
    aliases = {}
    if carried is not None:
        in_specs += [pl.BlockSpec(memory_space=pl.ANY)] * 2
        aliases = {7: 0, 8: 1}
        operands += list(carried)
    grid_spec = pltpu.PrefetchScalarGridSpec(
        num_scalar_prefetch=1,
        grid=(1,),
        in_specs=in_specs,
        out_specs=[
            mine,
            mine,
            whole(2, length, wide),
            whole(count, 2 * length, HD),
            whole(BIAS_ROWS, HD),
        ],
        scratch_shapes=[
            pltpu.VMEM((HD, cols), jnp.bfloat16),
            pltpu.VMEM((HD, cols), jnp.bfloat16),
            pltpu.VMEM((rows, cols), jnp.float32),
            pltpu.VMEM((HD, cols), jnp.float32),
            pltpu.VMEM((HD, cols), jnp.float32),
        ],
    )
    work = rows * GROUP * cols
    return pl.pallas_call(
        functools.partial(attention_kernel, carried=carried is not None),
        grid_spec=grid_spec,
        out_shape=out_shape,
        input_output_aliases=aliases,
        compiler_params=pltpu.CompilerParams(vmem_limit_bytes=60 * 1024 * 1024),
        cost_estimate=pl.CostEstimate(
            flops=12 * work * HD, transcendentals=work, bytes_accessed=8 * length * wide * 2
        ),
        name="attention",
    )(core, *operands)


def place_kernel(core_ref, first, second, attended_in, grad_in, attended, grad_query):
    for at, source in enumerate((first, second)):

        @pl.when(pl.program_id(0) == at)
        def _():
            attended[...] = source[0]
            grad_query[...] = source[1]


def place(core, swapped, attended, grad_query):
    chunks = len(swapped)
    _, length, wide = swapped[0].shape
    theirs = pl.BlockSpec((length, wide), lambda i, c: (0, chunks * (1 - c[0]) + i))
    grid_spec = pltpu.PrefetchScalarGridSpec(
        num_scalar_prefetch=1,
        grid=(chunks,),
        in_specs=[pl.BlockSpec((2, length, wide), lambda i, c: (0, 0, 0))] * chunks
        + [pl.BlockSpec(memory_space=pl.ANY)] * 2,
        out_specs=[theirs, theirs],
    )
    return pl.pallas_call(
        place_kernel,
        grid_spec=grid_spec,
        out_shape=[jax.ShapeDtypeStruct(attended.shape, attended.dtype)] * 2,
        input_output_aliases={3: 0, 4: 1},
        name="place",
    )(core, *swapped, attended, grad_query)


def finish_kernel(*refs):
    *pieces, grad_key, grad_value = refs
    chunks = len(pieces)
    length = grad_key.shape[0]
    for hh, piece in enumerate(pieces):
        for c in range(CORES):
            total = piece[c].astype(jnp.float32)
            for z in range(1, piece.shape[0] // CORES):
                total = total + piece[CORES * z + c].astype(jnp.float32)
            total = total.astype(jnp.bfloat16)
            at = slice((c * chunks + hh) * HD, (c * chunks + hh + 1) * HD)
            grad_key[:, at] = total[:length]
            grad_value[:, at] = total[length:]


def finish(pieces, shape):
    return pl.pallas_call(
        finish_kernel,
        out_shape=[jax.ShapeDtypeStruct(shape, jnp.bfloat16)] * 2,
        name="finish",
    )(*pieces)


def doubled(part, axis):
    size = lax.axis_size(axis)
    step = 1
    while step < size:
        part = part + lax.ppermute(part, axis, [(i, i ^ step) for i in range(size)])
        step *= 2
    return part


def local(query_rows, key_rows, value_rows, out_grad, destination, group_first):
    length = query_rows.shape[0]
    devices = lax.axis_size("ctx")
    replicas = lax.axis_size("dp")
    index = lax.axis_index("ctx")
    core = index % CORES
    kv_heads = key_rows.shape[1] // HD
    chunks = kv_heads // CORES
    wide = GROUP * HD
    plan = destination[0]
    flag = jnp.where(group_first[0, 0] < index, 1.0, 0.0).astype(jnp.bfloat16)
    flags = jnp.broadcast_to(flag, (EXTRA, HD))
    across = [(i, i ^ 1) for i in range(devices)]
    core_arg = core.astype(jnp.int32).reshape(1)

    gathered = []
    swapped_in = []
    for hh in range(chunks):
        blocks = []
        for c in range(CORES):
            head = c * chunks + hh
            at = slice(head * HD, (head + 1) * HD)
            blocks.append(jnp.concatenate([key_rows[:, at], value_rows[:, at], flags], axis=0))
        outgoing = jnp.stack(blocks * (devices // CORES))
        gathered.append(lax.all_to_all(outgoing, "ctx", split_axis=0, concat_axis=0, tiled=True))
        start = ((1 - core) * chunks + hh) * wide
        halves = jnp.stack(
            [
                lax.dynamic_slice_in_dim(query_rows, start, wide, axis=1),
                lax.dynamic_slice_in_dim(out_grad, start, wide, axis=1),
            ]
        )
        swapped_in.append(lax.ppermute(halves, "ctx", across))
    slot_own = lax.dynamic_slice_in_dim(plan, index * length, length)
    slot_far = lax.dynamic_slice_in_dim(plan, (index ^ 1) * length, length)
    slot_query = jnp.concatenate([slot_own, slot_far]).reshape(CORES * length, 1)
    slot_key = plan.reshape(1, devices * length)

    carried = None
    returned = []
    swapped_out = []
    sums = []
    for hh in range(chunks):
        attended, grad_query, far, parts, bias = attention(
            core_arg,
            hh,
            chunks,
            slot_query,
            slot_key,
            query_rows,
            out_grad,
            swapped_in[hh],
            gathered[hh],
            carried,
        )
        carried = (attended, grad_query)
        returned.append(lax.all_to_all(parts, "ctx", split_axis=0, concat_axis=0, tiled=True))
        swapped_out.append(lax.ppermute(far, "ctx", across))
        sums.append(bias)
    attended, grad_query = place(core_arg, swapped_out, *carried)
    partial = doubled(jnp.stack(sums), "dp")
    spread = lax.all_to_all(
        jnp.broadcast_to(partial[None], (devices,) + partial.shape),
        "ctx",
        split_axis=0,
        concat_axis=0,
        tiled=True,
    )
    grad_key, grad_value = finish(returned, key_rows.shape)
    total = jnp.sum(spread.reshape((devices // CORES, CORES) + partial.shape), axis=0)
    total = total.reshape(kv_heads, BIAS_ROWS, HD)
    bias_grad = jnp.concatenate(
        [total[:, :GROUP].reshape(-1), total[:, GROUP].reshape(-1)]
    ) * (1.0 / math.sqrt(length * devices * replicas))
    return (attended, grad_query, grad_key, grad_value, bias_grad)


def solution(mesh):
    rows = P(("dp", "ctx"), None)
    return jax.shard_map(
        local,
        mesh=mesh,
        in_specs=(rows, rows, rows, rows, P("dp", None), P("dp", "ctx")),
        out_specs=(rows, rows, rows, rows, P()),
        check_vma=False,
    )
```

profile of v0, /device:TPU:0, one launch (start us, length us, event | category | flops | bytes accessed | tf_op | source)
XLA Modules:
  0.0 129.6 jit_solution(6438941253307113175)
XLA Ops:
  1.3 0.9 fusion.3
  2.2 0.7 constant_dynamic-update-slice_fusion.15
  2.9 0.7 constant_dynamic-update-slice_fusion.14
  3.7 0.7 constant_dynamic-update-slice_fusion.13
  4.4 0.7 constant_dynamic-update-slice_fusion.12
  5.1 0.7 constant_dynamic-update-slice_fusion.11
  5.8 0.7 constant_dynamic-update-slice_fusion.10
  6.6 0.7 constant_dynamic-update-slice_fusion.9
  7.3 0.8 constant_dynamic-update-slice_fusion.8
  8.0 0.0 copy-start.6
  8.1 0.7 constant_dynamic-update-slice_fusion.6
  8.8 0.7 constant_dynamic-update-slice_fusion.5
  9.5 0.7 constant_dynamic-update-slice_fusion.4
  10.3 0.7 constant_dynamic-update-slice_fusion.3
  11.0 0.7 constant_dynamic-update-slice_fusion.2
  11.7 0.7 constant_dynamic-update-slice_fusion.1
  12.5 0.7 constant_dynamic-update-slice_fusion
  13.2 6.4 %all-to-all-start = ((bf16[8,264,128]{2,1,0:T(8,128)(2,1)}), bf16[8,264,128]{2,1,0:T(8,128)(2,1)S(1)}, u32[]{:S(2)}, u32[]{:S(2)}) async-start(bf16[8,264,128]{2,1,0:T(8,128)(2,1)} %constant_dynamic-update-slice_fusion), calls=%async_computation | async-start | bytes 1081344 | tf_op jit(solution)/shard_map/all_to_all | solution.py:244
  19.5 0.0 copy-done.6
  19.5 1.1 dynamic-slice_bitcast_fusion
  20.7 14.6 %all-to-all-done.pairs = bf16[8,264,128]{2,1,0:T(8,128)(2,1)S(1)} async-done(((bf16[8,264,128]{2,1,0:T(8,128)(2,1)}), bf16[8,264,128]{2,1,0:T(8,128)(2,1)S(1)}, u32[]{:S(2)}, u32[]{:S(2)}) %all-to-all-start) | async-done | bytes 540704 | tf_op jit(solution)/shard_map/all_to_all | solution.py:244
  35.2 0.0 copy-start.1
  35.2 0.8 copy-done.1
  36.1 3.5 %all-to-all-start.1 = ((bf16[8,264,128]{2,1,0:T(8,128)(2,1)}), bf16[8,264,128]{2,1,0:T(8,128)(2,1)S(1)}, u32[]{:S(2)}, u32[]{:S(2)}) async-start(bf16[8,264,128]{2,1,0:T(8,128)(2,1)} %get-tuple-element.47), calls=%async_computation.1 | async-start | bytes 1081344 | tf_op jit(solution)/shard_map/all_to_all | solution.py:244
  39.6 0.1 pad_maximum_fusion
  39.7 0.5 collective-permute-start
  40.1 0.1 pad_maximum_fusion.1
  40.2 0.2 collective-permute-start.2
  40.3 0.7 fusion
  41.0 0.8 copy.17.slot_query
  41.8 0.0 collective-permute-done.far_in
  41.8 0.0 copy-start.11
  41.8 0.8 copy-done.11
  42.6 12.3 %attention.2 = (bf16[128,4096]{1,0:T(8,128)(2,1)}, bf16[128,4096]{1,0:T(8,128)(2,1)}, bf16[2,128,1024]{2,1,0:T(8,128)(2,1)}, bf16[8,256,128]{2,1,0:T(8,128)(2,1)}, f32[16,128]{1,0:T(8,128)}) custom-call(s32[1]{0:T(128)} %bitcast.core_ref, s32[256,1]{1,0:T(8,128)} %copy.17.slot_query, s32[1,1024]{1,0:T(1,128)} %slot_key.3, bf16[128,4096]{1,0:T(8,128)(2,1)} %query_own.3, ...), custom_call_target="tpu_custom_call" | custom-call | flops 3221225472 | bytes 2097152 | tf_op jit(solution)/shard_map/attention/pallas_call | solution.py:146
  54.9 0.0 collective-permute-done.2.far_in
  54.9 0.3 all-to-all-done.1.pairs
  55.2 0.5 copy-done.10
  55.7 0.3 copy-done.2
  56.0 12.3 %attention.3 = (bf16[128,4096]{1,0:T(8,128)(2,1)}, bf16[128,4096]{1,0:T(8,128)(2,1)}, bf16[2,128,1024]{2,1,0:T(8,128)(2,1)}, bf16[8,256,128]{2,1,0:T(8,128)(2,1)}, f32[16,128]{1,0:T(8,128)}) custom-call(s32[1]{0:T(128)} %bitcast.core_ref, s32[256,1]{1,0:T(8,128)} %copy.17.slot_query, ...), custom_call_target="tpu_custom_call", output_to_operand_aliasing={{0}: (7, {}), {1}: (8, {})} | custom-call | flops 3221225472 | bytes 2097152 | tf_op jit(solution)/shard_map/attention/pallas_call | solution.py:146
  68.3 0.0 copy-done.7
  68.3 0.8 pad_maximum_fusion.2
  69.1 1.5 %collective-permute-start.4 = (f32[2,16,128]{2,1,0:T(8,128)S(1)}, f32[2,16,128]{2,1,0:T(8,128)S(1)}, u32[]{:S(2)}, u32[]{:S(2)}) collective-permute-start(f32[2,16,128]{2,1,0:T(8,128)S(1)} %pad_maximum_fusion.2), channel_id=1, source_target_pairs={{0,8},{8,0},{16,24},{24,16},{1,9},{9,1},{17,25},{25,17},{2,10},{10... | collective-permute-start | bytes 49160 | tf_op jit(solution)/shard_map/ppermute | solution.py:215
  70.6 2.2 %collective-permute-done.4 = f32[2,16,128]{2,1,0:T(8,128)S(1)} collective-permute-done((f32[2,16,128]{2,1,0:T(8,128)S(1)}, f32[2,16,128]{2,1,0:T(8,128)S(1)}, u32[]{:S(2)}, u32[]{:S(2)}) %collective-permute-start.4) | collective-permute-done | bytes 16416 | tf_op jit(solution)/shard_map/ppermute | solution.py:215
  72.8 0.7 fusion.2
  73.5 1.5 %collective-permute-start.5 = (f32[2,16,128]{2,1,0:T(8,128)S(1)}, f32[2,16,128]{2,1,0:T(8,128)S(1)}, u32[]{:S(2)}, u32[]{:S(2)}) collective-permute-start(f32[2,16,128]{2,1,0:T(8,128)S(1)} %fusion.2), channel_id=1, source_target_pairs={{0,16},{8,24},{16,0},{24,8},{1,17},{9,25},{17,1},{25,9},{2,18},{10... | collective-permute-start | bytes 49160 | tf_op jit(solution)/shard_map/ppermute | solution.py:215
  75.0 2.2 %collective-permute-done.5 = f32[2,16,128]{2,1,0:T(8,128)S(1)} collective-permute-done((f32[2,16,128]{2,1,0:T(8,128)S(1)}, f32[2,16,128]{2,1,0:T(8,128)S(1)}, u32[]{:S(2)}, u32[]{:S(2)}) %collective-permute-start.5) | collective-permute-done | bytes 16416 | tf_op jit(solution)/shard_map/ppermute | solution.py:215
  77.3 0.7 fusion.5
  78.0 11.5 %all_to_all.25 = f32[8,2,16,128]{3,2,1,0:T(8,128)S(1)} all-to-all(f32[8,2,16,128]{3,2,1,0:T(8,128)S(1)} %broadcast_in_dim.10), channel_id=1, replica_groups=mesh['dp'=4,'ctx'=8] {'ctx'}, dimensions={0} | all-to-all | bytes 262144 | tf_op jit(solution)/shard_map/all_to_all | solution.py:281
  89.5 0.0 copy-done.3
  89.5 18.4 %all_to_all.26.refs_0_ = bf16[8,256,128]{2,1,0:T(8,128)(2,1)} all-to-all(bf16[8,256,128]{2,1,0:T(8,128)(2,1)S(1)} %copy-done.3), channel_id=1, replica_groups=mesh['dp'=4,'ctx'=8] {'ctx'}, dimensions={0} | all-to-all | bytes 1048576 | tf_op jit(solution)/shard_map/all_to_all | solution.py:276
  107.9 3.6 %all-to-all-start.3 = ((bf16[8,256,128]{2,1,0:T(8,128)(2,1)}), bf16[8,256,128]{2,1,0:T(8,128)(2,1)S(1)}, u32[]{:S(2)}, u32[]{:S(2)}) async-start(bf16[8,256,128]{2,1,0:T(8,128)(2,1)} %get-tuple-element.28), calls=%async_computation.3 | async-start | bytes 1048576 | tf_op jit(solution)/shard_map/all_to_all | solution.py:276
  111.5 0.0 copy-done.8
  111.5 0.4 collective-permute-start.1
  111.9 0.0 copy-done.9
  111.9 0.2 collective-permute-start.3
  112.1 0.6 maximum_multiply_fusion
  112.7 0.9 collective-permute-done.1.first
  113.6 0.7 collective-permute-done.3.second
  114.3 0.1 copy-done.4
  114.4 0.7 copy-done.5
  115.1 2.2 %place.1 = (bf16[128,4096]{1,0:T(8,128)(2,1)}, bf16[128,4096]{1,0:T(8,128)(2,1)}) custom-call(s32[1]{0:T(128)} %bitcast.core_ref, bf16[2,128,1024]{2,1,0:T(8,128)(2,1)} %copy-done.4, bf16[2,128,1024]{2,1,0:T(8,128)(2,1)} %copy-done.5, bf16[128,4096]{1,0:T(8,128)(2,1)} %get-tuple-element.23.attended_in, ...), custom_call_target="tpu_custom_call", output_to_operand_aliasing={{0}: (3, {}), {1}: (4, {})} | custom-call | tf_op jit(solution)/shard_map/place/pallas_call | solution.py:179
  117.3 9.4 %all-to-all-done.3.refs_1_ = bf16[8,256,128]{2,1,0:T(8,128)(2,1)S(1)} async-done(((bf16[8,256,128]{2,1,0:T(8,128)(2,1)}), bf16[8,256,128]{2,1,0:T(8,128)(2,1)S(1)}, u32[]{:S(2)}, u32[]{:S(2)}) %all-to-all-start.3) | async-done | bytes 524320 | tf_op jit(solution)/shard_map/all_to_all | solution.py:276
  126.7 0.8 copy-done
  127.6 2.0 %finish.1 = (bf16[128,512]{1,0:T(8,128)(2,1)}, bf16[128,512]{1,0:T(8,128)(2,1)}) custom-call(bf16[8,256,128]{2,1,0:T(8,128)(2,1)} %all_to_all.26.refs_0_, bf16[8,256,128]{2,1,0:T(8,128)(2,1)} %copy-done), custom_call_target="tpu_custom_call" | custom-call | tf_op jit(solution)/shard_map/finish/pallas_call | solution.py:204
  (16 shorter events, 0.1 us)
Async XLA Ops:
  8.0 11.5 %copy-start.6 = (bf16[128,4096]{1,0:T(8,128)(2,1)S(1)}, bf16[128,4096]{1,0:T(8,128)(2,1)}, u32[]{:S(2)}) copy-start(bf16[128,4096]{1,0:T(8,128)(2,1)} %query_own.3) | copy-start | bytes 3145732
  13.2 22.0 %all-to-all-start = ((bf16[8,264,128]{2,1,0:T(8,128)(2,1)}), bf16[8,264,128]{2,1,0:T(8,128)(2,1)S(1)}, u32[]{:S(2)}, u32[]{:S(2)}) async-start(bf16[8,264,128]{2,1,0:T(8,128)(2,1)} %constant_dynamic-update-slice_fusion), calls=%async_computation | async-start | bytes 1081344 | tf_op jit(solution)/shard_map/all_to_all | solution.py:244
  35.2 0.8 copy-start.1
  36.1 19.1 %all-to-all-start.1 = ((bf16[8,264,128]{2,1,0:T(8,128)(2,1)}), bf16[8,264,128]{2,1,0:T(8,128)(2,1)S(1)}, u32[]{:S(2)}, u32[]{:S(2)}) async-start(bf16[8,264,128]{2,1,0:T(8,128)(2,1)} %get-tuple-element.47), calls=%async_computation.1 | async-start | bytes 1081344 | tf_op jit(solution)/shard_map/all_to_all | solution.py:244
  39.7 2.2 %collective-permute-start = (bf16[2,128,1024]{2,1,0:T(8,128)(2,1)S(1)}, bf16[2,128,1024]{2,1,0:T(8,128)(2,1)S(1)}, u32[]{:S(2)}, u32[]{:S(2)}) collective-permute-start(bf16[2,128,1024]{2,1,0:T(8,128)(2,1)S(1)} %pad_maximum_fusion), channel_id=1, source_target_pairs={{0,1},{1,0},{2,3},{3,2},{4,5},{5,4},{6,7},{7,6},{8,9},{9,8},{10,11... | collective-permute-start | bytes 1572872 | tf_op jit(solution)/shard_map/ppermute | solution.py:252
  40.2 14.8 %collective-permute-start.2 = (bf16[2,128,1024]{2,1,0:T(8,128)(2,1)S(1)}, bf16[2,128,1024]{2,1,0:T(8,128)(2,1)S(1)}, u32[]{:S(2)}, u32[]{:S(2)}) collective-permute-start(bf16[2,128,1024]{2,1,0:T(8,128)(2,1)S(1)} %pad_maximum_fusion.1), channel_id=1, source_target_pairs={{0,1},{1,0},{2,3},{3,2},{4,5},{5,4},{6,7},{7,6},{8,9},{9,8},{10,11... | collective-permute-start | bytes 1572872 | tf_op jit(solution)/shard_map/ppermute | solution.py:252
  41.8 0.8 copy-start.11
  54.9 0.8 copy-start.10
  55.2 0.8 copy-start.2
  56.0 12.3 %copy-start.7 = (f32[16,128]{1,0:T(8,128)S(1)}, f32[16,128]{1,0:T(8,128)}, u32[]{:S(2)}) copy-start(f32[16,128]{1,0:T(8,128)} %get-tuple-element.31) | copy-start | bytes 24580
  68.3 21.1 %copy-start.3 = (bf16[8,256,128]{2,1,0:T(8,128)(2,1)S(1)}, bf16[8,256,128]{2,1,0:T(8,128)(2,1)}, u32[]{:S(2)}) copy-start(bf16[8,256,128]{2,1,0:T(8,128)(2,1)} %get-tuple-element.27) | copy-start | bytes 1572868
  69.1 3.7 %collective-permute-start.4 = (f32[2,16,128]{2,1,0:T(8,128)S(1)}, f32[2,16,128]{2,1,0:T(8,128)S(1)}, u32[]{:S(2)}, u32[]{:S(2)}) collective-permute-start(f32[2,16,128]{2,1,0:T(8,128)S(1)} %pad_maximum_fusion.2), channel_id=1, source_target_pairs={{0,8},{8,0},{16,24},{24,16},{1,9},{9,1},{17,25},{25,17},{2,10},{10... | collective-permute-start | bytes 49160 | tf_op jit(solution)/shard_map/ppermute | solution.py:215
  73.5 3.7 %collective-permute-start.5 = (f32[2,16,128]{2,1,0:T(8,128)S(1)}, f32[2,16,128]{2,1,0:T(8,128)S(1)}, u32[]{:S(2)}, u32[]{:S(2)}) collective-permute-start(f32[2,16,128]{2,1,0:T(8,128)S(1)} %fusion.2), channel_id=1, source_target_pairs={{0,16},{8,24},{16,0},{24,8},{1,17},{9,25},{17,1},{25,9},{2,18},{10... | collective-permute-start | bytes 49160 | tf_op jit(solution)/shard_map/ppermute | solution.py:215
  107.8 3.6 %copy-start.8 = (bf16[2,128,1024]{2,1,0:T(8,128)(2,1)S(1)}, bf16[2,128,1024]{2,1,0:T(8,128)(2,1)}, u32[]{:S(2)}) copy-start(bf16[2,128,1024]{2,1,0:T(8,128)(2,1)} %get-tuple-element.19) | copy-start | bytes 1572868
  107.9 4.0 %copy-start.9 = (bf16[2,128,1024]{2,1,0:T(8,128)(2,1)S(1)}, bf16[2,128,1024]{2,1,0:T(8,128)(2,1)}, u32[]{:S(2)}) copy-start(bf16[2,128,1024]{2,1,0:T(8,128)(2,1)} %get-tuple-element.22) | copy-start | bytes 1572868
  107.9 18.9 %all-to-all-start.3 = ((bf16[8,256,128]{2,1,0:T(8,128)(2,1)}), bf16[8,256,128]{2,1,0:T(8,128)(2,1)S(1)}, u32[]{:S(2)}, u32[]{:S(2)}) async-start(bf16[8,256,128]{2,1,0:T(8,128)(2,1)} %get-tuple-element.28), calls=%async_computation.3 | async-start | bytes 1048576 | tf_op jit(solution)/shard_map/all_to_all | solution.py:276
  111.5 2.1 %collective-permute-start.1 = (bf16[2,128,1024]{2,1,0:T(8,128)(2,1)S(1)}, bf16[2,128,1024]{2,1,0:T(8,128)(2,1)S(1)}, u32[]{:S(2)}, u32[]{:S(2)}) collective-permute-start(bf16[2,128,1024]{2,1,0:T(8,128)(2,1)S(1)} %copy-done.8), channel_id=1, source_target_pairs={{0,1},{1,0},{2,3},{3,2},{4,5},{5,4},{6,7},{7,6},{8,9},{9,8},{10,11... | collective-permute-start | bytes 1572872 | tf_op jit(solution)/shard_map/ppermute | solution.py:277
  111.9 2.4 %collective-permute-start.3 = (bf16[2,128,1024]{2,1,0:T(8,128)(2,1)S(1)}, bf16[2,128,1024]{2,1,0:T(8,128)(2,1)S(1)}, u32[]{:S(2)}, u32[]{:S(2)}) collective-permute-start(bf16[2,128,1024]{2,1,0:T(8,128)(2,1)S(1)} %copy-done.9), channel_id=1, source_target_pairs={{0,1},{1,0},{2,3},{3,2},{4,5},{5,4},{6,7},{7,6},{8,9},{9,8},{10,11... | collective-permute-start | bytes 1572872 | tf_op jit(solution)/shard_map/ppermute | solution.py:277
  113.6 0.8 copy-start.4
  114.3 0.8 copy-start.5
  126.7 0.8 copy-start
where the time goes:
time: 130 us
  waiting for transfers between devices  30.3 us (23%)
  blocking collectives  29.9 us (23%)
  Pallas kernels  28.8 us (22%)
  starting transfers between devices  17.8 us (14%)
  other arithmetic  13.9 us (11%)
  local copies, waits for them, and re-layouts  7.61 us (6%)
  between operations  1.41 us (1%)
    pallas_call x2, Pallas kernels, attention(): pl.pallas_call(functools.partial(attention_kernel, carried=carried is not...  24.6 us
    all_to_all x1, blocking collectives, local(): lax.all_to_all(parts, 'ctx', split_axis=0, concat_axis=0, tiled=True)  18.4 us
    all_to_all x2, waiting for transfers between devices, local(): lax.all_to_all(outgoing, 'ctx', split_axis=0, concat_axis=0, tiled=True)  14.8 us
    all_to_all x1, blocking collectives, local(): lax.all_to_all(jnp.broadcast_to(partial[None], (devices,) + partial.shape...  11.5 us
    all_to_all x2, starting transfers between devices, local(): lax.all_to_all(outgoing, 'ctx', split_axis=0, concat_axis=0, tiled=True)  9.89 us
    unnamed x13, other arithmetic  9.47 us
    all_to_all x1, waiting for transfers between devices, local(): lax.all_to_all(parts, 'ctx', split_axis=0, concat_axis=0, tiled=True)  9.4 us
    ppermute x2, waiting for transfers between devices, doubled(): part = part + lax.ppermute(part, axis, [(i, i ^ step) for i in range(size)])  4.45 us
  transfers between devices with their start and end apart: 9, of which 7 were waited for; matrix products, arithmetic and copies ran while one was open for 3% of the time, Pallas kernels for 11%

commit v1 on v0

v1 whole, which is shorter than its diff:
```python
import functools
import math

import jax
import jax.numpy as jnp
from jax import lax
from jax.experimental import pallas as pl
from jax.experimental.pallas import tpu as pltpu
from jax.sharding import PartitionSpec as P


HD = 128
GROUP = 8
CORES = 2
EXTRA = 8
BIAS_ROWS = 16
NEG = -1e30
SPLIT = (True, False)
LOG2E = math.log2(math.e)


def nn(left, right):
    return lax.dot_general(
        left, right, (((1,), (0,)), ((), ())), preferred_element_type=jnp.float32
    )


def column(row):
    length = row.shape[1]
    down = lax.broadcasted_iota(jnp.int32, (length, length), 0)
    along = lax.broadcasted_iota(jnp.int32, (length, length), 1)
    spread = jnp.where(down == along, row.astype(jnp.float32), 0.0)
    return jnp.sum(spread, axis=1, keepdims=True).astype(jnp.int32)


def attention_kernel(index_ref, plan, query_own, grad_own, far_in, *refs, carried, split):
    chips = plan.shape[0] // CORES
    pairs = refs[:chips]
    refs = refs[chips + (4 if carried else 0) :]
    attended, grad_query, bias, far_out = refs[:4]
    parts = refs[4 : 4 + (chips if split else 1)]
    key_t, value_t, mask, key_sum, value_sum, *work = refs[4 + len(parts) :]
    score_refs, press_refs, weight_refs, slope_refs = (work[k : k + 2] for k in (0, 2, 4, 6))
    count = plan.shape[0]
    length = query_own.shape[0]
    scaling = HD ** (-0.5)

    def gathered(start):
        found = [p[j, start : start + length, :] for p in pairs for j in range(CORES)]
        return jnp.concatenate(found, axis=0)

    key_t[...] = gathered(0).T
    value_t[...] = gathered(length).T
    index = index_ref[0]
    slot = jnp.concatenate(
        [column(plan[pl.ds(index, 1), :]), column(plan[pl.ds(index ^ 1, 1), :])], axis=0
    )
    block = slot // length
    reach = jnp.zeros_like(slot)
    for r in range(count):
        flag = pairs[r // CORES][r % CORES, 2 * length : 2 * length + 1, 0:1]
        linked = (flag.astype(jnp.float32) > 0.5).astype(jnp.int32)
        reach = reach + jnp.where(block == (index ^ r), 1, 0) * linked
    first = (block - reach) * length
    for r in range(count):
        key_slot = plan[pl.ds(index ^ r, 1), :]
        mask[:, r * length : (r + 1) * length] = jnp.where(
            (key_slot <= slot) & (key_slot >= first), 0.0, NEG
        )
    key_sum[...] = jnp.zeros_like(key_sum)
    value_sum[...] = jnp.zeros_like(value_sum)
    bias[...] = jnp.zeros_like(bias)

    def pick(own, far, g):
        at = pl.ds(pl.multiple_of(g * HD, HD), HD)
        return jnp.concatenate([own[:, at], far_in[far, :, at]], axis=0)

    def before(g, s):
        score_refs[s][...] = nn(pick(query_own, 0, g), key_t[...])
        press_refs[s][...] = nn(pick(grad_own, 1, g), value_t[...])

    def during(s):
        for r in range(0, 2 * length, 32):
            rows = slice(r, r + 32)
            score = score_refs[s][rows, :] * (scaling * LOG2E) + mask[rows, :]
            raw = jnp.exp2(score - jnp.max(score, axis=1, keepdims=True))
            prob = raw * (1.0 / jnp.sum(raw, axis=1, keepdims=True))
            press = press_refs[s][rows, :]
            centred = jnp.sum(prob * press, axis=1, keepdims=True)
            weight_refs[s][rows, :] = prob.astype(jnp.bfloat16)
            slope_refs[s][rows, :] = (prob * (press - centred)).astype(jnp.bfloat16)

    def after(g, s):
        at = pl.ds(pl.multiple_of(g * HD, HD), HD)
        weight = weight_refs[s][...]
        slope = slope_refs[s][...]
        out = nn(weight, gathered(length)).astype(jnp.bfloat16)
        into = (nn(slope, gathered(0)) * scaling).astype(jnp.bfloat16)
        attended[:, at] = out[:length]
        grad_query[:, at] = into[:length]
        far_out[0, :, at] = out[length:]
        far_out[1, :, at] = into[length:]
        bias[pl.ds(g, 1), :] = jnp.sum(into.astype(jnp.float32), axis=0, keepdims=True)
        key_sum[...] += nn(pick(query_own, 0, g).T, slope)
        value_sum[...] += nn(pick(grad_own, 1, g).T, weight)


    def two_heads(j, _):
        g = 2 * j
        before(g, 0)
        before(g + 1, 1)
        during(0)
        during(1)
        after(g, 0)
        after(g + 1, 1)
        return 0

    lax.fori_loop(0, GROUP // 2, two_heads, 0)

    from_keys = key_sum[...].T * scaling
    from_values = value_sum[...].T
    bias[GROUP : GROUP + 1, :] = jnp.sum(from_values, axis=0, keepdims=True)
    for r in range(count):
        rows = slice(r * length, (r + 1) * length)
        both = jnp.concatenate([from_keys[rows], from_values[rows]], axis=0)
        both = both.astype(jnp.bfloat16)
        if split:
            parts[r // CORES][r % CORES] = both
        else:
            parts[0][pl.ds(index ^ r, 1)] = both[None]


def attention(index, chunk, chunks, plan, query, grad, far_in, pairs, carried, split):
    count = plan.shape[0]
    chips = count // CORES
    length = query.shape[0]
    wide = GROUP * HD
    whole = lambda *shape: pl.BlockSpec(shape, lambda i, c: (0,) * len(shape))
    mine = pl.BlockSpec((length, wide), lambda i, c: (0, chunks * (c[0] % CORES) + chunk))
    out_shape = [
        jax.ShapeDtypeStruct(query.shape, jnp.bfloat16),
        jax.ShapeDtypeStruct(query.shape, jnp.bfloat16),
        jax.ShapeDtypeStruct((chunks * BIAS_ROWS, HD), jnp.float32),
        jax.ShapeDtypeStruct((2, length, chunks * wide), jnp.bfloat16),
    ]
    part = (CORES, 2 * length, HD) if split else (count, 2 * length, HD)
    parts = chips if split else 1
    out_shape += [jax.ShapeDtypeStruct(part, jnp.bfloat16)] * parts
    rows = CORES * length
    cols = count * length
    far = pl.BlockSpec((2, length, wide), lambda i, c: (0, 0, chunk))
    in_specs = [whole(*plan.shape), mine, mine, far]
    in_specs += [whole(*pairs[0].shape)] * chips
    operands = [plan, query, grad, far_in, *pairs]
    aliases = {}
    if carried is not None:
        in_specs += [pl.BlockSpec(memory_space=pl.ANY)] * 4
        aliases = {5 + chips + k: k for k in range(4)}
        operands += list(carried)
    grid_spec = pltpu.PrefetchScalarGridSpec(
        num_scalar_prefetch=1,
        grid=(1,),
        in_specs=in_specs,
        out_specs=[
            mine,
            mine,
            pl.BlockSpec((BIAS_ROWS, HD), lambda i, c: (chunk, 0)),
            far,
        ]
        + [whole(*part)] * parts,
        scratch_shapes=[
            pltpu.VMEM((HD, cols), jnp.bfloat16),
            pltpu.VMEM((HD, cols), jnp.bfloat16),
            pltpu.VMEM((rows, cols), jnp.float32),
            pltpu.VMEM((HD, cols), jnp.float32),
            pltpu.VMEM((HD, cols), jnp.float32),
        ]
        + [pltpu.VMEM((rows, cols), jnp.float32)] * 4
        + [pltpu.VMEM((rows, cols), jnp.bfloat16)] * 4
        + [
        ],
    )
    work = rows * GROUP * cols
    return pl.pallas_call(
        functools.partial(attention_kernel, carried=carried is not None, split=split),
        grid_spec=grid_spec,
        out_shape=out_shape,
        input_output_aliases=aliases,
        compiler_params=pltpu.CompilerParams(
            vmem_limit_bytes=min(60, 8 + 10 * cols // 1024) * 1024 * 1024
        ),
        cost_estimate=pl.CostEstimate(
            flops=12 * work * HD, transcendentals=work, bytes_accessed=8 * length * wide * 2
        ),
        name="attention",
    )(index, *operands)


def payload_kernel(index_ref, first_ref, keys, values, near, away):
    chunks, _, _ = near.shape
    length = keys.shape[0]
    index = index_ref[0]
    linked = (first_ref[0, 0] < index).astype(jnp.float32)
    flags = jnp.full((EXTRA, HD), linked, jnp.float32).astype(jnp.bfloat16)
    even = index % CORES == 0
    for hh in range(chunks):
        heads = [slice((c * chunks + hh) * HD, (c * chunks + hh + 1) * HD) for c in range(CORES)]
        for at, source in ((0, keys), (length, values)):
            first, second = source[:, heads[0]], source[:, heads[1]]
            near[hh, at : at + length, :] = jnp.where(even, first, second)
            away[hh, at : at + length, :] = jnp.where(even, second, first)
        near[hh, 2 * length :, :] = flags
        away[hh, 2 * length :, :] = flags


def payload(index, group_first, keys, values, chunks):
    length = keys.shape[0]
    smem = pl.BlockSpec(memory_space=pltpu.SMEM)
    vmem = pl.BlockSpec(memory_space=pltpu.VMEM)
    shape = jax.ShapeDtypeStruct((chunks, 2 * length + EXTRA, HD), jnp.bfloat16)
    return pl.pallas_call(
        payload_kernel,
        in_specs=[smem, smem, vmem, vmem],
        out_shape=[shape] * 2,
        name="payload",
    )(index, group_first, keys, values)


def join_kernel(near, away, *outs):
    for hh, out in enumerate(outs):
        out[0] = near[hh]
        out[1] = away[hh]


def join(near, away):
    chunks, rows, _ = near.shape
    shape = jax.ShapeDtypeStruct((CORES, rows, HD), jnp.bfloat16)
    return pl.pallas_call(join_kernel, out_shape=[shape] * chunks, name="join")(near, away)


def place_kernel(index_ref, far, attended_in, grad_in, attended, grad_query):
    attended[...] = far[0]
    grad_query[...] = far[1]


def place(index, far, attended, grad_query):
    _, length, half = far.shape
    theirs = pl.BlockSpec((length, half), lambda i, c: (0, 1 - c[0] % CORES))
    grid_spec = pltpu.PrefetchScalarGridSpec(
        num_scalar_prefetch=1,
        grid=(1,),
        in_specs=[pl.BlockSpec((2, length, half), lambda i, c: (0, 0, 0))]
        + [pl.BlockSpec(memory_space=pl.ANY)] * 2,
        out_specs=[theirs, theirs],
    )
    return pl.pallas_call(
        place_kernel,
        grid_spec=grid_spec,
        out_shape=[jax.ShapeDtypeStruct(attended.shape, attended.dtype)] * 2,
        input_output_aliases={2: 0, 3: 1},
        compiler_params=pltpu.CompilerParams(vmem_limit_bytes=8 * 1024 * 1024),
        name="place",
    )(index, far, attended, grad_query)


def halves_kernel(index_ref, query, grad, out):
    out[0] = query[...]
    out[1] = grad[...]


def halves(index, query, grad):
    length, width = query.shape
    theirs = pl.BlockSpec((length, width // CORES), lambda i, c: (0, 1 - c[0] % CORES))
    grid_spec = pltpu.PrefetchScalarGridSpec(
        num_scalar_prefetch=1,
        grid=(1,),
        in_specs=[theirs, theirs],
        out_specs=pl.BlockSpec((2, length, width // CORES), lambda i, c: (0, 0, 0)),
    )
    return pl.pallas_call(
        halves_kernel,
        grid_spec=grid_spec,
        out_shape=jax.ShapeDtypeStruct((2, length, width // CORES), query.dtype),
        name="halves",
    )(index, query, grad)


def added(pieces):
    total = pieces[0].astype(jnp.float32)
    for piece in pieces[1:]:
        total = total + piece.astype(jnp.float32)
    return total.astype(jnp.bfloat16)


def finish_kernel(index_ref, piece, *refs):
    grad_key, grad_value = refs[-2:]
    length = grad_key.shape[0]
    total = added([piece[z, 0] for z in range(piece.shape[0])])
    grad_key[...] = total[:length]
    grad_value[...] = total[length:]


def settle_kernel(index_ref, *refs, count):
    grad_key, grad_value, away = refs[-3:]
    length = grad_key.shape[0]
    total = added([piece[0] for piece in refs[:count]])
    grad_key[...] = total[:length]
    grad_value[...] = total[length:]
    away[...] = added([piece[1] for piece in refs[:count]])


def into_grads(kernel, index, grid, specs, operands, heads, shape, extra, carried):
    specs = list(specs)
    aliases = {}
    if carried is not None:
        specs += [pl.BlockSpec(memory_space=pl.ANY)] * 2
        aliases = {1 + len(operands): 0, 2 + len(operands): 1}
        operands = [*operands, *carried]
    block = pl.BlockSpec((shape[0], HD), heads)
    out_specs = [block, block]
    out_shape = [jax.ShapeDtypeStruct(shape, jnp.bfloat16)] * 2
    if extra is not None:
        out_specs.append(pl.BlockSpec(extra, lambda i, c: (0,) * len(extra)))
        out_shape.append(jax.ShapeDtypeStruct(extra, jnp.bfloat16))
    grid_spec = pltpu.PrefetchScalarGridSpec(
        num_scalar_prefetch=1, grid=(grid,), in_specs=specs, out_specs=out_specs
    )
    return pl.pallas_call(
        kernel,
        grid_spec=grid_spec,
        out_shape=out_shape,
        input_output_aliases=aliases,
        compiler_params=pltpu.CompilerParams(vmem_limit_bytes=8 * 1024 * 1024),
    )(index, *operands)


def finish(index, chunk, chunks, piece, shape, carried):
    count, rows, _ = piece.shape
    piece = piece.reshape(count // CORES, CORES, rows, HD)
    spec = pl.BlockSpec((count // CORES, 1, rows, HD), lambda i, c: (0, i, 0, 0))
    heads = lambda i, c: (0, i * chunks + chunk)
    return into_grads(finish_kernel, index, CORES, [spec], [piece], heads, shape, None, carried)


def settle(index, chunk, chunks, pieces, shape, carried):
    spec = pl.BlockSpec(pieces[0].shape, lambda i, c: (0, 0, 0))
    heads = lambda i, c: (0, (c[0] % CORES) * chunks + chunk)
    kernel = functools.partial(settle_kernel, count=len(pieces))
    extra = pieces[0].shape[1:]
    return into_grads(kernel, index, 1, [spec] * len(pieces), pieces, heads, shape, extra, carried)


def receive(index, chunk, chunks, piece, shape, carried):
    piece = piece[None, None]
    spec = pl.BlockSpec(piece.shape, lambda i, c: (0, 0, 0, 0))
    heads = lambda i, c: (0, (1 - c[0] % CORES) * chunks + chunk)
    return into_grads(finish_kernel, index, 1, [spec], [piece], heads, shape, None, carried)


def bias_kernel(index_ref, sums, bias_grad, *, chunks, factor):
    core = index_ref[0] % CORES
    for c in range(CORES):
        ours = core == c
        for hh in range(chunks):
            head = c * chunks + hh
            rows = slice(hh * BIAS_ROWS, hh * BIAS_ROWS + GROUP)
            bias_grad[head * GROUP : (head + 1) * GROUP, :] = (
                jnp.where(ours, sums[0, rows, :], sums[1, rows, :]) * factor
            )
            row = slice(hh * BIAS_ROWS + GROUP, hh * BIAS_ROWS + GROUP + 1)
            at = CORES * chunks * GROUP + head
            bias_grad[at : at + 1, :] = (
                jnp.where(ours, sums[0, row, :], sums[1, row, :]) * factor
            )


def bias_total(index, sums, chunks, factor):
    return pl.pallas_call(
        functools.partial(bias_kernel, chunks=chunks, factor=factor),
        in_specs=[
            pl.BlockSpec(memory_space=pltpu.SMEM),
            pl.BlockSpec(memory_space=pltpu.VMEM),
        ],
        out_shape=jax.ShapeDtypeStruct((CORES * chunks * (GROUP + 1), HD), jnp.float32),
        compiler_params=pltpu.CompilerParams(vmem_limit_bytes=4 * 1024 * 1024),
        name="bias",
    )(index, sums)


def summed(part, axis, steps):
    size = lax.axis_size(axis)
    if len(steps) > 2:
        for step in steps:
            part = part + lax.ppermute(part, axis, [(i, i ^ step) for i in range(size)])
        return part
    total = part
    for pick in range(1, 2 ** len(steps)):
        mixed = sum(step for k, step in enumerate(steps) if pick >> k & 1)
        total = total + lax.ppermute(part, axis, [(i, i ^ mixed) for i in range(size)])
    return total


def powers(start, stop):
    found = []
    while start < stop:
        found.append(start)
        start *= 2
    return found


def body(query_rows, key_rows, value_rows, out_grad, destination, group_first):
    length = query_rows.shape[0]
    devices = lax.axis_size("ctx")
    replicas = lax.axis_size("dp")
    index = lax.axis_index("ctx").astype(jnp.int32)
    kv_heads = key_rows.shape[1] // HD
    chunks = kv_heads // CORES
    plan = destination.reshape(devices, length)
    across = [(i, i ^ 1) for i in range(devices)]
    index_arg = index.reshape(1)

    chips = devices // CORES
    order = range(chips - 1, 0, -1)

    def over(k):
        return [(i, i ^ (CORES * k)) for i in range(devices)]

    near, away = payload(index_arg, group_first, key_rows, value_rows, chunks)
    away = lax.ppermute(away, "ctx", across)
    joined = join(near, away)
    gathered = []
    for hh in range(chunks):
        pairs = [joined[hh]] * chips
        for k in order:
            pairs[k] = lax.ppermute(joined[hh], "ctx", over(k))
        gathered.append(pairs)
    far_in = halves(index_arg, query_rows, out_grad)
    far_in = lax.ppermute(far_in, "ctx", across)

    carried = None
    returned = []
    for hh in range(chunks):
        split = SPLIT[hh % len(SPLIT)]
        outs = attention(
            index_arg,
            hh,
            chunks,
            plan,
            query_rows,
            out_grad,
            far_in,
            gathered[hh],
            carried,
            split,
        )
        carried, parts = outs[:4], outs[4:]
        if split:
            pieces = list(parts)
            for k in order:
                pieces[k] = lax.ppermute(parts[k], "ctx", over(k))
            returned.append(pieces)
        else:
            returned.append(
                lax.all_to_all(parts[0], "ctx", split_axis=0, concat_axis=0, tiled=True)
            )
    attended, grad_query, bias, far_out = carried
    far_out = lax.ppermute(far_out, "ctx", across)
    attended, grad_query = place(index_arg, far_out, attended, grad_query)
    both = jnp.stack([bias, lax.ppermute(bias, "ctx", across)])
    both = summed(both, "dp", powers(1, replicas))
    both = summed(both, "ctx", powers(CORES, devices))
    factor = 1.0 / math.sqrt(length * devices * replicas)
    bias_grad = bias_total(index_arg, both, chunks, factor)
    grads = None
    shape = key_rows.shape
    for hh in range(chunks):
        if SPLIT[hh % len(SPLIT)]:
            *grads, away = settle(index_arg, hh, chunks, returned[hh], shape, grads)
            away = lax.ppermute(away, "ctx", across)
            grads = receive(index_arg, hh, chunks, away, shape, grads)
        else:
            grads = finish(index_arg, hh, chunks, returned[hh], shape, grads)
    return (attended, grad_query, *grads, bias_grad.reshape(-1))


def solution(mesh):
    rows = P(("dp", "ctx"), None)
    return jax.shard_map(
        body,
        mesh=mesh,
        in_specs=(rows, rows, rows, rows, P("dp", None), P("dp", "ctx")),
        out_specs=(rows, rows, rows, rows, P()),
        check_vma=False,
    )
```

time: 130 us -> 93 us (0.72)
  blocking collectives: 29.9 us -> 0 us
  starting transfers between devices: 17.8 us -> 37.4 us
  other arithmetic: 13.9 us -> 0.02 us
  waiting for transfers between devices: 30.3 us -> 21.6 us
  local copies, waits for them, and re-layouts: 7.61 us -> 1.57 us
  Pallas kernels: 28.8 us -> 30.8 us
    all_to_all x2 -> x0, blocking collectives: 29.9 us -> none  [the longest x1 18.4 us: local(): lax.all_to_all(parts, 'ctx', split_axis=0, concat_axis=0, tiled=True)]
    ppermute x6 -> x20, starting transfers between devices: 4.24 us -> 32.8 us  [the longest x6 15.8 us: body(): pairs[k] = lax.ppermute(joined[hh], 'ctx', over(k))]
    all_to_all x3 -> x1, waiting for transfers between devices: 24.2 us -> 0.01 us  [body(): lax.all_to_all(parts[0], 'ctx', split_axis=0, concat_axis=0, tiled=True)]
    ppermute x6 -> x20, waiting for transfers between devices: 6.07 us -> 21.6 us  [the longest x3 8.28 us: body(): pieces[k] = lax.ppermute(parts[k], 'ctx', over(k))]
    unnamed x13 -> x0, other arithmetic: 9.47 us -> none
    all_to_all x3 -> x1, starting transfers between devices: 13.5 us -> 4.55 us  [body(): lax.all_to_all(parts[0], 'ctx', split_axis=0, concat_axis=0, tiled=True)]
    pallas_call x1 -> x7, Pallas kernels: 2.02 us -> 8.46 us  [the longest x1 2.39 us: halves(): pl.pallas_call(halves_kernel, grid_spec=grid_spec, out_shape=jax.ShapeDty...]
    pallas_call x2, Pallas kernels: 24.6 us -> 21.3 us  [attention(): pl.pallas_call(functools.partial(attention_kernel, carried=carried is not...]
  transfers between devices with their start and end apart: 9 -> 21, of which waited for: 7 -> 7; matrix products, arithmetic and copies ran while one was open for 3% -> 0% of each run, Pallas kernels for 11% -> 18%
where the time goes in v1:
time: 93 us; the launch traced here: 92.7 us
  starting transfers between devices  37.4 us (40%)
  Pallas kernels  30.8 us (33%)
  waiting for transfers between devices  21.6 us (23%)
  local copies, waits for them, and re-layouts  1.57 us (2%)
  between operations  1.4 us (2%)
    pallas_call x2, Pallas kernels, attention(): pl.pallas_call(functools.partial(attention_kernel, carried=carried is not...  21.3 us
    ppermute x6, starting transfers between devices, body(): pairs[k] = lax.ppermute(joined[hh], 'ctx', over(k))  15.8 us
    ppermute x6, starting transfers between devices, summed(): lax.ppermute(part, axis, [(i, i ^ mixed) for i in range(size)])  9.54 us
    ppermute x3, waiting for transfers between devices, body(): pieces[k] = lax.ppermute(parts[k], 'ctx', over(k))  8.28 us
    ppermute x6, waiting for transfers between devices, body(): pairs[k] = lax.ppermute(joined[hh], 'ctx', over(k))  7.48 us
    ppermute x3, starting transfers between devices, body(): pieces[k] = lax.ppermute(parts[k], 'ctx', over(k))  6.44 us
    all_to_all x1, starting transfers between devices, body(): lax.all_to_all(parts[0], 'ctx', split_axis=0, concat_axis=0, tiled=True)  4.55 us
    ppermute x6, waiting for transfers between devices, summed(): lax.ppermute(part, axis, [(i, i ^ mixed) for i in range(size)])  3.34 us
  transfers between devices with their start and end apart: 21, of which 7 were waited for; matrix products, arithmetic and copies ran while one was open for 0% of the time, Pallas kernels for 18%

profile of v1, /device:TPU:0, one launch (start us, length us, event | category | flops | bytes accessed | tf_op | source)
XLA Modules:
  0.0 92.7 jit_solution(7147541363365517590)
XLA Ops:
  0.6 0.0 copy-start
  0.6 0.0 copy-start.1
  0.7 2.4 %halves.1 = bf16[2,128,2048]{2,1,0:T(8,128)(2,1)} custom-call(s32[1]{0:T(128)} %bitcast.index_ref, bf16[128,4096]{1,0:T(8,128)(2,1)} %query_own.3, bf16[128,4096]{1,0:T(8,128)(2,1)} %grad_own.3), custom_call_target="tpu_custom_call" | custom-call | tf_op jit(solution)/shard_map/halves/pallas_call | solution.py:280
  3.0 0.5 collective-permute-start
  4.2 1.7 %payload.1 = (bf16[2,264,128]{2,1,0:T(8,128)(2,1)}, bf16[2,264,128]{2,1,0:T(8,128)(2,1)}) custom-call(s32[1]{0:T(128)} %bitcast.index_ref, s32[1,1]{1,0:T(1,128)S(6)} %copy.31.first_ref, bf16[128,512]{1,0:T(8,128)(2,1)} %keys.1, bf16[128,512]{1,0:T(8,128)(2,1)} %values.1), custom_call_target="tpu_custom_call" | custom-call | tf_op jit(solution)/shard_map/payload/pallas_call | solution.py:221
  5.9 0.0 collective-permute-start.1
  5.9 1.5 %collective-permute-done.1.away = bf16[2,264,128]{2,1,0:T(8,128)(2,1)S(1)} collective-permute-done((bf16[2,264,128]{2,1,0:T(8,128)(2,1)}, bf16[2,264,128]{2,1,0:T(8,128)(2,1)S(1)}, u32[]{:S(2)}, u32[]{:S(2)}) %collective-permute-start.1) | collective-permute-done | bytes 135200 | tf_op jit(solution)/shard_map/ppermute | solution.py:429
  7.5 0.0 copy-start.7
  7.5 0.6 copy-done.7
  8.1 1.7 %join.1 = (bf16[2,264,128]{2,1,0:T(8,128)(2,1)}, bf16[2,264,128]{2,1,0:T(8,128)(2,1)}) custom-call(bf16[2,264,128]{2,1,0:T(8,128)(2,1)} %get-tuple-element.31.near, bf16[2,264,128]{2,1,0:T(8,128)(2,1)} %copy-done.7), custom_call_target="tpu_custom_call" | custom-call | tf_op jit(solution)/shard_map/join/pallas_call | solution.py:238
  9.8 4.7 %collective-permute-start.7 = (bf16[2,264,128]{2,1,0:T(8,128)(2,1)}, bf16[2,264,128]{2,1,0:T(8,128)(2,1)S(1)}, u32[]{:S(2)}, u32[]{:S(2)}) collective-permute-start(bf16[2,264,128]{2,1,0:T(8,128)(2,1)} %get-tuple-element.34.refs_0_), channel_id=1, source_target_pairs={{0,6},{1,7},{2,4},{3,5},{4,2},{5,3},{6,0},{7,1},{8,14},{9,15},{10,... | collective-permute-start | bytes 405512 | tf_op jit(solution)/shard_map/ppermute | solution.py:435
  14.5 0.0 collective-permute-start.6
  14.5 0.6 collective-permute-start.5
  15.1 3.8 %collective-permute-start.4 = (bf16[2,264,128]{2,1,0:T(8,128)(2,1)}, bf16[2,264,128]{2,1,0:T(8,128)(2,1)S(1)}, u32[]{:S(2)}, u32[]{:S(2)}) collective-permute-start(bf16[2,264,128]{2,1,0:T(8,128)(2,1)} %get-tuple-element.33.refs_0_), channel_id=1, source_target_pairs={{0,6},{1,7},{2,4},{3,5},{4,2},{5,3},{6,0},{7,1},{8,14},{9,15},{10,... | collective-permute-start | bytes 405512 | tf_op jit(solution)/shard_map/ppermute | solution.py:435
  18.9 0.4 collective-permute-done.7.refs_3_
  19.3 6.7 %collective-permute-start.3 = (bf16[2,264,128]{2,1,0:T(8,128)(2,1)}, bf16[2,264,128]{2,1,0:T(8,128)(2,1)S(1)}, u32[]{:S(2)}, u32[]{:S(2)}) collective-permute-start(bf16[2,264,128]{2,1,0:T(8,128)(2,1)} %get-tuple-element.33.refs_0_), channel_id=1, source_target_pairs={{0,4},{1,5},{2,6},{3,7},{4,0},{5,1},{6,2},{7,3},{8,12},{9,13},{10,... | collective-permute-start | bytes 405512 | tf_op jit(solution)/shard_map/ppermute | solution.py:435
  26.0 7.1 %collective-permute-done.6.refs_2_ = bf16[2,264,128]{2,1,0:T(8,128)(2,1)S(1)} collective-permute-done((bf16[2,264,128]{2,1,0:T(8,128)(2,1)}, bf16[2,264,128]{2,1,0:T(8,128)(2,1)S(1)}, u32[]{:S(2)}, u32[]{:S(2)}) %collective-permute-start.6) | collective-permute-done | bytes 135200 | tf_op jit(solution)/shard_map/ppermute | solution.py:435
  33.1 0.0 collective-permute-start.2
  33.1 0.0 collective-permute-done.5.refs_1_
  33.1 0.0 collective-permute-done.far_in
  33.1 0.0 copy-done
  33.1 0.0 copy-done.1
  33.1 0.0 copy-done.6
  33.1 0.0 copy-start.3
  33.1 0.9 copy-done.3
  34.0 10.6 %attention.2 = (bf16[128,4096]{1,0:T(8,128)(2,1)}, bf16[128,4096]{1,0:T(8,128)(2,1)}, f32[32,128]{1,0:T(8,128)S(1)}, bf16[2,128,2048]{2,1,0:T(8,128)(2,1)}, bf16...) custom-call(s32[1]{0:T(128)} %bitcast.index_ref, ...), custom_call_target="tpu_custom_call" | custom-call | flops 3221225472 | bytes 2097152 | tf_op jit(solution)/shard_map/attention/pallas_call | solution.py:184
  44.6 0.0 collective-permute-done.4.refs_3_
  44.6 0.0 collective-permute-done.3.refs_2_
  44.6 0.0 collective-permute-done.2.refs_1_
  44.7 0.0 copy-done.2
  44.7 10.7 %attention.3 = (bf16[128,4096]{1,0:T(8,128)(2,1)}, bf16[128,4096]{1,0:T(8,128)(2,1)}, f32[32,128]{1,0:T(8,128)S(1)}, bf16[2,128,2048]{2,1,0:T(8,128)(2,1)}, bf16[8,256,128]{2,1,0:T(8,128)(2,1)}) custom-call(s32[1]{0:T(128)} %bitcast.index_ref, s32[8,128]{1,0:T(8,128)S(1)} %bitcast.12, ...), custom_call_target="tpu_custom_call", output_to_operand_aliasing={{0}: (9, {}), {1}: (10, {}), {2}: (11, {}), {3}: (12, {})} | custom-call | flops 3221225472 | bytes 2097152 | tf_op jit(solution)/shard_map/attention/pallas_call | solution.py:184
  55.3 0.0 copy-done.4
  55.3 0.0 collective-permute-start.8
  55.3 4.6 %all-to-all-start = ((bf16[8,256,128]{2,1,0:T(8,128)(2,1)}), bf16[8,256,128]{2,1,0:T(8,128)(2,1)S(1)}, u32[]{:S(2)}, u32[]{:S(2)}) async-start(bf16[8,256,128]{2,1,0:T(8,128)(2,1)} %get-tuple-element.44), calls=%async_computation | async-start | bytes 1048576 | tf_op jit(solution)/shard_map/all_to_all | solution.py:464
  59.9 0.5 collective-permute-start.13
  60.4 1.0 %collective-permute-done.13 = f32[32,128]{1,0:T(8,128)S(1)} collective-permute-done((f32[32,128]{1,0:T(8,128)S(1)}, f32[32,128]{1,0:T(8,128)S(1)}, u32[]{:S(2)}, u32[]{:S(2)}) %collective-permute-start.13) | collective-permute-done | bytes 16416 | tf_op jit(solution)/shard_map/ppermute | solution.py:469
  61.4 1.5 %collective-permute-start.15 = (f32[2,32,128]{2,1,0:T(8,128)S(1)}, f32[2,32,128]{2,1,0:T(8,128)S(1)}, u32[]{:S(2)}, u32[]{:S(2)}) collective-permute-start(f32[2,32,128]{2,1,0:T(8,128)S(1)} %pad_maximum_fusion), channel_id=1, source_target_pairs={{0,16},{8,24},{16,0},{24,8},{1,17},{9,25},{17,1},{25,9},{2,18},{10... | collective-permute-start | bytes 98312 | tf_op jit(solution)/shard_map/ppermute | solution.py:399
  62.9 1.4 %collective-permute-start.16 = (f32[2,32,128]{2,1,0:T(8,128)S(1)}, f32[2,32,128]{2,1,0:T(8,128)S(1)}, u32[]{:S(2)}, u32[]{:S(2)}) collective-permute-start(f32[2,32,128]{2,1,0:T(8,128)S(1)} %pad_maximum_fusion), channel_id=1, source_target_pairs={{0,24},{8,16},{16,8},{24,0},{1,25},{9,17},{17,9},{25,1},{2,26},{10... | collective-permute-start | bytes 98312 | tf_op jit(solution)/shard_map/ppermute | solution.py:399
  64.3 0.5 collective-permute-start.14
  64.9 0.0 copy-done.5
  64.9 1.7 %collective-permute-start.9 = (bf16[2,256,128]{2,1,0:T(8,128)(2,1)S(1)}, bf16[2,256,128]{2,1,0:T(8,128)(2,1)S(1)}, u32[]{:S(2)}, u32[]{:S(2)}) collective-permute-start(bf16[2,256,128]{2,1,0:T(8,128)(2,1)S(1)} %copy-done.5), channel_id=1, source_target_pairs={{0,2},{1,3},{2,0},{3,1},{4,6},{5,7},{6,4},{7,5},{8,10},{9,11},{10,... | collective-permute-start | bytes 393224 | tf_op jit(solution)/shard_map/ppermute | solution.py:460
  66.6 0.0 collective-permute-done.15
  66.6 2.4 %collective-permute-start.10 = (bf16[2,256,128]{2,1,0:T(8,128)(2,1)S(1)}, bf16[2,256,128]{2,1,0:T(8,128)(2,1)S(1)}, u32[]{:S(2)}, u32[]{:S(2)}) collective-permute-start(bf16[2,256,128]{2,1,0:T(8,128)(2,1)S(1)} %get-tuple-element.47), channel_id=1, source_target_pairs={{0,4},{1,5},{2,6},{3,7},{4,0},{5,1},{6,2},{7,3},{8,12},{9,13},{10,... | collective-permute-start | bytes 393224 | tf_op jit(solution)/shard_map/ppermute | solution.py:460
  69.0 0.0 collective-permute-done.16
  69.0 2.3 %collective-permute-start.11 = (bf16[2,256,128]{2,1,0:T(8,128)(2,1)S(1)}, bf16[2,256,128]{2,1,0:T(8,128)(2,1)S(1)}, u32[]{:S(2)}, u32[]{:S(2)}) collective-permute-start(bf16[2,256,128]{2,1,0:T(8,128)(2,1)S(1)} %get-tuple-element.48), channel_id=1, source_target_pairs={{0,6},{1,7},{2,4},{3,5},{4,2},{5,3},{6,0},{7,1},{8,14},{9,15},{10,... | collective-permute-start | bytes 393224 | tf_op jit(solution)/shard_map/ppermute | solution.py:460
  71.3 0.0 collective-permute-done.14
  71.3 1.5 %collective-permute-start.19 = (f32[2,32,128]{2,1,0:T(8,128)S(1)}, f32[2,32,128]{2,1,0:T(8,128)S(1)}, u32[]{:S(2)}, u32[]{:S(2)}) collective-permute-start(f32[2,32,128]{2,1,0:T(8,128)S(1)} %add_add_fusion.1), channel_id=1, source_target_pairs={{0,6},{1,7},{2,4},{3,5},{4,2},{5,3},{6,0},{7,1},{8,14},{9,15},{10,... | collective-permute-start | bytes 98312 | tf_op jit(solution)/shard_map/ppermute | solution.py:399
  72.9 0.0 collective-permute-done.9.refs_1_
  72.9 4.5 %collective-permute-start.18 = (f32[2,32,128]{2,1,0:T(8,128)S(1)}, f32[2,32,128]{2,1,0:T(8,128)S(1)}, u32[]{:S(2)}, u32[]{:S(2)}) collective-permute-start(f32[2,32,128]{2,1,0:T(8,128)S(1)} %add_add_fusion.1), channel_id=1, source_target_pairs={{0,4},{1,5},{2,6},{3,7},{4,0},{5,1},{6,2},{7,3},{8,12},{9,13},{10,... | collective-permute-start | bytes 98312 | tf_op jit(solution)/shard_map/ppermute | solution.py:399
  77.4 8.3 %collective-permute-done.10.refs_2_ = bf16[2,256,128]{2,1,0:T(8,128)(2,1)S(1)} collective-permute-done((bf16[2,256,128]{2,1,0:T(8,128)(2,1)S(1)}, bf16[2,256,128]{2,1,0:T(8,128)(2,1)S(1)}, u32[]{:S(2)}, u32[]{:S(2)}) %collective-permute-start.10) | collective-permute-done | bytes 131104 | tf_op jit(solution)/shard_map/ppermute | solution.py:460
  85.7 0.0 collective-permute-start.17
  85.7 0.0 collective-permute-done.11.refs_3_
  85.7 0.7 shard_map.101
  86.3 0.0 collective-permute-start.12
  86.3 0.0 collective-permute-done.19
  86.3 3.0 %collective-permute-done.18 = f32[2,32,128]{2,1,0:T(8,128)S(1)} collective-permute-done((f32[2,32,128]{2,1,0:T(8,128)S(1)}, f32[2,32,128]{2,1,0:T(8,128)S(1)}, u32[]{:S(2)}, u32[]{:S(2)}) %collective-permute-start.18) | collective-permute-done | bytes 32800 | tf_op jit(solution)/shard_map/ppermute | solution.py:399
  89.3 0.3 collective-permute-done.17
  89.7 0.6 bias.1
  90.3 0.0 collective-permute-done.12
  90.3 0.6 shard_map.102
  90.9 0.0 all-to-all-done
  90.9 0.8 shard_map.103
  91.7 0.0 collective-permute-done.8.far
  91.7 1.0 %place.1 = (bf16[128,4096]{1,0:T(8,128)(2,1)}, bf16[128,4096]{1,0:T(8,128)(2,1)}) custom-call(s32[1]{0:T(128)} %bitcast.index_ref, bf16[2,128,2048]{2,1,0:T(8,128)(2,1)S(1)} %collective-permute-done.8.far, bf16[128,4096]{1,0:T(8,128)(2,1)} %get-tuple-element.40.attended_in, ...), custom_call_target="tpu_custom_call", output_to_operand_aliasing={{0}: (2, {}), {1}: (3, {})} | custom-call | tf_op jit(solution)/shard_map/place/pallas_call | solution.py:256
  (7 shorter events, 0.0 us)
Async XLA Ops:
  0.6 32.5 %copy-start = (bf16[128,4096]{1,0:T(8,128)(2,1)S(1)}, bf16[128,4096]{1,0:T(8,128)(2,1)}, u32[]{:S(2)}) copy-start(bf16[128,4096]{1,0:T(8,128)(2,1)} %query_own.3) | copy-start | bytes 3145732
  0.6 32.5 %copy-start.1 = (bf16[128,4096]{1,0:T(8,128)(2,1)S(1)}, bf16[128,4096]{1,0:T(8,128)(2,1)}, u32[]{:S(2)}) copy-start(bf16[128,4096]{1,0:T(8,128)(2,1)} %grad_own.3) | copy-start | bytes 3145732
  3.0 30.0 %collective-permute-start = (bf16[2,128,2048]{2,1,0:T(8,128)(2,1)}, bf16[2,128,2048]{2,1,0:T(8,128)(2,1)S(1)}, u32[]{:S(2)}, u32[]{:S(2)}) collective-permute-start(bf16[2,128,2048]{2,1,0:T(8,128)(2,1)} %halves.1), channel_id=1, source_target_pairs={{0,1},{1,0},{2,3},{3,2},{4,5},{5,4},{6,7},{7,6},{8,9},{9,8},{10,11... | collective-permute-start | bytes 3145736 | tf_op jit(solution)/shard_map/ppermute | solution.py:438
  5.9 1.6 %collective-permute-start.1 = (bf16[2,264,128]{2,1,0:T(8,128)(2,1)}, bf16[2,264,128]{2,1,0:T(8,128)(2,1)S(1)}, u32[]{:S(2)}, u32[]{:S(2)}) collective-permute-start(bf16[2,264,128]{2,1,0:T(8,128)(2,1)} %get-tuple-element.32), channel_id=1, source_target_pairs={{0,1},{1,0},{2,3},{3,2},{4,5},{5,4},{6,7},{7,6},{8,9},{9,8},{10,11... | collective-permute-start | bytes 405512 | tf_op jit(solution)/shard_map/ppermute | solution.py:429
  7.5 0.6 copy-start.7
  9.8 23.3 %copy-start.6 = (s32[1,1024]{1,0:T(1,128)S(1)}, s32[1,1024]{1,0:T(1,128)}, u32[]{:S(2)}) copy-start(s32[1,1024]{1,0:T(1,128)} %param.10) | copy-start | bytes 12292
  9.8 9.5 %collective-permute-start.7 = (bf16[2,264,128]{2,1,0:T(8,128)(2,1)}, bf16[2,264,128]{2,1,0:T(8,128)(2,1)S(1)}, u32[]{:S(2)}, u32[]{:S(2)}) collective-permute-start(bf16[2,264,128]{2,1,0:T(8,128)(2,1)} %get-tuple-element.34.refs_0_), channel_id=1, source_target_pairs={{0,6},{1,7},{2,4},{3,5},{4,2},{5,3},{6,0},{7,1},{8,14},{9,15},{10,... | collective-permute-start | bytes 405512 | tf_op jit(solution)/shard_map/ppermute | solution.py:435
  14.5 18.6 %collective-permute-start.6 = (bf16[2,264,128]{2,1,0:T(8,128)(2,1)}, bf16[2,264,128]{2,1,0:T(8,128)(2,1)S(1)}, u32[]{:S(2)}, u32[]{:S(2)}) collective-permute-start(bf16[2,264,128]{2,1,0:T(8,128)(2,1)} %get-tuple-element.34.refs_0_), channel_id=1, source_target_pairs={{0,4},{1,5},{2,6},{3,7},{4,0},{5,1},{6,2},{7,3},{8,12},{9,13},{10,... | collective-permute-start | bytes 405512 | tf_op jit(solution)/shard_map/ppermute | solution.py:435
  14.5 18.6 %collective-permute-start.5 = (bf16[2,264,128]{2,1,0:T(8,128)(2,1)}, bf16[2,264,128]{2,1,0:T(8,128)(2,1)S(1)}, u32[]{:S(2)}, u32[]{:S(2)}) collective-permute-start(bf16[2,264,128]{2,1,0:T(8,128)(2,1)} %get-tuple-element.34.refs_0_), channel_id=1, source_target_pairs={{0,2},{1,3},{2,0},{3,1},{4,6},{5,7},{6,4},{7,5},{8,10},{9,11},{10,... | collective-permute-start | bytes 405512 | tf_op jit(solution)/shard_map/ppermute | solution.py:435
  15.1 29.5 %collective-permute-start.4 = (bf16[2,264,128]{2,1,0:T(8,128)(2,1)}, bf16[2,264,128]{2,1,0:T(8,128)(2,1)S(1)}, u32[]{:S(2)}, u32[]{:S(2)}) collective-permute-start(bf16[2,264,128]{2,1,0:T(8,128)(2,1)} %get-tuple-element.33.refs_0_), channel_id=1, source_target_pairs={{0,6},{1,7},{2,4},{3,5},{4,2},{5,3},{6,0},{7,1},{8,14},{9,15},{10,... | collective-permute-start | bytes 405512 | tf_op jit(solution)/shard_map/ppermute | solution.py:435
  19.3 25.4 %collective-permute-start.3 = (bf16[2,264,128]{2,1,0:T(8,128)(2,1)}, bf16[2,264,128]{2,1,0:T(8,128)(2,1)S(1)}, u32[]{:S(2)}, u32[]{:S(2)}) collective-permute-start(bf16[2,264,128]{2,1,0:T(8,128)(2,1)} %get-tuple-element.33.refs_0_), channel_id=1, source_target_pairs={{0,4},{1,5},{2,6},{3,7},{4,0},{5,1},{6,2},{7,3},{8,12},{9,13},{10,... | collective-permute-start | bytes 405512 | tf_op jit(solution)/shard_map/ppermute | solution.py:435
  33.1 11.6 %collective-permute-start.2 = (bf16[2,264,128]{2,1,0:T(8,128)(2,1)}, bf16[2,264,128]{2,1,0:T(8,128)(2,1)S(1)}, u32[]{:S(2)}, u32[]{:S(2)}) collective-permute-start(bf16[2,264,128]{2,1,0:T(8,128)(2,1)} %get-tuple-element.33.refs_0_), channel_id=1, source_target_pairs={{0,2},{1,3},{2,0},{3,1},{4,6},{5,7},{6,4},{7,5},{8,10},{9,11},{10,... | collective-permute-start | bytes 405512 | tf_op jit(solution)/shard_map/ppermute | solution.py:435
  33.1 0.9 copy-start.3
  34.0 10.6 %copy-start.2 = (bf16[2,264,128]{2,1,0:T(8,128)(2,1)S(1)}, bf16[2,264,128]{2,1,0:T(8,128)(2,1)}, u32[]{:S(2)}) copy-start(bf16[2,264,128]{2,1,0:T(8,128)(2,1)} %get-tuple-element.33.refs_0_) | copy-start | bytes 405508
  44.6 10.7 %copy-start.4 = (bf16[2,256,128]{2,1,0:T(8,128)(2,1)}, bf16[2,256,128]{2,1,0:T(8,128)(2,1)S(1)}, u32[]{:S(2)}) copy-start(bf16[2,256,128]{2,1,0:T(8,128)(2,1)S(1)} %get-tuple-element.46) | copy-start | bytes 393220
  55.3 36.4 %collective-permute-start.8 = (bf16[2,128,2048]{2,1,0:T(8,128)(2,1)}, bf16[2,128,2048]{2,1,0:T(8,128)(2,1)S(1)}, u32[]{:S(2)}, u32[]{:S(2)}) collective-permute-start(bf16[2,128,2048]{2,1,0:T(8,128)(2,1)} %get-tuple-element.39), channel_id=1, source_target_pairs={{0,1},{1,0},{2,3},{3,2},{4,5},{5,4},{6,7},{7,6},{8,9},{9,8},{10,11... | collective-permute-start | bytes 3145736 | tf_op jit(solution)/shard_map/ppermute | solution.py:467
  55.3 9.5 %copy-start.5 = (bf16[2,256,128]{2,1,0:T(8,128)(2,1)S(1)}, bf16[2,256,128]{2,1,0:T(8,128)(2,1)}, u32[]{:S(2)}) copy-start(bf16[2,256,128]{2,1,0:T(8,128)(2,1)} %copy-done.4) | copy-start | bytes 393220
  55.3 35.6 %all-to-all-start = ((bf16[8,256,128]{2,1,0:T(8,128)(2,1)}), bf16[8,256,128]{2,1,0:T(8,128)(2,1)S(1)}, u32[]{:S(2)}, u32[]{:S(2)}) async-start(bf16[8,256,128]{2,1,0:T(8,128)(2,1)} %get-tuple-element.44), calls=%async_computation | async-start | bytes 1048576 | tf_op jit(solution)/shard_map/all_to_all | solution.py:464
  59.9 1.5 %collective-permute-start.13 = (f32[32,128]{1,0:T(8,128)S(1)}, f32[32,128]{1,0:T(8,128)S(1)}, u32[]{:S(2)}, u32[]{:S(2)}) collective-permute-start(f32[32,128]{1,0:T(8,128)S(1)} %get-tuple-element.56), channel_id=1, source_target_pairs={{0,1},{1,0},{2,3},{3,2},{4,5},{5,4},{6,7},{7,6},{8,9},{9,8},{10,11... | collective-permute-start | bytes 49160 | tf_op jit(solution)/shard_map/ppermute | solution.py:469
  61.4 5.2 %collective-permute-start.15 = (f32[2,32,128]{2,1,0:T(8,128)S(1)}, f32[2,32,128]{2,1,0:T(8,128)S(1)}, u32[]{:S(2)}, u32[]{:S(2)}) collective-permute-start(f32[2,32,128]{2,1,0:T(8,128)S(1)} %pad_maximum_fusion), channel_id=1, source_target_pairs={{0,16},{8,24},{16,0},{24,8},{1,17},{9,25},{17,1},{25,9},{2,18},{10... | collective-permute-start | bytes 98312 | tf_op jit(solution)/shard_map/ppermute | solution.py:399
  62.9 6.1 %collective-permute-start.16 = (f32[2,32,128]{2,1,0:T(8,128)S(1)}, f32[2,32,128]{2,1,0:T(8,128)S(1)}, u32[]{:S(2)}, u32[]{:S(2)}) collective-permute-start(f32[2,32,128]{2,1,0:T(8,128)S(1)} %pad_maximum_fusion), channel_id=1, source_target_pairs={{0,24},{8,16},{16,8},{24,0},{1,25},{9,17},{17,9},{25,1},{2,26},{10... | collective-permute-start | bytes 98312 | tf_op jit(solution)/shard_map/ppermute | solution.py:399
  64.3 7.0 %collective-permute-start.14 = (f32[2,32,128]{2,1,0:T(8,128)S(1)}, f32[2,32,128]{2,1,0:T(8,128)S(1)}, u32[]{:S(2)}, u32[]{:S(2)}) collective-permute-start(f32[2,32,128]{2,1,0:T(8,128)S(1)} %pad_maximum_fusion), channel_id=1, source_target_pairs={{0,8},{8,0},{16,24},{24,16},{1,9},{9,1},{17,25},{25,17},{2,10},{10... | collective-permute-start | bytes 98312 | tf_op jit(solution)/shard_map/ppermute | solution.py:399
  64.9 8.0 %collective-permute-start.9 = (bf16[2,256,128]{2,1,0:T(8,128)(2,1)S(1)}, bf16[2,256,128]{2,1,0:T(8,128)(2,1)S(1)}, u32[]{:S(2)}, u32[]{:S(2)}) collective-permute-start(bf16[2,256,128]{2,1,0:T(8,128)(2,1)S(1)} %copy-done.5), channel_id=1, source_target_pairs={{0,2},{1,3},{2,0},{3,1},{4,6},{5,7},{6,4},{7,5},{8,10},{9,11},{10,... | collective-permute-start | bytes 393224 | tf_op jit(solution)/shard_map/ppermute | solution.py:460
  66.6 19.1 %collective-permute-start.10 = (bf16[2,256,128]{2,1,0:T(8,128)(2,1)S(1)}, bf16[2,256,128]{2,1,0:T(8,128)(2,1)S(1)}, u32[]{:S(2)}, u32[]{:S(2)}) collective-permute-start(bf16[2,256,128]{2,1,0:T(8,128)(2,1)S(1)} %get-tuple-element.47), channel_id=1, source_target_pairs={{0,4},{1,5},{2,6},{3,7},{4,0},{5,1},{6,2},{7,3},{8,12},{9,13},{10,... | collective-permute-start | bytes 393224 | tf_op jit(solution)/shard_map/ppermute | solution.py:460
  69.0 16.7 %collective-permute-start.11 = (bf16[2,256,128]{2,1,0:T(8,128)(2,1)S(1)}, bf16[2,256,128]{2,1,0:T(8,128)(2,1)S(1)}, u32[]{:S(2)}, u32[]{:S(2)}) collective-permute-start(bf16[2,256,128]{2,1,0:T(8,128)(2,1)S(1)} %get-tuple-element.48), channel_id=1, source_target_pairs={{0,6},{1,7},{2,4},{3,5},{4,2},{5,3},{6,0},{7,1},{8,14},{9,15},{10,... | collective-permute-start | bytes 393224 | tf_op jit(solution)/shard_map/ppermute | solution.py:460
  71.3 15.0 %collective-permute-start.19 = (f32[2,32,128]{2,1,0:T(8,128)S(1)}, f32[2,32,128]{2,1,0:T(8,128)S(1)}, u32[]{:S(2)}, u32[]{:S(2)}) collective-permute-start(f32[2,32,128]{2,1,0:T(8,128)S(1)} %add_add_fusion.1), channel_id=1, source_target_pairs={{0,6},{1,7},{2,4},{3,5},{4,2},{5,3},{6,0},{7,1},{8,14},{9,15},{10,... | collective-permute-start | bytes 98312 | tf_op jit(solution)/shard_map/ppermute | solution.py:399
  72.9 16.4 %collective-permute-start.18 = (f32[2,32,128]{2,1,0:T(8,128)S(1)}, f32[2,32,128]{2,1,0:T(8,128)S(1)}, u32[]{:S(2)}, u32[]{:S(2)}) collective-permute-start(f32[2,32,128]{2,1,0:T(8,128)S(1)} %add_add_fusion.1), channel_id=1, source_target_pairs={{0,4},{1,5},{2,6},{3,7},{4,0},{5,1},{6,2},{7,3},{8,12},{9,13},{10,... | collective-permute-start | bytes 98312 | tf_op jit(solution)/shard_map/ppermute | solution.py:399
  85.7 4.0 %collective-permute-start.17 = (f32[2,32,128]{2,1,0:T(8,128)S(1)}, f32[2,32,128]{2,1,0:T(8,128)S(1)}, u32[]{:S(2)}, u32[]{:S(2)}) collective-permute-start(f32[2,32,128]{2,1,0:T(8,128)S(1)} %add_add_fusion.1), channel_id=1, source_target_pairs={{0,2},{1,3},{2,0},{3,1},{4,6},{5,7},{6,4},{7,5},{8,10},{9,11},{10,... | collective-permute-start | bytes 98312 | tf_op jit(solution)/shard_map/ppermute | solution.py:399
  86.3 4.0 %collective-permute-start.12 = (bf16[256,128]{1,0:T(8,128)(2,1)S(1)}, bf16[256,128]{1,0:T(8,128)(2,1)S(1)}, u32[]{:S(2)}, u32[]{:S(2)}) collective-permute-start(bf16[256,128]{1,0:T(8,128)(2,1)S(1)} %get-tuple-element.49), channel_id=1, source_target_pairs={{0,1},{1,0},{2,3},{3,2},{4,5},{5,4},{6,7},{7,6},{8,9},{9,8},{10,11... | collective-permute-start | bytes 196616 | tf_op jit(solution)/shard_map/ppermute | solution.py:479

commit v2 on v1

--- a/solution.py
+++ b/solution.py
@@ -15,6 +15,9 @@
 EXTRA = 8
 BIAS_ROWS = 16
 NEG = -1e30
+VMEM_MIB = 40
+ROW_TILE = 32
+JOIN = (False, True)
 SPLIT = (True, False)
 LOG2E = math.log2(math.e)
 
@@ -33,21 +36,30 @@
     return jnp.sum(spread, axis=1, keepdims=True).astype(jnp.int32)
 
 
-def attention_kernel(index_ref, plan, query_own, grad_own, far_in, *refs, carried, split):
-    chips = plan.shape[0] // CORES
-    pairs = refs[:chips]
-    refs = refs[chips + (4 if carried else 0) :]
+def lying(upright):
+    length = upright.shape[0]
+    down = lax.broadcasted_iota(jnp.int32, (length, length), 0)
+    along = lax.broadcasted_iota(jnp.int32, (length, length), 1)
+    return jnp.sum(jnp.where(down == along, upright, 0.0), axis=0, keepdims=True)
+
+
+def attention_kernel(index_ref, plan, near_in, far_in, *refs, carried, split, joined):
+    count, length = plan.shape
+    chips = count // CORES
+    blocks = chips if joined else count
+    pairs = refs[:blocks]
+    if joined:
+        pairs = [p.at[j] for p in pairs for j in range(CORES)]
+    refs = refs[blocks + (4 if carried else 0) :]
     attended, grad_query, bias, far_out = refs[:4]
     parts = refs[4 : 4 + (chips if split else 1)]
     key_t, value_t, mask, key_sum, value_sum, *work = refs[4 + len(parts) :]
-    score_refs, press_refs, weight_refs, slope_refs = (work[k : k + 2] for k in (0, 2, 4, 6))
-    count = plan.shape[0]
-    length = query_own.shape[0]
+    score_ref, press_ref, weight_ref, slope_ref = work
+    pack = score_ref.shape[0] // (CORES * length)
     scaling = HD ** (-0.5)
 
     def gathered(start):
-        found = [p[j, start : start + length, :] for p in pairs for j in range(CORES)]
-        return jnp.concatenate(found, axis=0)
+        return jnp.concatenate([p[start : start + length, :] for p in pairs], axis=0)
 
     key_t[...] = gathered(0).T
     value_t[...] = gathered(length).T
@@ -58,7 +70,7 @@
     block = slot // length
     reach = jnp.zeros_like(slot)
     for r in range(count):
-        flag = pairs[r // CORES][r % CORES, 2 * length : 2 * length + 1, 0:1]
+        flag = pairs[r][2 * length : 2 * length + 1, 0:1]
         linked = (flag.astype(jnp.float32) > 0.5).astype(jnp.int32)
         reach = reach + jnp.where(block == (index ^ r), 1, 0) * linked
     first = (block - reach) * length
@@ -71,92 +83,93 @@
     value_sum[...] = jnp.zeros_like(value_sum)
     bias[...] = jnp.zeros_like(bias)
 
-    def pick(own, far, g):
-        at = pl.ds(pl.multiple_of(g * HD, HD), HD)
-        return jnp.concatenate([own[:, at], far_in[far, :, at]], axis=0)
-
-    def before(g, s):
-        score_refs[s][...] = nn(pick(query_own, 0, g), key_t[...])
-        press_refs[s][...] = nn(pick(grad_own, 1, g), value_t[...])
-
-    def during(s):
-        for r in range(0, 2 * length, 32):
-            rows = slice(r, r + 32)
-            score = score_refs[s][rows, :] * (scaling * LOG2E) + mask[rows, :]
+    def pick(which, g):
+        found = []
+        for k in range(pack):
+            at = pl.ds(pl.multiple_of((g + k) * HD, HD), HD)
+            found += [near_in[which, :, at], far_in[which, :, at]]
+        return jnp.concatenate(found, axis=0)
+
+    def heads(j, _):
+        g = j * pack
+        query = pick(0, g)
+        grad = pick(1, g)
+        score_ref[...] = nn(query, key_t[...])
+        press_ref[...] = nn(grad, value_t[...])
+        span = CORES * length
+        for r in range(0, pack * span, ROW_TILE):
+            rows = slice(r, r + ROW_TILE)
+            at = slice(r % span, r % span + ROW_TILE)
+            score = score_ref[rows, :] * (scaling * LOG2E) + mask[at, :]
             raw = jnp.exp2(score - jnp.max(score, axis=1, keepdims=True))
             prob = raw * (1.0 / jnp.sum(raw, axis=1, keepdims=True))
-            press = press_refs[s][rows, :]
+            press = press_ref[rows, :]
             centred = jnp.sum(prob * press, axis=1, keepdims=True)
-            weight_refs[s][rows, :] = prob.astype(jnp.bfloat16)
-            slope_refs[s][rows, :] = (prob * (press - centred)).astype(jnp.bfloat16)
-
-    def after(g, s):
-        at = pl.ds(pl.multiple_of(g * HD, HD), HD)
-        weight = weight_refs[s][...]
-        slope = slope_refs[s][...]
+            weight_ref[rows, :] = prob.astype(jnp.bfloat16)
+            slope_ref[rows, :] = (prob * (press - centred)).astype(jnp.bfloat16)
+        weight = weight_ref[...]
+        slope = slope_ref[...]
         out = nn(weight, gathered(length)).astype(jnp.bfloat16)
         into = (nn(slope, gathered(0)) * scaling).astype(jnp.bfloat16)
-        attended[:, at] = out[:length]
-        grad_query[:, at] = into[:length]
-        far_out[0, :, at] = out[length:]
-        far_out[1, :, at] = into[length:]
-        bias[pl.ds(g, 1), :] = jnp.sum(into.astype(jnp.float32), axis=0, keepdims=True)
-        key_sum[...] += nn(pick(query_own, 0, g).T, slope)
-        value_sum[...] += nn(pick(grad_own, 1, g).T, weight)
-
-
-    def two_heads(j, _):
-        g = 2 * j
-        before(g, 0)
-        before(g + 1, 1)
-        during(0)
-        during(1)
-        after(g, 0)
-        after(g + 1, 1)
+        for k in range(pack):
+            at = pl.ds(pl.multiple_of((g + k) * HD, HD), HD)
+            near = slice(k * span, k * span + length)
+            away = slice(k * span + length, (k + 1) * span)
+            attended[:, at] = out[near]
+            grad_query[:, at] = into[near]
+            far_out[0, :, at] = out[away]
+            far_out[1, :, at] = into[away]
+            total = jnp.sum(into[k * span : (k + 1) * span].astype(jnp.float32), axis=0)
+            bias[pl.ds(g + k, 1), :] = total[None]
+        key_sum[...] += nn(query.T, slope)
+        value_sum[...] += nn(grad.T, weight)
         return 0
 
-    lax.fori_loop(0, GROUP // 2, two_heads, 0)
-
-    from_keys = key_sum[...].T * scaling
-    from_values = value_sum[...].T
-    bias[GROUP : GROUP + 1, :] = jnp.sum(from_values, axis=0, keepdims=True)
+    lax.fori_loop(0, GROUP // pack, heads, 0)
+    from_values = value_sum[...]
+    bias[GROUP : GROUP + 1, :] = lying(jnp.sum(from_values, axis=1, keepdims=True))
+    from_keys = (key_sum[...] * scaling).astype(jnp.bfloat16)
+    from_values = from_values.astype(jnp.bfloat16)
     for r in range(count):
-        rows = slice(r * length, (r + 1) * length)
-        both = jnp.concatenate([from_keys[rows], from_values[rows]], axis=0)
-        both = both.astype(jnp.bfloat16)
+        cols = slice(r * length, (r + 1) * length)
         if split:
-            parts[r // CORES][r % CORES] = both
+            parts[r // CORES][r % CORES, :HD, :] = from_keys[:, cols]
+            parts[r // CORES][r % CORES, HD:, :] = from_values[:, cols]
         else:
-            parts[0][pl.ds(index ^ r, 1)] = both[None]
-
-
-def attention(index, chunk, chunks, plan, query, grad, far_in, pairs, carried, split):
+            parts[0][index ^ r, :HD, :] = from_keys[:, cols]
+            parts[0][index ^ r, HD:, :] = from_values[:, cols]
+
+
+def attention(index, chunk, chunks, plan, near_in, far_in, pairs, carried, split):
     count = plan.shape[0]
     chips = count // CORES
-    length = query.shape[0]
+    _, length, half = near_in.shape
     wide = GROUP * HD
     whole = lambda *shape: pl.BlockSpec(shape, lambda i, c: (0,) * len(shape))
     mine = pl.BlockSpec((length, wide), lambda i, c: (0, chunks * (c[0] % CORES) + chunk))
     out_shape = [
-        jax.ShapeDtypeStruct(query.shape, jnp.bfloat16),
-        jax.ShapeDtypeStruct(query.shape, jnp.bfloat16),
+        jax.ShapeDtypeStruct((length, CORES * half), jnp.bfloat16),
+        jax.ShapeDtypeStruct((length, CORES * half), jnp.bfloat16),
         jax.ShapeDtypeStruct((chunks * BIAS_ROWS, HD), jnp.float32),
         jax.ShapeDtypeStruct((2, length, chunks * wide), jnp.bfloat16),
     ]
-    part = (CORES, 2 * length, HD) if split else (count, 2 * length, HD)
+    part = (CORES, 2 * HD, length) if split else (count, 2 * HD, length)
     parts = chips if split else 1
     out_shape += [jax.ShapeDtypeStruct(part, jnp.bfloat16)] * parts
     rows = CORES * length
     cols = count * length
     far = pl.BlockSpec((2, length, wide), lambda i, c: (0, 0, chunk))
-    in_specs = [whole(*plan.shape), mine, mine, far]
-    in_specs += [whole(*pairs[0].shape)] * chips
-    operands = [plan, query, grad, far_in, *pairs]
+    in_specs = [whole(*plan.shape), far, far]
+    in_specs += [whole(*pairs[0].shape)] * len(pairs)
+    operands = [plan, near_in, far_in, *pairs]
     aliases = {}
     if carried is not None:
         in_specs += [pl.BlockSpec(memory_space=pl.ANY)] * 4
-        aliases = {5 + chips + k: k for k in range(4)}
+        aliases = {4 + len(pairs) + k: k for k in range(4)}
         operands += list(carried)
+    pack = GROUP
+    while pack > 1 and pack * rows * cols > 2 * 1024 * 1024:
+        pack //= 2
     grid_spec = pltpu.PrefetchScalarGridSpec(
         num_scalar_prefetch=1,
         grid=(1,),
@@ -175,19 +188,24 @@
             pltpu.VMEM((HD, cols), jnp.float32),
             pltpu.VMEM((HD, cols), jnp.float32),
         ]
-        + [pltpu.VMEM((rows, cols), jnp.float32)] * 4
-        + [pltpu.VMEM((rows, cols), jnp.bfloat16)] * 4
+        + [pltpu.VMEM((pack * rows, cols), jnp.float32)] * 2
+        + [pltpu.VMEM((pack * rows, cols), jnp.bfloat16)] * 2
         + [
         ],
     )
     work = rows * GROUP * cols
     return pl.pallas_call(
-        functools.partial(attention_kernel, carried=carried is not None, split=split),
+        functools.partial(
+            attention_kernel,
+            carried=carried is not None,
+            split=split,
+            joined=len(pairs) == chips,
+        ),
         grid_spec=grid_spec,
         out_shape=out_shape,
         input_output_aliases=aliases,
         compiler_params=pltpu.CompilerParams(
-            vmem_limit_bytes=min(60, 8 + 10 * cols // 1024) * 1024 * 1024
+            vmem_limit_bytes=min(60, VMEM_MIB * cols // 1024) * 1024 * 1024
         ),
         cost_estimate=pl.CostEstimate(
             flops=12 * work * HD, transcendentals=work, bytes_accessed=8 * length * wide * 2
@@ -196,46 +214,45 @@
     )(index, *operands)
 
 
-def payload_kernel(index_ref, first_ref, keys, values, near, away):
-    chunks, _, _ = near.shape
+def payload_kernel(index_ref, first_ref, keys, values, *outs):
     length = keys.shape[0]
+    chunks = len(outs) // CORES
     index = index_ref[0]
     linked = (first_ref[0, 0] < index).astype(jnp.float32)
     flags = jnp.full((EXTRA, HD), linked, jnp.float32).astype(jnp.bfloat16)
     even = index % CORES == 0
     for hh in range(chunks):
+        near, away = outs[CORES * hh : CORES * (hh + 1)]
         heads = [slice((c * chunks + hh) * HD, (c * chunks + hh + 1) * HD) for c in range(CORES)]
         for at, source in ((0, keys), (length, values)):
             first, second = source[:, heads[0]], source[:, heads[1]]
-            near[hh, at : at + length, :] = jnp.where(even, first, second)
-            away[hh, at : at + length, :] = jnp.where(even, second, first)
-        near[hh, 2 * length :, :] = flags
-        away[hh, 2 * length :, :] = flags
+            near[at : at + length, :] = jnp.where(even, first, second)
+            away[at : at + length, :] = jnp.where(even, second, first)
+        near[2 * length :, :] = flags
+        away[2 * length :, :] = flags
 
 
 def payload(index, group_first, keys, values, chunks):
     length = keys.shape[0]
     smem = pl.BlockSpec(memory_space=pltpu.SMEM)
     vmem = pl.BlockSpec(memory_space=pltpu.VMEM)
-    shape = jax.ShapeDtypeStruct((chunks, 2 * length + EXTRA, HD), jnp.bfloat16)
+    shape = jax.ShapeDtypeStruct((2 * length + EXTRA, HD), jnp.bfloat16)
     return pl.pallas_call(
         payload_kernel,
         in_specs=[smem, smem, vmem, vmem],
-        out_shape=[shape] * 2,
+        out_shape=[shape] * (CORES * chunks),
         name="payload",
     )(index, group_first, keys, values)
 
 
-def join_kernel(near, away, *outs):
-    for hh, out in enumerate(outs):
-        out[0] = near[hh]
-        out[1] = away[hh]
+def join_kernel(near, away, out):
+    out[0] = near[...]
+    out[1] = away[...]
 
 
 def join(near, away):
-    chunks, rows, _ = near.shape
-    shape = jax.ShapeDtypeStruct((CORES, rows, HD), jnp.bfloat16)
-    return pl.pallas_call(join_kernel, out_shape=[shape] * chunks, name="join")(near, away)
+    shape = jax.ShapeDtypeStruct((CORES, *near.shape), jnp.bfloat16)
+    return pl.pallas_call(join_kernel, out_shape=shape, name="join")(near, away)
 
 
 def place_kernel(index_ref, far, attended_in, grad_in, attended, grad_query):
@@ -263,24 +280,23 @@
     )(index, far, attended, grad_query)
 
 
-def halves_kernel(index_ref, query, grad, out):
-    out[0] = query[...]
-    out[1] = grad[...]
+def halves_kernel(index_ref, query, grad, near, away):
+    half = near.shape[2]
+    even = index_ref[0] % CORES == 0
+    for which, source in enumerate((query, grad)):
+        first, second = source[:, :half], source[:, half:]
+        near[which] = jnp.where(even, first, second)
+        away[which] = jnp.where(even, second, first)
 
 
 def halves(index, query, grad):
     length, width = query.shape
-    theirs = pl.BlockSpec((length, width // CORES), lambda i, c: (0, 1 - c[0] % CORES))
-    grid_spec = pltpu.PrefetchScalarGridSpec(
-        num_scalar_prefetch=1,
-        grid=(1,),
-        in_specs=[theirs, theirs],
-        out_specs=pl.BlockSpec((2, length, width // CORES), lambda i, c: (0, 0, 0)),
-    )
+    shape = jax.ShapeDtypeStruct((2, length, width // CORES), query.dtype)
+    vmem = pl.BlockSpec(memory_space=pltpu.VMEM)
     return pl.pallas_call(
         halves_kernel,
-        grid_spec=grid_spec,
-        out_shape=jax.ShapeDtypeStruct((2, length, width // CORES), query.dtype),
+        in_specs=[pl.BlockSpec(memory_space=pltpu.SMEM), vmem, vmem],
+        out_shape=[shape, shape],
         name="halves",
     )(index, query, grad)
 
@@ -289,24 +305,22 @@
     total = pieces[0].astype(jnp.float32)
     for piece in pieces[1:]:
         total = total + piece.astype(jnp.float32)
-    return total.astype(jnp.bfloat16)
+    return total
 
 
 def finish_kernel(index_ref, piece, *refs):
     grad_key, grad_value = refs[-2:]
-    length = grad_key.shape[0]
     total = added([piece[z, 0] for z in range(piece.shape[0])])
-    grad_key[...] = total[:length]
-    grad_value[...] = total[length:]
+    grad_key[...] = total[:HD].T.astype(jnp.bfloat16)
+    grad_value[...] = total[HD:].T.astype(jnp.bfloat16)
 
 
 def settle_kernel(index_ref, *refs, count):
     grad_key, grad_value, away = refs[-3:]
-    length = grad_key.shape[0]
     total = added([piece[0] for piece in refs[:count]])
-    grad_key[...] = total[:length]
-    grad_value[...] = total[length:]
-    away[...] = added([piece[1] for piece in refs[:count]])
+    grad_key[...] = total[:HD].T.astype(jnp.bfloat16)
+    grad_value[...] = total[HD:].T.astype(jnp.bfloat16)
+    away[...] = added([piece[1] for piece in refs[:count]]).astype(jnp.bfloat16)
 
 
 def into_grads(kernel, index, grid, specs, operands, heads, shape, extra, carried):
@@ -335,11 +349,13 @@
 
 
 def finish(index, chunk, chunks, piece, shape, carried):
-    count, rows, _ = piece.shape
-    piece = piece.reshape(count // CORES, CORES, rows, HD)
-    spec = pl.BlockSpec((count // CORES, 1, rows, HD), lambda i, c: (0, i, 0, 0))
+    count, rows, length = piece.shape
+    piece = piece.reshape(count // CORES, CORES, rows, length)
+    spec = pl.BlockSpec((count // CORES, 1, rows, length), lambda i, c: (0, i, 0, 0))
     heads = lambda i, c: (0, i * chunks + chunk)
-    return into_grads(finish_kernel, index, CORES, [spec], [piece], heads, shape, None, carried)
+    return into_grads(
+        finish_kernel, index, CORES, [spec], [piece], heads, shape, None, carried
+    )
 
 
 def settle(index, chunk, chunks, pieces, shape, carried):
@@ -347,14 +363,18 @@
     heads = lambda i, c: (0, (c[0] % CORES) * chunks + chunk)
     kernel = functools.partial(settle_kernel, count=len(pieces))
     extra = pieces[0].shape[1:]
-    return into_grads(kernel, index, 1, [spec] * len(pieces), pieces, heads, shape, extra, carried)
+    return into_grads(
+        kernel, index, 1, [spec] * len(pieces), pieces, heads, shape, extra, carried
+    )
 
 
 def receive(index, chunk, chunks, piece, shape, carried):
     piece = piece[None, None]
     spec = pl.BlockSpec(piece.shape, lambda i, c: (0, 0, 0, 0))
     heads = lambda i, c: (0, (1 - c[0] % CORES) * chunks + chunk)
-    return into_grads(finish_kernel, index, 1, [spec], [piece], heads, shape, None, carried)
+    return into_grads(
+        finish_kernel, index, 1, [spec], [piece], heads, shape, None, carried
+    )
 
 
 def bias_kernel(index_ref, sums, bias_grad, *, chunks, factor):
@@ -396,7 +416,8 @@
     total = part
     for pick in range(1, 2 ** len(steps)):
         mixed = sum(step for k, step in enumerate(steps) if pick >> k & 1)
-        total = total + lax.ppermute(part, axis, [(i, i ^ mixed) for i in range(size)])
+        moved = lax.ppermute(part, axis, [(i, i ^ mixed) for i in range(size)])
+        total = total + moved
     return total
 
 
@@ -425,16 +446,25 @@
     def over(k):
         return [(i, i ^ (CORES * k)) for i in range(devices)]
 
-    near, away = payload(index_arg, group_first, key_rows, value_rows, chunks)
-    away = lax.ppermute(away, "ctx", across)
-    joined = join(near, away)
+    def xor(r):
+        return [(i, i ^ r) for i in range(devices)]
+
+    blocks = payload(index_arg, group_first, key_rows, value_rows, chunks)
     gathered = []
     for hh in range(chunks):
-        pairs = [joined[hh]] * chips
-        for k in order:
-            pairs[k] = lax.ppermute(joined[hh], "ctx", over(k))
+        mine = blocks[CORES * hh : CORES * (hh + 1)]
+        if JOIN[hh % len(JOIN)]:
+            away = lax.ppermute(mine[1], "ctx", across)
+            both = join(mine[0], away)
+            pairs = [both] * chips
+            for k in order:
+                pairs[k] = lax.ppermute(both, "ctx", over(k))
+        else:
+            pairs = [mine[0]] * devices
+            for r in range(devices - 1, 0, -1):
+                pairs[r] = lax.ppermute(mine[r % CORES], "ctx", xor(r))
         gathered.append(pairs)
-    far_in = halves(index_arg, query_rows, out_grad)
+    near_in, far_in = halves(index_arg, query_rows, out_grad)
     far_in = lax.ppermute(far_in, "ctx", across)
 
     carried = None
@@ -446,8 +476,7 @@
             hh,
             chunks,
             plan,
-            query_rows,
-            out_grad,
+            near_in,
             far_in,
             gathered[hh],
             carried,

time: 93 us -> 85.2 us (0.916)
  Pallas kernels: 30.8 us -> 27.9 us
  starting transfers between devices: 37.4 us -> 34.9 us
  waiting for transfers between devices: 21.6 us -> 19.4 us
    pallas_call x2, Pallas kernels: 21.3 us -> 17.5 us  [attention(): pl.pallas_call(functools.partial(attention_kernel, carried=carried is not...]
    ppermute x12 -> x17, starting transfers between devices: 25.4 us -> 23.2 us  [the longest x6 9.53 us: summed(): moved = lax.ppermute(part, axis, [(i, i ^ mixed) for i in range(size)])]
    ppermute x2 -> x1, waiting for transfers between devices: 1.55 us -> 0.01 us  [body(): away = lax.ppermute(away, 'ctx', across)]
    ppermute x12 -> x17, waiting for transfers between devices: 10.8 us -> 10.2 us  [the longest x7 4.91 us: body(): pairs[r] = lax.ppermute(mine[r % CORES], 'ctx', xor(r))]
  transfers between devices with their start and end apart: 21 -> 25, of which waited for: 7 -> 6; matrix products, arithmetic and copies ran while one was open for 0% -> 0% of each run, Pallas kernels for 18% -> 18%
where the time goes in v2:
time: 85.2 us; the launch traced here: 84.9 us
  starting transfers between devices  34.9 us (41%)
  Pallas kernels  27.9 us (33%)
  waiting for transfers between devices  19.4 us (23%)
  between operations  1.38 us (2%)
  local copies, waits for them, and re-layouts  1.24 us (1%)
    pallas_call x2, Pallas kernels, attention(): pl.pallas_call(functools.partial(attention_kernel, carried=carried is not...  17.5 us
    ppermute x6, starting transfers between devices, summed(): moved = lax.ppermute(part, axis, [(i, i ^ mixed) for i in range(size)])  9.53 us
    ppermute x7, starting transfers between devices, body(): pairs[r] = lax.ppermute(mine[r % CORES], 'ctx', xor(r))  8.29 us
    ppermute x3, waiting for transfers between devices, body(): pieces[k] = lax.ppermute(parts[k], 'ctx', over(k))  8.28 us
    ppermute x3, starting transfers between devices, body(): pieces[k] = lax.ppermute(parts[k], 'ctx', over(k))  6.45 us
    ppermute x3, starting transfers between devices, body(): pairs[k] = lax.ppermute(both, 'ctx', over(k))  5.4 us
    ppermute x7, waiting for transfers between devices, body(): pairs[r] = lax.ppermute(mine[r % CORES], 'ctx', xor(r))  4.91 us
    all_to_all x1, starting transfers between devices, body(): lax.all_to_all(parts[0], 'ctx', split_axis=0, concat_axis=0, tiled=True)  4.17 us
  transfers between devices with their start and end apart: 25, of which 6 were waited for; matrix products, arithmetic and copies ran while one was open for 0% of the time, Pallas kernels for 18%

profile of v2, /device:TPU:0, one launch (start us, length us, event | category | flops | bytes accessed | tf_op | source)
XLA Modules:
  0.0 84.9 jit_solution(17402327891960098542)
XLA Ops:
  0.6 3.0 %halves.1 = (bf16[2,128,2048]{2,1,0:T(8,128)(2,1)}, bf16[2,128,2048]{2,1,0:T(8,128)(2,1)}) custom-call(s32[1]{0:T(128)} %bitcast.index_ref, bf16[128,4096]{1,0:T(8,128)(2,1)} %query.1, bf16[128,4096]{1,0:T(8,128)(2,1)} %grad.1), custom_call_target="tpu_custom_call" | custom-call | tf_op jit(solution)/shard_map/halves/pallas_call | solution.py:296
  3.6 0.5 collective-permute-start
  4.8 1.7 %payload.1 = (bf16[264,128]{1,0:T(8,128)(2,1)}, bf16[264,128]{1,0:T(8,128)(2,1)}, bf16[264,128]{1,0:T(8,128)(2,1)}, bf16[264,128]{1,0:T(8,128)(2,1)}) custom-call(s32[1]{0:T(128)} %bitcast.index_ref, s32[1,1]{1,0:T(1,128)S(6)} %copy.31.first_ref, bf16[128,512]{1,0:T(8,128)(2,1)} %keys.1, bf16[128,512]{1,0:T(8,128)(2,1)} %values.1), custom_call_target="tpu_custom_call" | custom-call | tf_op jit(solution)/shard_map/payload/pallas_call | solution.py:240
  6.5 0.0 collective-permute-start.1
  6.5 5.1 %collective-permute-start.10 = (bf16[264,128]{1,0:T(8,128)(2,1)}, bf16[264,128]{1,0:T(8,128)(2,1)S(1)}, u32[]{:S(2)}, u32[]{:S(2)}) collective-permute-start(bf16[264,128]{1,0:T(8,128)(2,1)} %get-tuple-element.37.refs_0_), channel_id=1, source_target_pairs={{0,6},{1,7},{2,4},{3,5},{4,2},{5,3},{6,0},{7,1},{8,14},{9,15},{10,... | collective-permute-start | bytes 202760 | tf_op jit(solution)/shard_map/ppermute | solution.py:465
  11.6 0.0 collective-permute-start.8
  11.6 0.6 collective-permute-start.6
  12.2 0.0 collective-permute-done.1.away
  12.2 2.6 %collective-permute-start.11 = (bf16[264,128]{1,0:T(8,128)(2,1)}, bf16[264,128]{1,0:T(8,128)(2,1)S(1)}, u32[]{:S(2)}, u32[]{:S(2)}) collective-permute-start(bf16[264,128]{1,0:T(8,128)(2,1)} %get-tuple-element.38), channel_id=1, source_target_pairs={{0,7},{1,6},{2,5},{3,4},{4,3},{5,2},{6,1},{7,0},{8,15},{9,14},{10,... | collective-permute-start | bytes 202760 | tf_op jit(solution)/shard_map/ppermute | solution.py:465
  14.7 0.0 collective-permute-done.10.refs_6_
  14.8 0.1 collective-permute-start.9
  14.8 4.9 %collective-permute-done.8.refs_4_ = bf16[264,128]{1,0:T(8,128)(2,1)S(1)} collective-permute-done((bf16[264,128]{1,0:T(8,128)(2,1)}, bf16[264,128]{1,0:T(8,128)(2,1)S(1)}, u32[]{:S(2)}, u32[]{:S(2)}) %collective-permute-start.8) | collective-permute-done | bytes 67616 | tf_op jit(solution)/shard_map/ppermute | solution.py:465
  19.7 0.0 collective-permute-start.7
  19.7 0.0 collective-permute-done.6.refs_2_
  19.7 0.0 collective-permute-start.5
  19.7 0.0 copy-start.3
  19.7 1.6 %join.1.refs_0_ = bf16[2,264,128]{2,1,0:T(8,128)(2,1)} custom-call(bf16[264,128]{1,0:T(8,128)(2,1)} %get-tuple-element.35.near, bf16[264,128]{1,0:T(8,128)(2,1)} %copy-done.4), custom_call_target="tpu_custom_call" | custom-call | tf_op jit(solution)/shard_map/join/pallas_call | solution.py:255
  21.3 0.0 collective-permute-done.11.refs_7_
  21.4 4.1 %collective-permute-start.4 = (bf16[2,264,128]{2,1,0:T(8,128)(2,1)}, bf16[2,264,128]{2,1,0:T(8,128)(2,1)S(1)}, u32[]{:S(2)}, u32[]{:S(2)}) collective-permute-start(bf16[2,264,128]{2,1,0:T(8,128)(2,1)} %join.1.refs_0_), channel_id=1, source_target_pairs={{0,6},{1,7},{2,4},{3,5},{4,2},{5,3},{6,0},{7,1},{8,14},{9,15},{10,... | collective-permute-start | bytes 405512 | tf_op jit(solution)/shard_map/ppermute | solution.py:461
  25.5 0.0 collective-permute-done.9.refs_5_
  25.5 0.7 collective-permute-start.3
  26.2 0.0 collective-permute-done.7.refs_3_
  26.2 0.6 collective-permute-start.2
  26.8 0.0 collective-permute-done.5.refs_1_
  26.8 0.0 collective-permute-done.far_in
  26.8 0.0 copy-done.2
  26.8 0.0 copy-start.1
  26.8 1.2 %copy-done.1 = bf16[2,128,2048]{2,1,0:T(8,128)(2,1)S(1)} copy-done((bf16[2,128,2048]{2,1,0:T(8,128)(2,1)S(1)}, bf16[2,128,2048]{2,1,0:T(8,128)(2,1)}, u32[]{:S(2)}) %copy-start.1) | copy-done | bytes 1048600
  28.0 8.6 %attention.2 = (bf16[128,4096]{1,0:T(8,128)(2,1)}, bf16[128,4096]{1,0:T(8,128)(2,1)}, f32[32,128]{1,0:T(8,128)S(1)}, bf16[2,128,2048]{2,1,0:T(8,128)(2,1)S(1)}, ...) custom-call(s32[1]{0:T(128)} %bitcast.index_ref, ...), custom_call_target="tpu_custom_call" | custom-call | flops 3221225472 | bytes 2097152 | tf_op jit(solution)/shard_map/attention/pallas_call | solution.py:197
  36.6 0.0 collective-permute-done.4.refs_3_
  36.6 2.0 %collective-permute-done.3.refs_2_ = bf16[2,264,128]{2,1,0:T(8,128)(2,1)S(1)} collective-permute-done((bf16[2,264,128]{2,1,0:T(8,128)(2,1)}, bf16[2,264,128]{2,1,0:T(8,128)(2,1)S(1)}, u32[]{:S(2)}, u32[]{:S(2)}) %collective-permute-start.3) | collective-permute-done | bytes 135200 | tf_op jit(solution)/shard_map/ppermute | solution.py:461
  38.6 0.0 collective-permute-done.2.refs_1_
  38.6 9.0 %attention.3 = (bf16[128,4096]{1,0:T(8,128)(2,1)}, bf16[128,4096]{1,0:T(8,128)(2,1)}, f32[32,128]{1,0:T(8,128)S(1)}, bf16[2,128,2048]{2,1,0:T(8,128)(2,1)S(1)}, bf16[8,256,128]{2,1,0:T(8,128)(2,1)}) custom-call(s32[1]{0:T(128)} %bitcast.index_ref, s32[8,128]{1,0:T(8,128)S(1)} %bitcast.12, ...), custom_call_target="tpu_custom_call", output_to_operand_aliasing={{0}: (8, {}), {1}: (9, {}), {2}: (10, {}), {3}: (11, {})} | custom-call | flops 3221225472 | bytes 2097152 | tf_op jit(solution)/shard_map/attention/pallas_call | solution.py:197
  47.6 0.0 collective-permute-start.12
  47.6 4.2 %all-to-all-start = ((bf16[8,256,128]{2,1,0:T(8,128)(2,1)}), bf16[8,256,128]{2,1,0:T(8,128)(2,1)S(1)}, u32[]{:S(2)}, u32[]{:S(2)}) async-start(bf16[8,256,128]{2,1,0:T(8,128)(2,1)} %get-tuple-element.48), calls=%async_computation | async-start | bytes 1048576 | tf_op jit(solution)/shard_map/all_to_all | solution.py:493
  51.8 0.5 collective-permute-start.17
  52.3 1.0 %collective-permute-done.17 = f32[32,128]{1,0:T(8,128)S(1)} collective-permute-done((f32[32,128]{1,0:T(8,128)S(1)}, f32[32,128]{1,0:T(8,128)S(1)}, u32[]{:S(2)}, u32[]{:S(2)}) %collective-permute-start.17) | collective-permute-done | bytes 16416 | tf_op jit(solution)/shard_map/ppermute | solution.py:498
  53.3 1.5 %collective-permute-start.19 = (f32[2,32,128]{2,1,0:T(8,128)S(1)}, f32[2,32,128]{2,1,0:T(8,128)S(1)}, u32[]{:S(2)}, u32[]{:S(2)}) collective-permute-start(f32[2,32,128]{2,1,0:T(8,128)S(1)} %pad_maximum_fusion), channel_id=1, source_target_pairs={{0,16},{8,24},{16,0},{24,8},{1,17},{9,25},{17,1},{25,9},{2,18},{10... | collective-permute-start | bytes 98312 | tf_op jit(solution)/shard_map/ppermute | solution.py:419
  54.8 1.4 %collective-permute-start.20 = (f32[2,32,128]{2,1,0:T(8,128)S(1)}, f32[2,32,128]{2,1,0:T(8,128)S(1)}, u32[]{:S(2)}, u32[]{:S(2)}) collective-permute-start(f32[2,32,128]{2,1,0:T(8,128)S(1)} %pad_maximum_fusion), channel_id=1, source_target_pairs={{0,24},{8,16},{16,8},{24,0},{1,25},{9,17},{17,9},{25,1},{2,26},{10... | collective-permute-start | bytes 98312 | tf_op jit(solution)/shard_map/ppermute | solution.py:419
  56.2 0.5 collective-permute-start.18
  56.8 1.7 %collective-permute-start.13 = (bf16[2,256,128]{2,1,0:T(8,128)(2,1)S(1)}, bf16[2,256,128]{2,1,0:T(8,128)(2,1)S(1)}, u32[]{:S(2)}, u32[]{:S(2)}) collective-permute-start(bf16[2,256,128]{2,1,0:T(8,128)(2,1)S(1)} %get-tuple-element.50), channel_id=1, source_target_pairs={{0,2},{1,3},{2,0},{3,1},{4,6},{5,7},{6,4},{7,5},{8,10},{9,11},{10,... | collective-permute-start | bytes 393224 | tf_op jit(solution)/shard_map/ppermute | solution.py:489
  58.5 0.0 collective-permute-done.19
  58.5 2.4 %collective-permute-start.14 = (bf16[2,256,128]{2,1,0:T(8,128)(2,1)S(1)}, bf16[2,256,128]{2,1,0:T(8,128)(2,1)S(1)}, u32[]{:S(2)}, u32[]{:S(2)}) collective-permute-start(bf16[2,256,128]{2,1,0:T(8,128)(2,1)S(1)} %get-tuple-element.51), channel_id=1, source_target_pairs={{0,4},{1,5},{2,6},{3,7},{4,0},{5,1},{6,2},{7,3},{8,12},{9,13},{10,... | collective-permute-start | bytes 393224 | tf_op jit(solution)/shard_map/ppermute | solution.py:489
  60.9 0.0 collective-permute-done.20
  60.9 2.4 %collective-permute-start.15 = (bf16[2,256,128]{2,1,0:T(8,128)(2,1)S(1)}, bf16[2,256,128]{2,1,0:T(8,128)(2,1)S(1)}, u32[]{:S(2)}, u32[]{:S(2)}) collective-permute-start(bf16[2,256,128]{2,1,0:T(8,128)(2,1)S(1)} %get-tuple-element.52), channel_id=1, source_target_pairs={{0,6},{1,7},{2,4},{3,5},{4,2},{5,3},{6,0},{7,1},{8,14},{9,15},{10,... | collective-permute-start | bytes 393224 | tf_op jit(solution)/shard_map/ppermute | solution.py:489
  63.2 0.0 collective-permute-done.18
  63.2 1.5 %collective-permute-start.23 = (f32[2,32,128]{2,1,0:T(8,128)S(1)}, f32[2,32,128]{2,1,0:T(8,128)S(1)}, u32[]{:S(2)}, u32[]{:S(2)}) collective-permute-start(f32[2,32,128]{2,1,0:T(8,128)S(1)} %add_add_fusion.1), channel_id=1, source_target_pairs={{0,6},{1,7},{2,4},{3,5},{4,2},{5,3},{6,0},{7,1},{8,14},{9,15},{10,... | collective-permute-start | bytes 98312 | tf_op jit(solution)/shard_map/ppermute | solution.py:419
  64.8 0.0 collective-permute-done.13.refs_1_
  64.8 4.5 %collective-permute-start.22 = (f32[2,32,128]{2,1,0:T(8,128)S(1)}, f32[2,32,128]{2,1,0:T(8,128)S(1)}, u32[]{:S(2)}, u32[]{:S(2)}) collective-permute-start(f32[2,32,128]{2,1,0:T(8,128)S(1)} %add_add_fusion.1), channel_id=1, source_target_pairs={{0,4},{1,5},{2,6},{3,7},{4,0},{5,1},{6,2},{7,3},{8,12},{9,13},{10,... | collective-permute-start | bytes 98312 | tf_op jit(solution)/shard_map/ppermute | solution.py:419
  69.3 8.3 %collective-permute-done.14.refs_2_ = bf16[2,256,128]{2,1,0:T(8,128)(2,1)S(1)} collective-permute-done((bf16[2,256,128]{2,1,0:T(8,128)(2,1)S(1)}, bf16[2,256,128]{2,1,0:T(8,128)(2,1)S(1)}, u32[]{:S(2)}, u32[]{:S(2)}) %collective-permute-start.14) | collective-permute-done | bytes 131104 | tf_op jit(solution)/shard_map/ppermute | solution.py:489
  77.6 0.0 collective-permute-start.21
  77.6 0.0 collective-permute-done.15.refs_3_
  77.6 0.7 shard_map.101
  78.3 0.0 collective-permute-start.16
  78.3 0.0 collective-permute-done.23
  78.3 2.9 %collective-permute-done.22 = f32[2,32,128]{2,1,0:T(8,128)S(1)} collective-permute-done((f32[2,32,128]{2,1,0:T(8,128)S(1)}, f32[2,32,128]{2,1,0:T(8,128)S(1)}, u32[]{:S(2)}, u32[]{:S(2)}) %collective-permute-start.22) | collective-permute-done | bytes 32800 | tf_op jit(solution)/shard_map/ppermute | solution.py:419
  81.2 0.3 collective-permute-done.21
  81.6 0.6 bias.1
  82.2 0.0 collective-permute-done.16
  82.2 0.7 shard_map.102
  82.9 0.0 all-to-all-done
  82.9 0.9 %shard_map.103 = (bf16[128,512]{1,0:T(8,128)(2,1)}, bf16[128,512]{1,0:T(8,128)(2,1)}) custom-call(s32[1]{0:T(128)} %bitcast.index_ref, bf16[4,2,256,128]{3,2,1,0:T(8,128)(2,1)S(1)} %bitcast.7, bf16[128,512]{1,0:T(8,128)(2,1)} %get-tuple-element.56.refs_0_, bf16[128,512]{1,0:T(8,128)(2,1)} %get-tuple-element.57.refs_1_), custom_call_target="tpu_custom_call", output_to_operand_aliasing={{0}: (2, {}), {1}: (3, {})} | custom-call | tf_op jit(solution)/shard_map/pallas_call | solution.py:342
  83.8 0.0 collective-permute-done.12.far
  83.8 1.0 %place.1 = (bf16[128,4096]{1,0:T(8,128)(2,1)}, bf16[128,4096]{1,0:T(8,128)(2,1)}) custom-call(s32[1]{0:T(128)} %bitcast.index_ref, bf16[2,128,2048]{2,1,0:T(8,128)(2,1)S(1)} %collective-permute-done.12.far, bf16[128,4096]{1,0:T(8,128)(2,1)} %get-tuple-element.44.attended_in, ...), custom_call_target="tpu_custom_call", output_to_operand_aliasing={{0}: (2, {}), {1}: (3, {})} | custom-call | tf_op jit(solution)/shard_map/place/pallas_call | solution.py:273
  (9 shorter events, 0.0 us)
Async XLA Ops:
  3.6 23.1 %collective-permute-start = (bf16[2,128,2048]{2,1,0:T(8,128)(2,1)}, bf16[2,128,2048]{2,1,0:T(8,128)(2,1)S(1)}, u32[]{:S(2)}, u32[]{:S(2)}) collective-permute-start(bf16[2,128,2048]{2,1,0:T(8,128)(2,1)} %get-tuple-element.34), channel_id=1, source_target_pairs={{0,1},{1,0},{2,3},{3,2},{4,5},{5,4},{6,7},{7,6},{8,9},{9,8},{10,11... | collective-permute-start | bytes 3145736 | tf_op jit(solution)/shard_map/ppermute | solution.py:468
  6.5 5.7 %collective-permute-start.1 = (bf16[264,128]{1,0:T(8,128)(2,1)}, bf16[264,128]{1,0:T(8,128)(2,1)S(1)}, u32[]{:S(2)}, u32[]{:S(2)}) collective-permute-start(bf16[264,128]{1,0:T(8,128)(2,1)} %get-tuple-element.36), channel_id=1, source_target_pairs={{0,1},{1,0},{2,3},{3,2},{4,5},{5,4},{6,7},{7,6},{8,9},{9,8},{10,11... | collective-permute-start | bytes 202760 | tf_op jit(solution)/shard_map/ppermute | solution.py:457
  6.5 8.2 %collective-permute-start.10 = (bf16[264,128]{1,0:T(8,128)(2,1)}, bf16[264,128]{1,0:T(8,128)(2,1)S(1)}, u32[]{:S(2)}, u32[]{:S(2)}) collective-permute-start(bf16[264,128]{1,0:T(8,128)(2,1)} %get-tuple-element.37.refs_0_), channel_id=1, source_target_pairs={{0,6},{1,7},{2,4},{3,5},{4,2},{5,3},{6,0},{7,1},{8,14},{9,15},{10,... | collective-permute-start | bytes 202760 | tf_op jit(solution)/shard_map/ppermute | solution.py:465
  11.6 8.1 %collective-permute-start.8 = (bf16[264,128]{1,0:T(8,128)(2,1)}, bf16[264,128]{1,0:T(8,128)(2,1)S(1)}, u32[]{:S(2)}, u32[]{:S(2)}) collective-permute-start(bf16[264,128]{1,0:T(8,128)(2,1)} %get-tuple-element.37.refs_0_), channel_id=1, source_target_pairs={{0,4},{1,5},{2,6},{3,7},{4,0},{5,1},{6,2},{7,3},{8,12},{9,13},{10,... | collective-permute-start | bytes 202760 | tf_op jit(solution)/shard_map/ppermute | solution.py:465
  11.6 8.1 %collective-permute-start.6 = (bf16[264,128]{1,0:T(8,128)(2,1)}, bf16[264,128]{1,0:T(8,128)(2,1)S(1)}, u32[]{:S(2)}, u32[]{:S(2)}) collective-permute-start(bf16[264,128]{1,0:T(8,128)(2,1)} %get-tuple-element.37.refs_0_), channel_id=1, source_target_pairs={{0,2},{1,3},{2,0},{3,1},{4,6},{5,7},{6,4},{7,5},{8,10},{9,11},{10,... | collective-permute-start | bytes 202760 | tf_op jit(solution)/shard_map/ppermute | solution.py:465
  12.2 7.6 %copy-start.4 = (bf16[264,128]{1,0:T(8,128)(2,1)}, bf16[264,128]{1,0:T(8,128)(2,1)S(1)}, u32[]{:S(2)}) copy-start(bf16[264,128]{1,0:T(8,128)(2,1)S(1)} %collective-permute-done.1.away) | copy-start | bytes 202756
  12.2 9.2 %collective-permute-start.11 = (bf16[264,128]{1,0:T(8,128)(2,1)}, bf16[264,128]{1,0:T(8,128)(2,1)S(1)}, u32[]{:S(2)}, u32[]{:S(2)}) collective-permute-start(bf16[264,128]{1,0:T(8,128)(2,1)} %get-tuple-element.38), channel_id=1, source_target_pairs={{0,7},{1,6},{2,5},{3,4},{4,3},{5,2},{6,1},{7,0},{8,15},{9,14},{10,... | collective-permute-start | bytes 202760 | tf_op jit(solution)/shard_map/ppermute | solution.py:465
  14.8 10.7 %collective-permute-start.9 = (bf16[264,128]{1,0:T(8,128)(2,1)}, bf16[264,128]{1,0:T(8,128)(2,1)S(1)}, u32[]{:S(2)}, u32[]{:S(2)}) collective-permute-start(bf16[264,128]{1,0:T(8,128)(2,1)} %get-tuple-element.38), channel_id=1, source_target_pairs={{0,5},{1,4},{2,7},{3,6},{4,1},{5,0},{6,3},{7,2},{8,13},{9,12},{10,... | collective-permute-start | bytes 202760 | tf_op jit(solution)/shard_map/ppermute | solution.py:465
  19.7 6.5 %collective-permute-start.7 = (bf16[264,128]{1,0:T(8,128)(2,1)}, bf16[264,128]{1,0:T(8,128)(2,1)S(1)}, u32[]{:S(2)}, u32[]{:S(2)}) collective-permute-start(bf16[264,128]{1,0:T(8,128)(2,1)} %get-tuple-element.38), channel_id=1, source_target_pairs={{0,3},{1,2},{2,1},{3,0},{4,7},{5,6},{6,5},{7,4},{8,11},{9,10},{10,... | collective-permute-start | bytes 202760 | tf_op jit(solution)/shard_map/ppermute | solution.py:465
  19.7 7.1 %collective-permute-start.5 = (bf16[264,128]{1,0:T(8,128)(2,1)}, bf16[264,128]{1,0:T(8,128)(2,1)S(1)}, u32[]{:S(2)}, u32[]{:S(2)}) collective-permute-start(bf16[264,128]{1,0:T(8,128)(2,1)} %get-tuple-element.38), channel_id=1, source_target_pairs={{0,1},{1,0},{2,3},{3,2},{4,5},{5,4},{6,7},{7,6},{8,9},{9,8},{10,11... | collective-permute-start | bytes 202760 | tf_op jit(solution)/shard_map/ppermute | solution.py:465
  19.7 7.0 %copy-start.2 = (bf16[264,128]{1,0:T(8,128)(2,1)S(1)}, bf16[264,128]{1,0:T(8,128)(2,1)}, u32[]{:S(2)}) copy-start(bf16[264,128]{1,0:T(8,128)(2,1)} %get-tuple-element.37.refs_0_) | copy-start | bytes 202756
  19.7 7.0 %copy-start.3 = (s32[1,1024]{1,0:T(1,128)S(1)}, s32[1,1024]{1,0:T(1,128)}, u32[]{:S(2)}) copy-start(s32[1,1024]{1,0:T(1,128)} %param.10) | copy-start | bytes 12292
  21.4 15.2 %collective-permute-start.4 = (bf16[2,264,128]{2,1,0:T(8,128)(2,1)}, bf16[2,264,128]{2,1,0:T(8,128)(2,1)S(1)}, u32[]{:S(2)}, u32[]{:S(2)}) collective-permute-start(bf16[2,264,128]{2,1,0:T(8,128)(2,1)} %join.1.refs_0_), channel_id=1, source_target_pairs={{0,6},{1,7},{2,4},{3,5},{4,2},{5,3},{6,0},{7,1},{8,14},{9,15},{10,... | collective-permute-start | bytes 405512 | tf_op jit(solution)/shard_map/ppermute | solution.py:461
  25.5 13.1 %collective-permute-start.3 = (bf16[2,264,128]{2,1,0:T(8,128)(2,1)}, bf16[2,264,128]{2,1,0:T(8,128)(2,1)S(1)}, u32[]{:S(2)}, u32[]{:S(2)}) collective-permute-start(bf16[2,264,128]{2,1,0:T(8,128)(2,1)} %join.1.refs_0_), channel_id=1, source_target_pairs={{0,4},{1,5},{2,6},{3,7},{4,0},{5,1},{6,2},{7,3},{8,12},{9,13},{10,... | collective-permute-start | bytes 405512 | tf_op jit(solution)/shard_map/ppermute | solution.py:461
  26.2 12.4 %collective-permute-start.2 = (bf16[2,264,128]{2,1,0:T(8,128)(2,1)}, bf16[2,264,128]{2,1,0:T(8,128)(2,1)S(1)}, u32[]{:S(2)}, u32[]{:S(2)}) collective-permute-start(bf16[2,264,128]{2,1,0:T(8,128)(2,1)} %join.1.refs_0_), channel_id=1, source_target_pairs={{0,2},{1,3},{2,0},{3,1},{4,6},{5,7},{6,4},{7,5},{8,10},{9,11},{10,... | collective-permute-start | bytes 405512 | tf_op jit(solution)/shard_map/ppermute | solution.py:461
  26.8 1.2 %copy-start.1 = (bf16[2,128,2048]{2,1,0:T(8,128)(2,1)S(1)}, bf16[2,128,2048]{2,1,0:T(8,128)(2,1)}, u32[]{:S(2)}) copy-start(bf16[2,128,2048]{2,1,0:T(8,128)(2,1)} %get-tuple-element.33.near_in) | copy-start | bytes 3145732
  28.0 10.6 %copy-start = (bf16[2,264,128]{2,1,0:T(8,128)(2,1)S(1)}, bf16[2,264,128]{2,1,0:T(8,128)(2,1)}, u32[]{:S(2)}) copy-start(bf16[2,264,128]{2,1,0:T(8,128)(2,1)} %join.1.refs_0_) | copy-start | bytes 405508
  47.6 36.3 %collective-permute-start.12 = (bf16[2,128,2048]{2,1,0:T(8,128)(2,1)S(1)}, bf16[2,128,2048]{2,1,0:T(8,128)(2,1)S(1)}, u32[]{:S(2)}, u32[]{:S(2)}) collective-permute-start(bf16[2,128,2048]{2,1,0:T(8,128)(2,1)S(1)} %get-tuple-element.43), channel_id=1, source_target_pairs={{0,1},{1,0},{2,3},{3,2},{4,5},{5,4},{6,7},{7,6},{8,9},{9,8},{10,11... | collective-permute-start | bytes 3145736 | tf_op jit(solution)/shard_map/ppermute | solution.py:496
  47.6 35.3 %all-to-all-start = ((bf16[8,256,128]{2,1,0:T(8,128)(2,1)}), bf16[8,256,128]{2,1,0:T(8,128)(2,1)S(1)}, u32[]{:S(2)}, u32[]{:S(2)}) async-start(bf16[8,256,128]{2,1,0:T(8,128)(2,1)} %get-tuple-element.48), calls=%async_computation | async-start | bytes 1048576 | tf_op jit(solution)/shard_map/all_to_all | solution.py:493
  51.8 1.5 %collective-permute-start.17 = (f32[32,128]{1,0:T(8,128)S(1)}, f32[32,128]{1,0:T(8,128)S(1)}, u32[]{:S(2)}, u32[]{:S(2)}) collective-permute-start(f32[32,128]{1,0:T(8,128)S(1)} %get-tuple-element.60), channel_id=1, source_target_pairs={{0,1},{1,0},{2,3},{3,2},{4,5},{5,4},{6,7},{7,6},{8,9},{9,8},{10,11... | collective-permute-start | bytes 49160 | tf_op jit(solution)/shard_map/ppermute | solution.py:498
  53.3 5.2 %collective-permute-start.19 = (f32[2,32,128]{2,1,0:T(8,128)S(1)}, f32[2,32,128]{2,1,0:T(8,128)S(1)}, u32[]{:S(2)}, u32[]{:S(2)}) collective-permute-start(f32[2,32,128]{2,1,0:T(8,128)S(1)} %pad_maximum_fusion), channel_id=1, source_target_pairs={{0,16},{8,24},{16,0},{24,8},{1,17},{9,25},{17,1},{25,9},{2,18},{10... | collective-permute-start | bytes 98312 | tf_op jit(solution)/shard_map/ppermute | solution.py:419
  54.8 6.1 %collective-permute-start.20 = (f32[2,32,128]{2,1,0:T(8,128)S(1)}, f32[2,32,128]{2,1,0:T(8,128)S(1)}, u32[]{:S(2)}, u32[]{:S(2)}) collective-permute-start(f32[2,32,128]{2,1,0:T(8,128)S(1)} %pad_maximum_fusion), channel_id=1, source_target_pairs={{0,24},{8,16},{16,8},{24,0},{1,25},{9,17},{17,9},{25,1},{2,26},{10... | collective-permute-start | bytes 98312 | tf_op jit(solution)/shard_map/ppermute | solution.py:419
  56.2 7.0 %collective-permute-start.18 = (f32[2,32,128]{2,1,0:T(8,128)S(1)}, f32[2,32,128]{2,1,0:T(8,128)S(1)}, u32[]{:S(2)}, u32[]{:S(2)}) collective-permute-start(f32[2,32,128]{2,1,0:T(8,128)S(1)} %pad_maximum_fusion), channel_id=1, source_target_pairs={{0,8},{8,0},{16,24},{24,16},{1,9},{9,1},{17,25},{25,17},{2,10},{10... | collective-permute-start | bytes 98312 | tf_op jit(solution)/shard_map/ppermute | solution.py:419
  56.8 8.0 %collective-permute-start.13 = (bf16[2,256,128]{2,1,0:T(8,128)(2,1)S(1)}, bf16[2,256,128]{2,1,0:T(8,128)(2,1)S(1)}, u32[]{:S(2)}, u32[]{:S(2)}) collective-permute-start(bf16[2,256,128]{2,1,0:T(8,128)(2,1)S(1)} %get-tuple-element.50), channel_id=1, source_target_pairs={{0,2},{1,3},{2,0},{3,1},{4,6},{5,7},{6,4},{7,5},{8,10},{9,11},{10,... | collective-permute-start | bytes 393224 | tf_op jit(solution)/shard_map/ppermute | solution.py:489
  58.5 19.1 %collective-permute-start.14 = (bf16[2,256,128]{2,1,0:T(8,128)(2,1)S(1)}, bf16[2,256,128]{2,1,0:T(8,128)(2,1)S(1)}, u32[]{:S(2)}, u32[]{:S(2)}) collective-permute-start(bf16[2,256,128]{2,1,0:T(8,128)(2,1)S(1)} %get-tuple-element.51), channel_id=1, source_target_pairs={{0,4},{1,5},{2,6},{3,7},{4,0},{5,1},{6,2},{7,3},{8,12},{9,13},{10,... | collective-permute-start | bytes 393224 | tf_op jit(solution)/shard_map/ppermute | solution.py:489
  60.9 16.7 %collective-permute-start.15 = (bf16[2,256,128]{2,1,0:T(8,128)(2,1)S(1)}, bf16[2,256,128]{2,1,0:T(8,128)(2,1)S(1)}, u32[]{:S(2)}, u32[]{:S(2)}) collective-permute-start(bf16[2,256,128]{2,1,0:T(8,128)(2,1)S(1)} %get-tuple-element.52), channel_id=1, source_target_pairs={{0,6},{1,7},{2,4},{3,5},{4,2},{5,3},{6,0},{7,1},{8,14},{9,15},{10,... | collective-permute-start | bytes 393224 | tf_op jit(solution)/shard_map/ppermute | solution.py:489
  63.2 15.1 %collective-permute-start.23 = (f32[2,32,128]{2,1,0:T(8,128)S(1)}, f32[2,32,128]{2,1,0:T(8,128)S(1)}, u32[]{:S(2)}, u32[]{:S(2)}) collective-permute-start(f32[2,32,128]{2,1,0:T(8,128)S(1)} %add_add_fusion.1), channel_id=1, source_target_pairs={{0,6},{1,7},{2,4},{3,5},{4,2},{5,3},{6,0},{7,1},{8,14},{9,15},{10,... | collective-permute-start | bytes 98312 | tf_op jit(solution)/shard_map/ppermute | solution.py:419
  64.8 16.4 %collective-permute-start.22 = (f32[2,32,128]{2,1,0:T(8,128)S(1)}, f32[2,32,128]{2,1,0:T(8,128)S(1)}, u32[]{:S(2)}, u32[]{:S(2)}) collective-permute-start(f32[2,32,128]{2,1,0:T(8,128)S(1)} %add_add_fusion.1), channel_id=1, source_target_pairs={{0,4},{1,5},{2,6},{3,7},{4,0},{5,1},{6,2},{7,3},{8,12},{9,13},{10,... | collective-permute-start | bytes 98312 | tf_op jit(solution)/shard_map/ppermute | solution.py:419
  77.6 4.0 %collective-permute-start.21 = (f32[2,32,128]{2,1,0:T(8,128)S(1)}, f32[2,32,128]{2,1,0:T(8,128)S(1)}, u32[]{:S(2)}, u32[]{:S(2)}) collective-permute-start(f32[2,32,128]{2,1,0:T(8,128)S(1)} %add_add_fusion.1), channel_id=1, source_target_pairs={{0,2},{1,3},{2,0},{3,1},{4,6},{5,7},{6,4},{7,5},{8,10},{9,11},{10,... | collective-permute-start | bytes 98312 | tf_op jit(solution)/shard_map/ppermute | solution.py:419
  78.3 3.9 %collective-permute-start.16 = (bf16[256,128]{1,0:T(8,128)(2,1)S(1)}, bf16[256,128]{1,0:T(8,128)(2,1)S(1)}, u32[]{:S(2)}, u32[]{:S(2)}) collective-permute-start(bf16[256,128]{1,0:T(8,128)(2,1)S(1)} %get-tuple-element.53), channel_id=1, source_target_pairs={{0,1},{1,0},{2,3},{3,2},{4,5},{5,4},{6,7},{7,6},{8,9},{9,8},{10,11... | collective-permute-start | bytes 196616 | tf_op jit(solution)/shard_map/ppermute | solution.py:508

commit v3 on v2

--- a/solution.py
+++ b/solution.py
@@ -18,7 +18,6 @@
 VMEM_MIB = 40
 ROW_TILE = 32
 JOIN = (False, True)
-SPLIT = (True, False)
 LOG2E = math.log2(math.e)
 
 
@@ -43,7 +42,9 @@
     return jnp.sum(jnp.where(down == along, upright, 0.0), axis=0, keepdims=True)
 
 
-def attention_kernel(index_ref, plan, near_in, far_in, *refs, carried, split, joined):
+def attention_kernel(
+    index_ref, plan, query_own, grad_own, query_far, grad_far, *refs, carried, split, joined
+):
     count, length = plan.shape
     chips = count // CORES
     blocks = chips if joined else count
@@ -83,17 +84,17 @@
     value_sum[...] = jnp.zeros_like(value_sum)
     bias[...] = jnp.zeros_like(bias)
 
-    def pick(which, g):
+    def pick(own, far, g):
         found = []
         for k in range(pack):
             at = pl.ds(pl.multiple_of((g + k) * HD, HD), HD)
-            found += [near_in[which, :, at], far_in[which, :, at]]
+            found += [own[:, at], far[:, at]]
         return jnp.concatenate(found, axis=0)
 
     def heads(j, _):
         g = j * pack
-        query = pick(0, g)
-        grad = pick(1, g)
+        query = pick(query_own, query_far, g)
+        grad = pick(grad_own, grad_far, g)
         score_ref[...] = nn(query, key_t[...])
         press_ref[...] = nn(grad, value_t[...])
         span = CORES * length
@@ -140,16 +141,16 @@
             parts[0][index ^ r, HD:, :] = from_values[:, cols]
 
 
-def attention(index, chunk, chunks, plan, near_in, far_in, pairs, carried, split):
+def attention(index, chunk, chunks, plan, rows_in, pairs, carried, split):
     count = plan.shape[0]
     chips = count // CORES
-    _, length, half = near_in.shape
+    length, width = rows_in[-1].shape
     wide = GROUP * HD
     whole = lambda *shape: pl.BlockSpec(shape, lambda i, c: (0,) * len(shape))
     mine = pl.BlockSpec((length, wide), lambda i, c: (0, chunks * (c[0] % CORES) + chunk))
     out_shape = [
-        jax.ShapeDtypeStruct((length, CORES * half), jnp.bfloat16),
-        jax.ShapeDtypeStruct((length, CORES * half), jnp.bfloat16),
+        jax.ShapeDtypeStruct((length, width), jnp.bfloat16),
+        jax.ShapeDtypeStruct((length, width), jnp.bfloat16),
         jax.ShapeDtypeStruct((chunks * BIAS_ROWS, HD), jnp.float32),
         jax.ShapeDtypeStruct((2, length, chunks * wide), jnp.bfloat16),
     ]
@@ -159,13 +160,14 @@
     rows = CORES * length
     cols = count * length
     far = pl.BlockSpec((2, length, wide), lambda i, c: (0, 0, chunk))
-    in_specs = [whole(*plan.shape), far, far]
+    near = pl.BlockSpec((length, wide), lambda i, c: (0, chunk))
+    in_specs = [whole(*plan.shape), near, near, mine, mine]
     in_specs += [whole(*pairs[0].shape)] * len(pairs)
-    operands = [plan, near_in, far_in, *pairs]
+    operands = [plan, *rows_in, *pairs]
     aliases = {}
     if carried is not None:
         in_specs += [pl.BlockSpec(memory_space=pl.ANY)] * 4
-        aliases = {4 + len(pairs) + k: k for k in range(4)}
+        aliases = {6 + len(pairs) + k: k for k in range(4)}
         operands += list(carried)
     pack = GROUP
     while pack > 1 and pack * rows * cols > 2 * 1024 * 1024:
@@ -190,8 +192,7 @@
         ]
         + [pltpu.VMEM((pack * rows, cols), jnp.float32)] * 2
         + [pltpu.VMEM((pack * rows, cols), jnp.bfloat16)] * 2
-        + [
-        ],
+        + [],
     )
     work = rows * GROUP * cols
     return pl.pallas_call(
@@ -255,50 +256,36 @@
     return pl.pallas_call(join_kernel, out_shape=shape, name="join")(near, away)
 
 
-def place_kernel(index_ref, far, attended_in, grad_in, attended, grad_query):
+def place_kernel(index_ref, far, piece, *refs):
+    attended, grad_query, grad_key, grad_value = refs[-4:]
     attended[...] = far[0]
     grad_query[...] = far[1]
-
-
-def place(index, far, attended, grad_query):
+    grad_key[...] = piece[:HD].astype(jnp.float32).T.astype(jnp.bfloat16)
+    grad_value[...] = piece[HD:].astype(jnp.float32).T.astype(jnp.bfloat16)
+
+
+def place(index, chunk, chunks, far, piece, filled):
     _, length, half = far.shape
     theirs = pl.BlockSpec((length, half), lambda i, c: (0, 1 - c[0] % CORES))
+    head = pl.BlockSpec((length, HD), lambda i, c: (0, (1 - c[0] % CORES) * chunks + chunk))
     grid_spec = pltpu.PrefetchScalarGridSpec(
         num_scalar_prefetch=1,
         grid=(1,),
-        in_specs=[pl.BlockSpec((2, length, half), lambda i, c: (0, 0, 0))]
-        + [pl.BlockSpec(memory_space=pl.ANY)] * 2,
-        out_specs=[theirs, theirs],
+        in_specs=[
+            pl.BlockSpec(far.shape, lambda i, c: (0, 0, 0)),
+            pl.BlockSpec(piece.shape, lambda i, c: (0, 0)),
+        ]
+        + [pl.BlockSpec(memory_space=pl.ANY)] * 4,
+        out_specs=[theirs, theirs, head, head],
     )
     return pl.pallas_call(
         place_kernel,
         grid_spec=grid_spec,
-        out_shape=[jax.ShapeDtypeStruct(attended.shape, attended.dtype)] * 2,
-        input_output_aliases={2: 0, 3: 1},
+        out_shape=[jax.ShapeDtypeStruct(x.shape, x.dtype) for x in filled],
+        input_output_aliases={3 + k: k for k in range(4)},
         compiler_params=pltpu.CompilerParams(vmem_limit_bytes=8 * 1024 * 1024),
         name="place",
-    )(index, far, attended, grad_query)
-
-
-def halves_kernel(index_ref, query, grad, near, away):
-    half = near.shape[2]
-    even = index_ref[0] % CORES == 0
-    for which, source in enumerate((query, grad)):
-        first, second = source[:, :half], source[:, half:]
-        near[which] = jnp.where(even, first, second)
-        away[which] = jnp.where(even, second, first)
-
-
-def halves(index, query, grad):
-    length, width = query.shape
-    shape = jax.ShapeDtypeStruct((2, length, width // CORES), query.dtype)
-    vmem = pl.BlockSpec(memory_space=pltpu.VMEM)
-    return pl.pallas_call(
-        halves_kernel,
-        in_specs=[pl.BlockSpec(memory_space=pltpu.SMEM), vmem, vmem],
-        out_shape=[shape, shape],
-        name="halves",
-    )(index, query, grad)
+    )(index, far, piece, *filled)
 
 
 def added(pieces):
@@ -306,13 +293,6 @@
     for piece in pieces[1:]:
         total = total + piece.astype(jnp.float32)
     return total
-
-
-def finish_kernel(index_ref, piece, *refs):
-    grad_key, grad_value = refs[-2:]
-    total = added([piece[z, 0] for z in range(piece.shape[0])])
-    grad_key[...] = total[:HD].T.astype(jnp.bfloat16)
-    grad_value[...] = total[HD:].T.astype(jnp.bfloat16)
 
 
 def settle_kernel(index_ref, *refs, count):
@@ -348,36 +328,18 @@
     )(index, *operands)
 
 
-def finish(index, chunk, chunks, piece, shape, carried):
-    count, rows, length = piece.shape
-    piece = piece.reshape(count // CORES, CORES, rows, length)
-    spec = pl.BlockSpec((count // CORES, 1, rows, length), lambda i, c: (0, i, 0, 0))
-    heads = lambda i, c: (0, i * chunks + chunk)
-    return into_grads(
-        finish_kernel, index, CORES, [spec], [piece], heads, shape, None, carried
-    )
-
-
 def settle(index, chunk, chunks, pieces, shape, carried):
     spec = pl.BlockSpec(pieces[0].shape, lambda i, c: (0, 0, 0))
     heads = lambda i, c: (0, (c[0] % CORES) * chunks + chunk)
     kernel = functools.partial(settle_kernel, count=len(pieces))
     extra = pieces[0].shape[1:]
-    return into_grads(
-        kernel, index, 1, [spec] * len(pieces), pieces, heads, shape, extra, carried
-    )
-
-
-def receive(index, chunk, chunks, piece, shape, carried):
-    piece = piece[None, None]
-    spec = pl.BlockSpec(piece.shape, lambda i, c: (0, 0, 0, 0))
-    heads = lambda i, c: (0, (1 - c[0] % CORES) * chunks + chunk)
-    return into_grads(
-        finish_kernel, index, 1, [spec], [piece], heads, shape, None, carried
-    )
-
-
-def bias_kernel(index_ref, sums, bias_grad, *, chunks, factor):
+    return into_grads(kernel, index, 1, [spec] * len(pieces), pieces, heads, shape, extra, carried)
+
+
+def last_kernel(index_ref, sums, piece, *refs, chunks, factor):
+    grad_key, grad_value, bias_grad = refs[-3:]
+    grad_key[...] = piece[:HD].astype(jnp.float32).T.astype(jnp.bfloat16)
+    grad_value[...] = piece[HD:].astype(jnp.float32).T.astype(jnp.bfloat16)
     core = index_ref[0] % CORES
     for c in range(CORES):
         ours = core == c
@@ -394,17 +356,29 @@
             )
 
 
-def bias_total(index, sums, chunks, factor):
+def last(index, sums, chunk, chunks, piece, grads, factor):
+    length = grads[0].shape[0]
+    head = pl.BlockSpec((length, HD), lambda i, c: (0, (1 - c[0] % CORES) * chunks + chunk))
+    bias_shape = (CORES * chunks * (GROUP + 1), HD)
+    grid_spec = pltpu.PrefetchScalarGridSpec(
+        num_scalar_prefetch=1,
+        grid=(1,),
+        in_specs=[
+            pl.BlockSpec(sums.shape, lambda i, c: (0, 0, 0)),
+            pl.BlockSpec(piece.shape, lambda i, c: (0, 0)),
+        ]
+        + [pl.BlockSpec(memory_space=pl.ANY)] * 2,
+        out_specs=[head, head, pl.BlockSpec(bias_shape, lambda i, c: (0, 0))],
+    )
     return pl.pallas_call(
-        functools.partial(bias_kernel, chunks=chunks, factor=factor),
-        in_specs=[
-            pl.BlockSpec(memory_space=pltpu.SMEM),
-            pl.BlockSpec(memory_space=pltpu.VMEM),
-        ],
-        out_shape=jax.ShapeDtypeStruct((CORES * chunks * (GROUP + 1), HD), jnp.float32),
-        compiler_params=pltpu.CompilerParams(vmem_limit_bytes=4 * 1024 * 1024),
-        name="bias",
-    )(index, sums)
+        functools.partial(last_kernel, chunks=chunks, factor=factor),
+        grid_spec=grid_spec,
+        out_shape=[jax.ShapeDtypeStruct(x.shape, x.dtype) for x in grads]
+        + [jax.ShapeDtypeStruct(bias_shape, jnp.float32)],
+        input_output_aliases={3: 0, 4: 1},
+        compiler_params=pltpu.CompilerParams(vmem_limit_bytes=8 * 1024 * 1024),
+        name="last",
+    )(index, sums, piece, *grads)
 
 
 def summed(part, axis, steps):
@@ -449,6 +423,12 @@
     def xor(r):
         return [(i, i ^ r) for i in range(devices)]
 
+    query_far = lax.ppermute(query_rows, "ctx", across)
+    grad_far = lax.ppermute(out_grad, "ctx", across)
+    half = query_rows.shape[1] // CORES
+    begin = (index % CORES) * half
+    near = [lax.dynamic_slice_in_dim(rows, begin, half, axis=1) for rows in (query_rows, out_grad)]
+    rows_in = (*near, query_far, grad_far)
     blocks = payload(index_arg, group_first, key_rows, value_rows, chunks)
     gathered = []
     for hh in range(chunks):
@@ -464,51 +444,39 @@
             for r in range(devices - 1, 0, -1):
                 pairs[r] = lax.ppermute(mine[r % CORES], "ctx", xor(r))
         gathered.append(pairs)
-    near_in, far_in = halves(index_arg, query_rows, out_grad)
-    far_in = lax.ppermute(far_in, "ctx", across)
-
     carried = None
     returned = []
     for hh in range(chunks):
-        split = SPLIT[hh % len(SPLIT)]
         outs = attention(
             index_arg,
             hh,
             chunks,
             plan,
-            near_in,
-            far_in,
+            rows_in,
             gathered[hh],
             carried,
-            split,
+            True,
         )
         carried, parts = outs[:4], outs[4:]
-        if split:
-            pieces = list(parts)
-            for k in order:
-                pieces[k] = lax.ppermute(parts[k], "ctx", over(k))
-            returned.append(pieces)
-        else:
-            returned.append(
-                lax.all_to_all(parts[0], "ctx", split_axis=0, concat_axis=0, tiled=True)
-            )
+        pieces = list(parts)
+        for k in order:
+            pieces[k] = lax.ppermute(parts[k], "ctx", over(k))
+        returned.append(pieces)
     attended, grad_query, bias, far_out = carried
     far_out = lax.ppermute(far_out, "ctx", across)
-    attended, grad_query = place(index_arg, far_out, attended, grad_query)
     both = jnp.stack([bias, lax.ppermute(bias, "ctx", across)])
     both = summed(both, "dp", powers(1, replicas))
     both = summed(both, "ctx", powers(CORES, devices))
     factor = 1.0 / math.sqrt(length * devices * replicas)
-    bias_grad = bias_total(index_arg, both, chunks, factor)
     grads = None
-    shape = key_rows.shape
     for hh in range(chunks):
-        if SPLIT[hh % len(SPLIT)]:
-            *grads, away = settle(index_arg, hh, chunks, returned[hh], shape, grads)
-            away = lax.ppermute(away, "ctx", across)
-            grads = receive(index_arg, hh, chunks, away, shape, grads)
-        else:
-            grads = finish(index_arg, hh, chunks, returned[hh], shape, grads)
+        *grads, away = settle(index_arg, hh, chunks, returned[hh], key_rows.shape, grads)
+        away = lax.ppermute(away, "ctx", across)
+        if hh < chunks - 1:
+            attended, grad_query, *grads = place(
+                index_arg, hh, chunks, far_out, away, (attended, grad_query, *grads)
+            )
+    *grads, bias_grad = last(index_arg, both, chunks - 1, chunks, away, grads, factor)
     return (attended, grad_query, *grads, bias_grad.reshape(-1))
 
 

time: 85.2 us -> 84.2 us (0.988)
  starting transfers between devices: 34.9 us -> 38.4 us
  Pallas kernels: 27.9 us -> 24.9 us
  waiting for transfers between devices: 19.4 us -> 17.2 us
    ppermute x7, starting transfers between devices: 8.29 us -> 14.3 us  [body(): pairs[r] = lax.ppermute(mine[r % CORES], 'ctx', xor(r))]
    all_to_all x1 -> x0, starting transfers between devices: 4.17 us -> none  [body(): lax.all_to_all(parts[0], 'ctx', split_axis=0, concat_axis=0, tiled=True)]
    pallas_call x2 -> x1, Pallas kernels: 3.62 us -> 0.74 us  [last(): pl.pallas_call(functools.partial(last_kernel, chunks=chunks, factor=facto...]
    ppermute x3 -> x6, starting transfers between devices: 6.45 us -> 9.06 us  [body(): pieces[k] = lax.ppermute(parts[k], 'ctx', over(k))]
    ppermute x3 -> x6, waiting for transfers between devices: 8.28 us -> 10.7 us  [body(): pieces[k] = lax.ppermute(parts[k], 'ctx', over(k))]
    ppermute x3, waiting for transfers between devices: 2.01 us -> 0.01 us  [body(): pairs[k] = lax.ppermute(both, 'ctx', over(k))]
    dynamic_slice x0 -> x1, local copies, waits for them, and re-layouts: none -> 1.3 us  [body(): lax.dynamic_slice_in_dim(rows, begin, half, axis=1)]
    ppermute x3, starting transfers between devices: 5.4 us -> 4.39 us  [body(): pairs[k] = lax.ppermute(both, 'ctx', over(k))]
  transfers between devices with their start and end apart: 25 -> 29, of which waited for: 6 -> 8; matrix products, arithmetic and copies ran while one was open for 0% -> 2% of each run, Pallas kernels for 18% -> 18%
where the time goes in v3:
time: 84.2 us; the launch traced here: 83.9 us
  starting transfers between devices  38.4 us (46%)
  Pallas kernels  24.9 us (30%)
  waiting for transfers between devices  17.2 us (20%)
  local copies, waits for them, and re-layouts  1.94 us (2%)
  between operations  1.39 us (2%)
    pallas_call x2, Pallas kernels, attention(): pl.pallas_call(functools.partial(attention_kernel, carried=carried is not...  18.4 us
    ppermute x7, starting transfers between devices, body(): pairs[r] = lax.ppermute(mine[r % CORES], 'ctx', xor(r))  14.3 us
    ppermute x6, waiting for transfers between devices, body(): pieces[k] = lax.ppermute(parts[k], 'ctx', over(k))  10.7 us
    ppermute x6, starting transfers between devices, summed(): moved = lax.ppermute(part, axis, [(i, i ^ mixed) for i in range(size)])  9.79 us
    ppermute x6, starting transfers between devices, body(): pieces[k] = lax.ppermute(parts[k], 'ctx', over(k))  9.06 us
    ppermute x3, starting transfers between devices, body(): pairs[k] = lax.ppermute(both, 'ctx', over(k))  4.39 us
    ppermute x7, waiting for transfers between devices, body(): pairs[r] = lax.ppermute(mine[r % CORES], 'ctx', xor(r))  3.91 us
    ppermute x6, waiting for transfers between devices, summed(): moved = lax.ppermute(part, axis, [(i, i ^ mixed) for i in range(size)])  2.53 us
  transfers between devices with their start and end apart: 29, of which 8 were waited for; matrix products, arithmetic and copies ran while one was open for 2% of the time, Pallas kernels for 18%

profile of v3, /device:TPU:0, one launch (start us, length us, event | category | flops | bytes accessed | tf_op | source)
XLA Modules:
  0.0 83.9 jit_solution(5459415247572767737)
XLA Ops:
  0.6 0.6 collective-permute-start
  1.2 0.1 collective-permute-start.1
  1.9 1.7 %payload.1 = (bf16[264,128]{1,0:T(8,128)(2,1)}, bf16[264,128]{1,0:T(8,128)(2,1)}, bf16[264,128]{1,0:T(8,128)(2,1)}, bf16[264,128]{1,0:T(8,128)(2,1)}) custom-call(s32[1]{0:T(128)} %bitcast.index_ref, s32[1,1]{1,0:T(1,128)S(6)} %copy.35.first_ref, bf16[128,512]{1,0:T(8,128)(2,1)} %keys.1, bf16[128,512]{1,0:T(8,128)(2,1)} %values.1), custom_call_target="tpu_custom_call" | custom-call | tf_op jit(solution)/shard_map/payload/pallas_call | solution.py:241
  3.6 3.7 %collective-permute-start.10 = (bf16[264,128]{1,0:T(8,128)(2,1)}, bf16[264,128]{1,0:T(8,128)(2,1)S(1)}, u32[]{:S(2)}, u32[]{:S(2)}) collective-permute-start(bf16[264,128]{1,0:T(8,128)(2,1)} %get-tuple-element.41), channel_id=1, source_target_pairs={{0,5},{1,4},{2,7},{3,6},{4,1},{5,0},{6,3},{7,2},{8,13},{9,12},{10,... | collective-permute-start | bytes 202760 | tf_op jit(solution)/shard_map/ppermute | solution.py:445
  7.3 1.3 %collective-permute-start.11 = (bf16[264,128]{1,0:T(8,128)(2,1)}, bf16[264,128]{1,0:T(8,128)(2,1)S(1)}, u32[]{:S(2)}, u32[]{:S(2)}) collective-permute-start(bf16[264,128]{1,0:T(8,128)(2,1)} %get-tuple-element.40.refs_0_), channel_id=1, source_target_pairs={{0,6},{1,7},{2,4},{3,5},{4,2},{5,3},{6,0},{7,1},{8,14},{9,15},{10,... | collective-permute-start | bytes 202760 | tf_op jit(solution)/shard_map/ppermute | solution.py:445
  8.7 2.2 %collective-permute-start.12 = (bf16[264,128]{1,0:T(8,128)(2,1)}, bf16[264,128]{1,0:T(8,128)(2,1)S(1)}, u32[]{:S(2)}, u32[]{:S(2)}) collective-permute-start(bf16[264,128]{1,0:T(8,128)(2,1)} %get-tuple-element.41), channel_id=1, source_target_pairs={{0,7},{1,6},{2,5},{3,4},{4,3},{5,2},{6,1},{7,0},{8,15},{9,14},{10,... | collective-permute-start | bytes 202760 | tf_op jit(solution)/shard_map/ppermute | solution.py:445
  10.9 0.0 collective-permute-done.10.refs_5_
  10.9 0.4 collective-permute-start.6
  11.3 2.8 %collective-permute-done.11.refs_6_ = bf16[264,128]{1,0:T(8,128)(2,1)S(1)} collective-permute-done((bf16[264,128]{1,0:T(8,128)(2,1)}, bf16[264,128]{1,0:T(8,128)(2,1)S(1)}, u32[]{:S(2)}, u32[]{:S(2)}) %collective-permute-start.11) | collective-permute-done | bytes 67616 | tf_op jit(solution)/shard_map/ppermute | solution.py:445
  14.1 0.0 collective-permute-start.2
  14.1 1.1 %collective-permute-done.12.refs_7_ = bf16[264,128]{1,0:T(8,128)(2,1)S(1)} collective-permute-done((bf16[264,128]{1,0:T(8,128)(2,1)}, bf16[264,128]{1,0:T(8,128)(2,1)S(1)}, u32[]{:S(2)}, u32[]{:S(2)}) %collective-permute-start.12) | collective-permute-done | bytes 67616 | tf_op jit(solution)/shard_map/ppermute | solution.py:445
  15.2 3.4 %collective-permute-start.7 = (bf16[264,128]{1,0:T(8,128)(2,1)}, bf16[264,128]{1,0:T(8,128)(2,1)}, u32[]{:S(2)}, u32[]{:S(2)}) collective-permute-start(bf16[264,128]{1,0:T(8,128)(2,1)} %get-tuple-element.40.refs_0_), channel_id=1, source_target_pairs={{0,2},{1,3},{2,0},{3,1},{4,6},{5,7},{6,4},{7,5},{8,10},{9,11},{10,... | collective-permute-start | bytes 202760 | tf_op jit(solution)/shard_map/ppermute | solution.py:445
  18.6 0.0 collective-permute-done.6.refs_1_
  18.6 0.0 collective-permute-start.8
  18.6 0.0 collective-permute-done.2.away
  18.6 0.0 copy-start.3
  18.6 0.6 copy-done.3
  19.3 3.2 %collective-permute-start.9 = (bf16[264,128]{1,0:T(8,128)(2,1)}, bf16[264,128]{1,0:T(8,128)(2,1)}, u32[]{:S(2)}, u32[]{:S(2)}) collective-permute-start(bf16[264,128]{1,0:T(8,128)(2,1)} %get-tuple-element.40.refs_0_), channel_id=1, source_target_pairs={{0,4},{1,5},{2,6},{3,7},{4,0},{5,1},{6,2},{7,3},{8,12},{9,13},{10,... | collective-permute-start | bytes 202760 | tf_op jit(solution)/shard_map/ppermute | solution.py:445
  22.5 1.3 %constant_dynamic-slice_fusion = (bf16[128,2048]{1,0:T(8,128)(2,1)S(1)}, bf16[128,2048]{1,0:T(8,128)(2,1)S(1)}) fusion(bf16[128,4096]{1,0:T(8,128)(2,1)} %param.9, s32[]{:T(128)S(6)} %select_n.12, bf16[128,4096]{1,0:T(8,128)(2,1)} %param.6), kind=kLoop, calls=%fused_computation.3 | loop fusion | bytes 2097156 | tf_op jit(solution)/shard_map/dynamic_slice | solution.py:430
  23.8 0.0 copy-start.1
  23.8 1.6 %join.1.refs_0_ = bf16[2,264,128]{2,1,0:T(8,128)(2,1)} custom-call(bf16[264,128]{1,0:T(8,128)(2,1)} %get-tuple-element.38.near, bf16[264,128]{1,0:T(8,128)(2,1)} %copy-done.3), custom_call_target="tpu_custom_call" | custom-call | tf_op jit(solution)/shard_map/join/pallas_call | solution.py:256
  25.4 0.0 collective-permute-done.7.refs_2_
  25.4 0.6 collective-permute-start.3
  26.0 0.0 collective-permute-done.8.refs_3_
  26.0 0.5 collective-permute-start.4
  26.6 0.0 collective-permute-done.9.refs_4_
  26.6 3.3 %collective-permute-start.5 = (bf16[2,264,128]{2,1,0:T(8,128)(2,1)}, bf16[2,264,128]{2,1,0:T(8,128)(2,1)S(1)}, u32[]{:S(2)}, u32[]{:S(2)}) collective-permute-start(bf16[2,264,128]{2,1,0:T(8,128)(2,1)} %join.1.refs_0_), channel_id=1, source_target_pairs={{0,6},{1,7},{2,4},{3,5},{4,2},{5,3},{6,0},{7,1},{8,14},{9,15},{10,... | collective-permute-start | bytes 405512 | tf_op jit(solution)/shard_map/ppermute | solution.py:441
  29.8 0.0 collective-permute-done.query_far
  29.8 0.0 collective-permute-done.1.grad_far
  29.9 9.6 %attention.2 = (bf16[128,4096]{1,0:T(8,128)(2,1)}, bf16[128,4096]{1,0:T(8,128)(2,1)}, f32[32,128]{1,0:T(8,128)S(1)}, bf16[2,128,2048]{2,1,0:T(8,128)(2,1)S(1)}, ...) custom-call(s32[1]{0:T(128)} %bitcast.index_ref, ...), custom_call_target="tpu_custom_call" | custom-call | flops 3221225472 | bytes 2097152 | tf_op jit(solution)/shard_map/attention/pallas_call | solution.py:198
  39.5 0.0 collective-permute-done.3.refs_1_
  39.5 8.8 %attention.3 = (bf16[128,4096]{1,0:T(8,128)(2,1)}, bf16[128,4096]{1,0:T(8,128)(2,1)}, f32[32,128]{1,0:T(8,128)S(1)}, bf16[2,128,2048]{2,1,0:T(8,128)(2,1)S(1)}, ...) custom-call(s32[1]{0:T(128)} %bitcast.index_ref, ...), custom_call_target="tpu_custom_call", output_to_operand_aliasing={{0}: (10, {}), {1}: (11, {}), {2}: (12, {}), {3}: (13, {})} | custom-call | flops 3221225472 | bytes 2097152 | tf_op jit(solution)/shard_map/attention/pallas_call | solution.py:198
  48.3 0.0 collective-permute-start.13
  48.3 2.3 %collective-permute-start.14 = (bf16[2,256,128]{2,1,0:T(8,128)(2,1)S(1)}, bf16[2,256,128]{2,1,0:T(8,128)(2,1)S(1)}, u32[]{:S(2)}, u32[]{:S(2)}) collective-permute-start(bf16[2,256,128]{2,1,0:T(8,128)(2,1)S(1)} %get-tuple-element.48), channel_id=1, source_target_pairs={{0,2},{1,3},{2,0},{3,1},{4,6},{5,7},{6,4},{7,5},{8,10},{9,11},{10,... | collective-permute-start | bytes 393224 | tf_op jit(solution)/shard_map/ppermute | solution.py:463
  50.6 0.7 collective-permute-start.15
  51.3 0.2 collective-permute-start.18
  51.5 1.6 %collective-permute-start.16 = (bf16[2,256,128]{2,1,0:T(8,128)(2,1)S(1)}, bf16[2,256,128]{2,1,0:T(8,128)(2,1)S(1)}, u32[]{:S(2)}, u32[]{:S(2)}) collective-permute-start(bf16[2,256,128]{2,1,0:T(8,128)(2,1)S(1)} %get-tuple-element.50), channel_id=1, source_target_pairs={{0,6},{1,7},{2,4},{3,5},{4,2},{5,3},{6,0},{7,1},{8,14},{9,15},{10,... | collective-permute-start | bytes 393224 | tf_op jit(solution)/shard_map/ppermute | solution.py:463
  53.2 0.0 collective-permute-done.18
  53.2 1.5 %collective-permute-start.19 = (f32[2,32,128]{2,1,0:T(8,128)S(1)}, f32[2,32,128]{2,1,0:T(8,128)S(1)}, u32[]{:S(2)}, u32[]{:S(2)}) collective-permute-start(f32[2,32,128]{2,1,0:T(8,128)S(1)} %pad_maximum_fusion), channel_id=1, source_target_pairs={{0,8},{8,0},{16,24},{24,16},{1,9},{9,1},{17,25},{25,17},{2,10},{10... | collective-permute-start | bytes 98312 | tf_op jit(solution)/shard_map/ppermute | solution.py:393
  54.7 2.2 %collective-permute-done.14.refs_1_ = bf16[2,256,128]{2,1,0:T(8,128)(2,1)S(1)} collective-permute-done((bf16[2,256,128]{2,1,0:T(8,128)(2,1)S(1)}, bf16[2,256,128]{2,1,0:T(8,128)(2,1)S(1)}, u32[]{:S(2)}, u32[]{:S(2)}) %collective-permute-start.14) | collective-permute-done | bytes 131104 | tf_op jit(solution)/shard_map/ppermute | solution.py:463
  56.9 1.5 %collective-permute-start.20 = (f32[2,32,128]{2,1,0:T(8,128)S(1)}, f32[2,32,128]{2,1,0:T(8,128)S(1)}, u32[]{:S(2)}, u32[]{:S(2)}) collective-permute-start(f32[2,32,128]{2,1,0:T(8,128)S(1)} %pad_maximum_fusion), channel_id=1, source_target_pairs={{0,16},{8,24},{16,0},{24,8},{1,17},{9,25},{17,1},{25,9},{2,18},{10... | collective-permute-start | bytes 98312 | tf_op jit(solution)/shard_map/ppermute | solution.py:393
  58.4 5.1 %collective-permute-done.15.refs_2_ = bf16[2,256,128]{2,1,0:T(8,128)(2,1)S(1)} collective-permute-done((bf16[2,256,128]{2,1,0:T(8,128)(2,1)S(1)}, bf16[2,256,128]{2,1,0:T(8,128)(2,1)S(1)}, u32[]{:S(2)}, u32[]{:S(2)}) %collective-permute-start.15) | collective-permute-done | bytes 131104 | tf_op jit(solution)/shard_map/ppermute | solution.py:463
  63.5 2.5 %collective-permute-start.21 = (f32[2,32,128]{2,1,0:T(8,128)S(1)}, f32[2,32,128]{2,1,0:T(8,128)S(1)}, u32[]{:S(2)}, u32[]{:S(2)}) collective-permute-start(f32[2,32,128]{2,1,0:T(8,128)S(1)} %pad_maximum_fusion), channel_id=1, source_target_pairs={{0,24},{8,16},{16,8},{24,0},{1,25},{9,17},{17,9},{25,1},{2,26},{10... | collective-permute-start | bytes 98312 | tf_op jit(solution)/shard_map/ppermute | solution.py:393
  66.0 0.0 collective-permute-done.16.refs_3_
  66.0 0.2 collective-permute-start.25
  66.1 0.7 shard_map.101
  66.9 0.0 collective-permute-done.19
  66.9 2.6 %collective-permute-start.26 = (bf16[2,256,128]{2,1,0:T(8,128)(2,1)S(1)}, bf16[2,256,128]{2,1,0:T(8,128)(2,1)S(1)}, u32[]{:S(2)}, u32[]{:S(2)}) collective-permute-start(bf16[2,256,128]{2,1,0:T(8,128)(2,1)S(1)} %get-tuple-element.61), channel_id=1, source_target_pairs={{0,4},{1,5},{2,6},{3,7},{4,0},{5,1},{6,2},{7,3},{8,12},{9,13},{10,... | collective-permute-start | bytes 393224 | tf_op jit(solution)/shard_map/ppermute | solution.py:463
  69.5 1.6 %collective-permute-start.27 = (bf16[2,256,128]{2,1,0:T(8,128)(2,1)S(1)}, bf16[2,256,128]{2,1,0:T(8,128)(2,1)S(1)}, u32[]{:S(2)}, u32[]{:S(2)}) collective-permute-start(bf16[2,256,128]{2,1,0:T(8,128)(2,1)S(1)} %get-tuple-element.62), channel_id=1, source_target_pairs={{0,6},{1,7},{2,4},{3,5},{4,2},{5,3},{6,0},{7,1},{8,14},{9,15},{10,... | collective-permute-start | bytes 393224 | tf_op jit(solution)/shard_map/ppermute | solution.py:463
  71.1 0.0 collective-permute-done.21
  71.1 0.0 collective-permute-start.17
  71.1 1.2 %collective-permute-done.25.refs_1_ = bf16[2,256,128]{2,1,0:T(8,128)(2,1)S(1)} collective-permute-done((bf16[2,256,128]{2,1,0:T(8,128)(2,1)S(1)}, bf16[2,256,128]{2,1,0:T(8,128)(2,1)S(1)}, u32[]{:S(2)}, u32[]{:S(2)}) %collective-permute-start.25) | collective-permute-done | bytes 131104 | tf_op jit(solution)/shard_map/ppermute | solution.py:463
  72.3 0.0 collective-permute-start.22
  72.3 0.1 collective-permute-done.17.piece
  72.4 2.6 %collective-permute-start.23 = (f32[2,32,128]{2,1,0:T(8,128)S(1)}, f32[2,32,128]{2,1,0:T(8,128)S(1)}, u32[]{:S(2)}, u32[]{:S(2)}) collective-permute-start(f32[2,32,128]{2,1,0:T(8,128)S(1)} %add_add_fusion.1), channel_id=1, source_target_pairs={{0,4},{1,5},{2,6},{3,7},{4,0},{5,1},{6,2},{7,3},{8,12},{9,13},{10,... | collective-permute-start | bytes 98312 | tf_op jit(solution)/shard_map/ppermute | solution.py:393
  75.0 1.7 %collective-permute-start.24 = (f32[2,32,128]{2,1,0:T(8,128)S(1)}, f32[2,32,128]{2,1,0:T(8,128)S(1)}, u32[]{:S(2)}, u32[]{:S(2)}) collective-permute-start(f32[2,32,128]{2,1,0:T(8,128)S(1)} %add_add_fusion.1), channel_id=1, source_target_pairs={{0,6},{1,7},{2,4},{3,5},{4,2},{5,3},{6,0},{7,1},{8,14},{9,15},{10,... | collective-permute-start | bytes 98312 | tf_op jit(solution)/shard_map/ppermute | solution.py:393
  76.7 1.0 %place.1 = (bf16[128,4096]{1,0:T(8,128)(2,1)}, bf16[128,4096]{1,0:T(8,128)(2,1)}, bf16[128,512]{1,0:T(8,128)(2,1)}, bf16[128,512]{1,0:T(8,128)(2,1)}) custom-call(s32[1]{0:T(128)} %bitcast.index_ref, bf16[2,128,2048]{2,1,0:T(8,128)(2,1)S(1)} %collective-permute-done.13.far, ...), custom_call_target="tpu_custom_call", output_to_operand_aliasing={{0}: (3, {}), {1}: (4, {}), {2}: (5, {}), {3}: (6, {})} | custom-call | tf_op jit(solution)/shard_map/place/pallas_call | solution.py:281
  77.7 2.2 %collective-permute-done.26.refs_2_ = bf16[2,256,128]{2,1,0:T(8,128)(2,1)S(1)} collective-permute-done((bf16[2,256,128]{2,1,0:T(8,128)(2,1)S(1)}, bf16[2,256,128]{2,1,0:T(8,128)(2,1)S(1)}, u32[]{:S(2)}, u32[]{:S(2)}) %collective-permute-start.26) | collective-permute-done | bytes 131104 | tf_op jit(solution)/shard_map/ppermute | solution.py:463
  79.9 0.0 collective-permute-done.27.refs_3_
  79.9 0.7 shard_map.102
  80.6 0.0 collective-permute-start.28
  80.6 0.0 collective-permute-done.22
  80.6 2.5 %collective-permute-done.23 = f32[2,32,128]{2,1,0:T(8,128)S(1)} collective-permute-done((f32[2,32,128]{2,1,0:T(8,128)S(1)}, f32[2,32,128]{2,1,0:T(8,128)S(1)}, u32[]{:S(2)}, u32[]{:S(2)}) %collective-permute-start.23) | collective-permute-done | bytes 32800 | tf_op jit(solution)/shard_map/ppermute | solution.py:393
  83.2 0.7 last.1
  (14 shorter events, 0.1 us)
Async XLA Ops:
  0.6 29.2 %collective-permute-start = (bf16[128,4096]{1,0:T(8,128)(2,1)}, bf16[128,4096]{1,0:T(8,128)(2,1)S(1)}, u32[]{:S(2)}, u32[]{:S(2)}) collective-permute-start(bf16[128,4096]{1,0:T(8,128)(2,1)} %param.6), channel_id=1, source_target_pairs={{0,1},{1,0},{2,3},{3,2},{4,5},{5,4},{6,7},{7,6},{8,9},{9,8},{10,11... | collective-permute-start | bytes 3145736 | tf_op jit(solution)/shard_map/ppermute | solution.py:426
  1.2 28.7 %collective-permute-start.1 = (bf16[128,4096]{1,0:T(8,128)(2,1)}, bf16[128,4096]{1,0:T(8,128)(2,1)S(1)}, u32[]{:S(2)}, u32[]{:S(2)}) collective-permute-start(bf16[128,4096]{1,0:T(8,128)(2,1)} %param.9), channel_id=1, source_target_pairs={{0,1},{1,0},{2,3},{3,2},{4,5},{5,4},{6,7},{7,6},{8,9},{9,8},{10,11... | collective-permute-start | bytes 3145736 | tf_op jit(solution)/shard_map/ppermute | solution.py:427
  3.6 7.3 %collective-permute-start.10 = (bf16[264,128]{1,0:T(8,128)(2,1)}, bf16[264,128]{1,0:T(8,128)(2,1)S(1)}, u32[]{:S(2)}, u32[]{:S(2)}) collective-permute-start(bf16[264,128]{1,0:T(8,128)(2,1)} %get-tuple-element.41), channel_id=1, source_target_pairs={{0,5},{1,4},{2,7},{3,6},{4,1},{5,0},{6,3},{7,2},{8,13},{9,12},{10,... | collective-permute-start | bytes 202760 | tf_op jit(solution)/shard_map/ppermute | solution.py:445
  7.3 6.8 %collective-permute-start.11 = (bf16[264,128]{1,0:T(8,128)(2,1)}, bf16[264,128]{1,0:T(8,128)(2,1)S(1)}, u32[]{:S(2)}, u32[]{:S(2)}) collective-permute-start(bf16[264,128]{1,0:T(8,128)(2,1)} %get-tuple-element.40.refs_0_), channel_id=1, source_target_pairs={{0,6},{1,7},{2,4},{3,5},{4,2},{5,3},{6,0},{7,1},{8,14},{9,15},{10,... | collective-permute-start | bytes 202760 | tf_op jit(solution)/shard_map/ppermute | solution.py:445
  8.7 6.5 %collective-permute-start.12 = (bf16[264,128]{1,0:T(8,128)(2,1)}, bf16[264,128]{1,0:T(8,128)(2,1)S(1)}, u32[]{:S(2)}, u32[]{:S(2)}) collective-permute-start(bf16[264,128]{1,0:T(8,128)(2,1)} %get-tuple-element.41), channel_id=1, source_target_pairs={{0,7},{1,6},{2,5},{3,4},{4,3},{5,2},{6,1},{7,0},{8,15},{9,14},{10,... | collective-permute-start | bytes 202760 | tf_op jit(solution)/shard_map/ppermute | solution.py:445
  10.9 7.7 %collective-permute-start.6 = (bf16[264,128]{1,0:T(8,128)(2,1)}, bf16[264,128]{1,0:T(8,128)(2,1)S(1)}, u32[]{:S(2)}, u32[]{:S(2)}) collective-permute-start(bf16[264,128]{1,0:T(8,128)(2,1)} %get-tuple-element.41), channel_id=1, source_target_pairs={{0,1},{1,0},{2,3},{3,2},{4,5},{5,4},{6,7},{7,6},{8,9},{9,8},{10,11... | collective-permute-start | bytes 202760 | tf_op jit(solution)/shard_map/ppermute | solution.py:445
  14.1 4.5 %collective-permute-start.2 = (bf16[264,128]{1,0:T(8,128)(2,1)}, bf16[264,128]{1,0:T(8,128)(2,1)S(1)}, u32[]{:S(2)}, u32[]{:S(2)}) collective-permute-start(bf16[264,128]{1,0:T(8,128)(2,1)} %get-tuple-element.39), channel_id=1, source_target_pairs={{0,1},{1,0},{2,3},{3,2},{4,5},{5,4},{6,7},{7,6},{8,9},{9,8},{10,11... | collective-permute-start | bytes 202760 | tf_op jit(solution)/shard_map/ppermute | solution.py:437
  15.2 10.3 %collective-permute-start.7 = (bf16[264,128]{1,0:T(8,128)(2,1)}, bf16[264,128]{1,0:T(8,128)(2,1)}, u32[]{:S(2)}, u32[]{:S(2)}) collective-permute-start(bf16[264,128]{1,0:T(8,128)(2,1)} %get-tuple-element.40.refs_0_), channel_id=1, source_target_pairs={{0,2},{1,3},{2,0},{3,1},{4,6},{5,7},{6,4},{7,5},{8,10},{9,11},{10,... | collective-permute-start | bytes 202760 | tf_op jit(solution)/shard_map/ppermute | solution.py:445
  18.6 7.4 %collective-permute-start.8 = (bf16[264,128]{1,0:T(8,128)(2,1)}, bf16[264,128]{1,0:T(8,128)(2,1)}, u32[]{:S(2)}, u32[]{:S(2)}) collective-permute-start(bf16[264,128]{1,0:T(8,128)(2,1)} %get-tuple-element.41), channel_id=1, source_target_pairs={{0,3},{1,2},{2,1},{3,0},{4,7},{5,6},{6,5},{7,4},{8,11},{9,10},{10,... | collective-permute-start | bytes 202760 | tf_op jit(solution)/shard_map/ppermute | solution.py:445
  18.6 0.6 copy-start.3
  19.3 7.3 %collective-permute-start.9 = (bf16[264,128]{1,0:T(8,128)(2,1)}, bf16[264,128]{1,0:T(8,128)(2,1)}, u32[]{:S(2)}, u32[]{:S(2)}) collective-permute-start(bf16[264,128]{1,0:T(8,128)(2,1)} %get-tuple-element.40.refs_0_), channel_id=1, source_target_pairs={{0,4},{1,5},{2,6},{3,7},{4,0},{5,1},{6,2},{7,3},{8,12},{9,13},{10,... | collective-permute-start | bytes 202760 | tf_op jit(solution)/shard_map/ppermute | solution.py:445
  23.8 6.0 %copy-start.1 = (bf16[264,128]{1,0:T(8,128)(2,1)S(1)}, bf16[264,128]{1,0:T(8,128)(2,1)}, u32[]{:S(2)}) copy-start(bf16[264,128]{1,0:T(8,128)(2,1)} %get-tuple-element.40.refs_0_) | copy-start | bytes 202756
  25.4 4.4 %copy-start.2 = (s32[1,1024]{1,0:T(1,128)S(1)}, s32[1,1024]{1,0:T(1,128)}, u32[]{:S(2)}) copy-start(s32[1,1024]{1,0:T(1,128)} %param.10) | copy-start | bytes 12292
  25.4 14.0 %collective-permute-start.3 = (bf16[2,264,128]{2,1,0:T(8,128)(2,1)}, bf16[2,264,128]{2,1,0:T(8,128)(2,1)S(1)}, u32[]{:S(2)}, u32[]{:S(2)}) collective-permute-start(bf16[2,264,128]{2,1,0:T(8,128)(2,1)} %join.1.refs_0_), channel_id=1, source_target_pairs={{0,2},{1,3},{2,0},{3,1},{4,6},{5,7},{6,4},{7,5},{8,10},{9,11},{10,... | collective-permute-start | bytes 405512 | tf_op jit(solution)/shard_map/ppermute | solution.py:441
  26.0 13.5 %collective-permute-start.4 = (bf16[2,264,128]{2,1,0:T(8,128)(2,1)}, bf16[2,264,128]{2,1,0:T(8,128)(2,1)S(1)}, u32[]{:S(2)}, u32[]{:S(2)}) collective-permute-start(bf16[2,264,128]{2,1,0:T(8,128)(2,1)} %join.1.refs_0_), channel_id=1, source_target_pairs={{0,4},{1,5},{2,6},{3,7},{4,0},{5,1},{6,2},{7,3},{8,12},{9,13},{10,... | collective-permute-start | bytes 405512 | tf_op jit(solution)/shard_map/ppermute | solution.py:441
  26.6 12.9 %collective-permute-start.5 = (bf16[2,264,128]{2,1,0:T(8,128)(2,1)}, bf16[2,264,128]{2,1,0:T(8,128)(2,1)S(1)}, u32[]{:S(2)}, u32[]{:S(2)}) collective-permute-start(bf16[2,264,128]{2,1,0:T(8,128)(2,1)} %join.1.refs_0_), channel_id=1, source_target_pairs={{0,6},{1,7},{2,4},{3,5},{4,2},{5,3},{6,0},{7,1},{8,14},{9,15},{10,... | collective-permute-start | bytes 405512 | tf_op jit(solution)/shard_map/ppermute | solution.py:441
  29.9 9.6 %copy-start = (bf16[2,264,128]{2,1,0:T(8,128)(2,1)S(1)}, bf16[2,264,128]{2,1,0:T(8,128)(2,1)}, u32[]{:S(2)}) copy-start(bf16[2,264,128]{2,1,0:T(8,128)(2,1)} %join.1.refs_0_) | copy-start | bytes 405508
  48.3 26.7 %collective-permute-start.13 = (bf16[2,128,2048]{2,1,0:T(8,128)(2,1)S(1)}, bf16[2,128,2048]{2,1,0:T(8,128)(2,1)S(1)}, u32[]{:S(2)}, u32[]{:S(2)}) collective-permute-start(bf16[2,128,2048]{2,1,0:T(8,128)(2,1)S(1)} %get-tuple-element.46), channel_id=1, source_target_pairs={{0,1},{1,0},{2,3},{3,2},{4,5},{5,4},{6,7},{7,6},{8,9},{9,8},{10,11... | collective-permute-start | bytes 3145736 | tf_op jit(solution)/shard_map/ppermute | solution.py:466
  48.3 8.6 %collective-permute-start.14 = (bf16[2,256,128]{2,1,0:T(8,128)(2,1)S(1)}, bf16[2,256,128]{2,1,0:T(8,128)(2,1)S(1)}, u32[]{:S(2)}, u32[]{:S(2)}) collective-permute-start(bf16[2,256,128]{2,1,0:T(8,128)(2,1)S(1)} %get-tuple-element.48), channel_id=1, source_target_pairs={{0,2},{1,3},{2,0},{3,1},{4,6},{5,7},{6,4},{7,5},{8,10},{9,11},{10,... | collective-permute-start | bytes 393224 | tf_op jit(solution)/shard_map/ppermute | solution.py:463
  50.6 12.9 %collective-permute-start.15 = (bf16[2,256,128]{2,1,0:T(8,128)(2,1)S(1)}, bf16[2,256,128]{2,1,0:T(8,128)(2,1)S(1)}, u32[]{:S(2)}, u32[]{:S(2)}) collective-permute-start(bf16[2,256,128]{2,1,0:T(8,128)(2,1)S(1)} %get-tuple-element.49), channel_id=1, source_target_pairs={{0,4},{1,5},{2,6},{3,7},{4,0},{5,1},{6,2},{7,3},{8,12},{9,13},{10,... | collective-permute-start | bytes 393224 | tf_op jit(solution)/shard_map/ppermute | solution.py:463
  51.3 1.9 %collective-permute-start.18 = (f32[32,128]{1,0:T(8,128)S(1)}, f32[32,128]{1,0:T(8,128)S(1)}, u32[]{:S(2)}, u32[]{:S(2)}) collective-permute-start(f32[32,128]{1,0:T(8,128)S(1)} %get-tuple-element.58), channel_id=1, source_target_pairs={{0,1},{1,0},{2,3},{3,2},{4,5},{5,4},{6,7},{7,6},{8,9},{9,8},{10,11... | collective-permute-start | bytes 49160 | tf_op jit(solution)/shard_map/ppermute | solution.py:467
  51.5 14.4 %collective-permute-start.16 = (bf16[2,256,128]{2,1,0:T(8,128)(2,1)S(1)}, bf16[2,256,128]{2,1,0:T(8,128)(2,1)S(1)}, u32[]{:S(2)}, u32[]{:S(2)}) collective-permute-start(bf16[2,256,128]{2,1,0:T(8,128)(2,1)S(1)} %get-tuple-element.50), channel_id=1, source_target_pairs={{0,6},{1,7},{2,4},{3,5},{4,2},{5,3},{6,0},{7,1},{8,14},{9,15},{10,... | collective-permute-start | bytes 393224 | tf_op jit(solution)/shard_map/ppermute | solution.py:463
  53.2 13.7 %collective-permute-start.19 = (f32[2,32,128]{2,1,0:T(8,128)S(1)}, f32[2,32,128]{2,1,0:T(8,128)S(1)}, u32[]{:S(2)}, u32[]{:S(2)}) collective-permute-start(f32[2,32,128]{2,1,0:T(8,128)S(1)} %pad_maximum_fusion), channel_id=1, source_target_pairs={{0,8},{8,0},{16,24},{24,16},{1,9},{9,1},{17,25},{25,17},{2,10},{10... | collective-permute-start | bytes 98312 | tf_op jit(solution)/shard_map/ppermute | solution.py:393
  56.9 12.6 %collective-permute-start.20 = (f32[2,32,128]{2,1,0:T(8,128)S(1)}, f32[2,32,128]{2,1,0:T(8,128)S(1)}, u32[]{:S(2)}, u32[]{:S(2)}) collective-permute-start(f32[2,32,128]{2,1,0:T(8,128)S(1)} %pad_maximum_fusion), channel_id=1, source_target_pairs={{0,16},{8,24},{16,0},{24,8},{1,17},{9,25},{17,1},{25,9},{2,18},{10... | collective-permute-start | bytes 98312 | tf_op jit(solution)/shard_map/ppermute | solution.py:393
  63.5 7.6 %collective-permute-start.21 = (f32[2,32,128]{2,1,0:T(8,128)S(1)}, f32[2,32,128]{2,1,0:T(8,128)S(1)}, u32[]{:S(2)}, u32[]{:S(2)}) collective-permute-start(f32[2,32,128]{2,1,0:T(8,128)S(1)} %pad_maximum_fusion), channel_id=1, source_target_pairs={{0,24},{8,16},{16,8},{24,0},{1,25},{9,17},{17,9},{25,1},{2,26},{10... | collective-permute-start | bytes 98312 | tf_op jit(solution)/shard_map/ppermute | solution.py:393
  66.0 6.3 %collective-permute-start.25 = (bf16[2,256,128]{2,1,0:T(8,128)(2,1)S(1)}, bf16[2,256,128]{2,1,0:T(8,128)(2,1)S(1)}, u32[]{:S(2)}, u32[]{:S(2)}) collective-permute-start(bf16[2,256,128]{2,1,0:T(8,128)(2,1)S(1)} %get-tuple-element.60), channel_id=1, source_target_pairs={{0,2},{1,3},{2,0},{3,1},{4,6},{5,7},{6,4},{7,5},{8,10},{9,11},{10,... | collective-permute-start | bytes 393224 | tf_op jit(solution)/shard_map/ppermute | solution.py:463
  66.9 13.0 %collective-permute-start.26 = (bf16[2,256,128]{2,1,0:T(8,128)(2,1)S(1)}, bf16[2,256,128]{2,1,0:T(8,128)(2,1)S(1)}, u32[]{:S(2)}, u32[]{:S(2)}) collective-permute-start(bf16[2,256,128]{2,1,0:T(8,128)(2,1)S(1)} %get-tuple-element.61), channel_id=1, source_target_pairs={{0,4},{1,5},{2,6},{3,7},{4,0},{5,1},{6,2},{7,3},{8,12},{9,13},{10,... | collective-permute-start | bytes 393224 | tf_op jit(solution)/shard_map/ppermute | solution.py:463
  69.5 10.4 %collective-permute-start.27 = (bf16[2,256,128]{2,1,0:T(8,128)(2,1)S(1)}, bf16[2,256,128]{2,1,0:T(8,128)(2,1)S(1)}, u32[]{:S(2)}, u32[]{:S(2)}) collective-permute-start(bf16[2,256,128]{2,1,0:T(8,128)(2,1)S(1)} %get-tuple-element.62), channel_id=1, source_target_pairs={{0,6},{1,7},{2,4},{3,5},{4,2},{5,3},{6,0},{7,1},{8,14},{9,15},{10,... | collective-permute-start | bytes 393224 | tf_op jit(solution)/shard_map/ppermute | solution.py:463
  71.1 1.3 %collective-permute-start.17 = (bf16[256,128]{1,0:T(8,128)(2,1)S(1)}, bf16[256,128]{1,0:T(8,128)(2,1)S(1)}, u32[]{:S(2)}, u32[]{:S(2)}) collective-permute-start(bf16[256,128]{1,0:T(8,128)(2,1)S(1)} %get-tuple-element.51), channel_id=1, source_target_pairs={{0,1},{1,0},{2,3},{3,2},{4,5},{5,4},{6,7},{7,6},{8,9},{9,8},{10,11... | collective-permute-start | bytes 196616 | tf_op jit(solution)/shard_map/ppermute | solution.py:474
  72.3 8.3 %collective-permute-start.22 = (f32[2,32,128]{2,1,0:T(8,128)S(1)}, f32[2,32,128]{2,1,0:T(8,128)S(1)}, u32[]{:S(2)}, u32[]{:S(2)}) collective-permute-start(f32[2,32,128]{2,1,0:T(8,128)S(1)} %add_add_fusion.1), channel_id=1, source_target_pairs={{0,2},{1,3},{2,0},{3,1},{4,6},{5,7},{6,4},{7,5},{8,10},{9,11},{10,... | collective-permute-start | bytes 98312 | tf_op jit(solution)/shard_map/ppermute | solution.py:393
  72.4 10.8 %collective-permute-start.23 = (f32[2,32,128]{2,1,0:T(8,128)S(1)}, f32[2,32,128]{2,1,0:T(8,128)S(1)}, u32[]{:S(2)}, u32[]{:S(2)}) collective-permute-start(f32[2,32,128]{2,1,0:T(8,128)S(1)} %add_add_fusion.1), channel_id=1, source_target_pairs={{0,4},{1,5},{2,6},{3,7},{4,0},{5,1},{6,2},{7,3},{8,12},{9,13},{10,... | collective-permute-start | bytes 98312 | tf_op jit(solution)/shard_map/ppermute | solution.py:393
  75.0 8.2 %collective-permute-start.24 = (f32[2,32,128]{2,1,0:T(8,128)S(1)}, f32[2,32,128]{2,1,0:T(8,128)S(1)}, u32[]{:S(2)}, u32[]{:S(2)}) collective-permute-start(f32[2,32,128]{2,1,0:T(8,128)S(1)} %add_add_fusion.1), channel_id=1, source_target_pairs={{0,6},{1,7},{2,4},{3,5},{4,2},{5,3},{6,0},{7,1},{8,14},{9,15},{10,... | collective-permute-start | bytes 98312 | tf_op jit(solution)/shard_map/ppermute | solution.py:393
  80.6 2.5 %collective-permute-start.28 = (bf16[256,128]{1,0:T(8,128)(2,1)S(1)}, bf16[256,128]{1,0:T(8,128)(2,1)S(1)}, u32[]{:S(2)}, u32[]{:S(2)}) collective-permute-start(bf16[256,128]{1,0:T(8,128)(2,1)S(1)} %get-tuple-element.65), channel_id=1, source_target_pairs={{0,1},{1,0},{2,3},{3,2},{4,5},{5,4},{6,7},{7,6},{8,9},{9,8},{10,11... | collective-permute-start | bytes 196616 | tf_op jit(solution)/shard_map/ppermute | solution.py:474

commit v4 on v3

--- a/solution.py
+++ b/solution.py
@@ -246,16 +246,6 @@
     )(index, group_first, keys, values)
 
 
-def join_kernel(near, away, out):
-    out[0] = near[...]
-    out[1] = away[...]
-
-
-def join(near, away):
-    shape = jax.ShapeDtypeStruct((CORES, *near.shape), jnp.bfloat16)
-    return pl.pallas_call(join_kernel, out_shape=shape, name="join")(near, away)
-
-
 def place_kernel(index_ref, far, piece, *refs):
     attended, grad_query, grad_key, grad_value = refs[-4:]
     attended[...] = far[0]
@@ -435,7 +425,7 @@
         mine = blocks[CORES * hh : CORES * (hh + 1)]
         if JOIN[hh % len(JOIN)]:
             away = lax.ppermute(mine[1], "ctx", across)
-            both = join(mine[0], away)
+            both = jnp.stack([mine[0], away])
             pairs = [both] * chips
             for k in order:
                 pairs[k] = lax.ppermute(both, "ctx", over(k))

time: 84.2 us -> 83 us (0.986)
  starting transfers between devices: 38.4 us -> 43.5 us
  waiting for transfers between devices: 17.2 us -> 14.2 us
  Pallas kernels: 24.9 us -> 22.3 us
    ppermute x6, starting transfers between devices: 9.06 us -> 12 us  [body(): pieces[k] = lax.ppermute(parts[k], 'ctx', over(k))]
    ppermute x3, starting transfers between devices: 4.39 us -> 6.56 us  [body(): pairs[k] = lax.ppermute(both, 'ctx', over(k))]
    pallas_call x1 -> x0, Pallas kernels: 1.61 us -> none  [join(): return pl.pallas_call(join_kernel, out_shape=shape, name='join')(near, away)]
    ppermute x6, waiting for transfers between devices: 10.7 us -> 9.3 us  [body(): pieces[k] = lax.ppermute(parts[k], 'ctx', over(k))]
    ppermute x7, waiting for transfers between devices: 3.91 us -> 2.83 us  [body(): pairs[r] = lax.ppermute(mine[r % CORES], 'ctx', xor(r))]
    pallas_call x2, Pallas kernels: 18.4 us -> 17.4 us  [attention(): pl.pallas_call(functools.partial(attention_kernel, carried=carried is not...]
  transfers between devices with their start and end apart: 29 -> 29, of which waited for: 8 -> 6; matrix products, arithmetic and copies ran while one was open for 2% -> 2% of each run, Pallas kernels for 18% -> 15%
where the time goes in v4:
time: 83 us; the launch traced here: 82.8 us
  starting transfers between devices  43.5 us (52%)
  Pallas kernels  22.3 us (27%)
  waiting for transfers between devices  14.2 us (17%)
  between operations  1.4 us (2%)
  local copies, waits for them, and re-layouts  1.33 us (2%)
    pallas_call x2, Pallas kernels, attention(): pl.pallas_call(functools.partial(attention_kernel, carried=carried is not...  17.4 us
    ppermute x7, starting transfers between devices, body(): pairs[r] = lax.ppermute(mine[r % CORES], 'ctx', xor(r))  14.4 us
    ppermute x6, starting transfers between devices, body(): pieces[k] = lax.ppermute(parts[k], 'ctx', over(k))  12 us
    ppermute x6, starting transfers between devices, summed(): moved = lax.ppermute(part, axis, [(i, i ^ mixed) for i in range(size)])  9.68 us
    ppermute x6, waiting for transfers between devices, body(): pieces[k] = lax.ppermute(parts[k], 'ctx', over(k))  9.3 us
    ppermute x3, starting transfers between devices, body(): pairs[k] = lax.ppermute(both, 'ctx', over(k))  6.56 us
    ppermute x7, waiting for transfers between devices, body(): pairs[r] = lax.ppermute(mine[r % CORES], 'ctx', xor(r))  2.83 us
    ppermute x6, waiting for transfers between devices, summed(): moved = lax.ppermute(part, axis, [(i, i ^ mixed) for i in range(size)])  1.76 us
  transfers between devices with their start and end apart: 29, of which 6 were waited for; matrix products, arithmetic and copies ran while one was open for 2% of the time, Pallas kernels for 15%

profile of v4, /device:TPU:0, one launch (start us, length us, event | category | flops | bytes accessed | tf_op | source)
XLA Modules:
  0.0 82.8 jit_solution(15931677730255266224)
XLA Ops:
  0.6 0.6 collective-permute-start
  1.2 0.1 collective-permute-start.1
  1.9 1.7 %payload.1 = (bf16[264,128]{1,0:T(8,128)(2,1)}, bf16[264,128]{1,0:T(8,128)(2,1)}, bf16[264,128]{1,0:T(8,128)(2,1)}, bf16[264,128]{1,0:T(8,128)(2,1)}) custom-call(s32[1]{0:T(128)} %bitcast.index_ref, s32[1,1]{1,0:T(1,128)S(6)} %copy.35.first_ref, bf16[128,512]{1,0:T(8,128)(2,1)} %keys.1, bf16[128,512]{1,0:T(8,128)(2,1)} %values.1), custom_call_target="tpu_custom_call" | custom-call | tf_op jit(solution)/shard_map/payload/pallas_call | solution.py:241
  3.6 3.7 %collective-permute-start.10 = (bf16[264,128]{1,0:T(8,128)(2,1)}, bf16[264,128]{1,0:T(8,128)(2,1)S(1)}, u32[]{:S(2)}, u32[]{:S(2)}) collective-permute-start(bf16[264,128]{1,0:T(8,128)(2,1)} %get-tuple-element.41), channel_id=1, source_target_pairs={{0,5},{1,4},{2,7},{3,6},{4,1},{5,0},{6,3},{7,2},{8,13},{9,12},{10,... | collective-permute-start | bytes 202760 | tf_op jit(solution)/shard_map/ppermute | solution.py:435
  7.3 1.3 %collective-permute-start.11 = (bf16[264,128]{1,0:T(8,128)(2,1)}, bf16[264,128]{1,0:T(8,128)(2,1)S(1)}, u32[]{:S(2)}, u32[]{:S(2)}) collective-permute-start(bf16[264,128]{1,0:T(8,128)(2,1)} %get-tuple-element.40.refs_0_), channel_id=1, source_target_pairs={{0,6},{1,7},{2,4},{3,5},{4,2},{5,3},{6,0},{7,1},{8,14},{9,15},{10,... | collective-permute-start | bytes 202760 | tf_op jit(solution)/shard_map/ppermute | solution.py:435
  8.7 2.2 %collective-permute-start.12 = (bf16[264,128]{1,0:T(8,128)(2,1)}, bf16[264,128]{1,0:T(8,128)(2,1)S(1)}, u32[]{:S(2)}, u32[]{:S(2)}) collective-permute-start(bf16[264,128]{1,0:T(8,128)(2,1)} %get-tuple-element.41), channel_id=1, source_target_pairs={{0,7},{1,6},{2,5},{3,4},{4,3},{5,2},{6,1},{7,0},{8,15},{9,14},{10,... | collective-permute-start | bytes 202760 | tf_op jit(solution)/shard_map/ppermute | solution.py:435
  10.9 0.0 collective-permute-done.10.refs_5_
  10.9 0.4 collective-permute-start.6
  11.3 2.8 %collective-permute-done.11.refs_6_ = bf16[264,128]{1,0:T(8,128)(2,1)S(1)} collective-permute-done((bf16[264,128]{1,0:T(8,128)(2,1)}, bf16[264,128]{1,0:T(8,128)(2,1)S(1)}, u32[]{:S(2)}, u32[]{:S(2)}) %collective-permute-start.11) | collective-permute-done | bytes 67616 | tf_op jit(solution)/shard_map/ppermute | solution.py:435
  14.1 0.0 collective-permute-start.2
  14.1 1.3 %constant_dynamic-slice_fusion = (bf16[128,2048]{1,0:T(8,128)(2,1)S(1)}, bf16[128,2048]{1,0:T(8,128)(2,1)S(1)}) fusion(bf16[128,4096]{1,0:T(8,128)(2,1)} %param.9, s32[]{:T(128)S(6)} %select_n.12, bf16[128,4096]{1,0:T(8,128)(2,1)} %param.6), kind=kLoop, calls=%fused_computation.4 | loop fusion | bytes 2097156 | tf_op jit(solution)/shard_map/dynamic_slice | solution.py:420
  15.4 0.0 collective-permute-done.12.refs_7_
  15.4 3.2 %collective-permute-start.7 = (bf16[264,128]{1,0:T(8,128)(2,1)S(1)}, bf16[264,128]{1,0:T(8,128)(2,1)S(1)}, u32[]{:S(2)}, u32[]{:S(2)}) collective-permute-start(bf16[264,128]{1,0:T(8,128)(2,1)S(1)} %copy-done), channel_id=1, source_target_pairs={{0,2},{1,3},{2,0},{3,1},{4,6},{5,7},{6,4},{7,5},{8,10},{9,11},{10,... | collective-permute-start | bytes 202760 | tf_op jit(solution)/shard_map/ppermute | solution.py:435
  18.7 0.0 collective-permute-done.6.refs_1_
  18.7 0.1 collective-permute-start.8
  18.8 0.0 collective-permute-done.2
  18.8 3.5 %collective-permute-start.9 = (bf16[264,128]{1,0:T(8,128)(2,1)S(1)}, bf16[264,128]{1,0:T(8,128)(2,1)S(1)}, u32[]{:S(2)}, u32[]{:S(2)}) collective-permute-start(bf16[264,128]{1,0:T(8,128)(2,1)S(1)} %copy-done), channel_id=1, source_target_pairs={{0,4},{1,5},{2,6},{3,7},{4,0},{5,1},{6,2},{7,3},{8,12},{9,13},{10,... | collective-permute-start | bytes 202760 | tf_op jit(solution)/shard_map/ppermute | solution.py:435
  22.3 0.0 copy-start.1
  22.3 0.0 collective-permute-done.7.refs_2_
  22.3 1.4 %collective-permute-start.3 = (bf16[2,264,128]{2,1,0:T(8,128)(2,1)S(1)}, bf16[2,264,128]{2,1,0:T(8,128)(2,1)S(1)}, u32[]{:S(2)}, u32[]{:S(2)}) collective-permute-start(bf16[2,264,128]{2,1,0:T(8,128)(2,1)S(1)} %pad_maximum_fusion.refs_0_), channel_id=1, source_target_pairs={{0,2},{1,3},{2,0},{3,1},{4,6},{5,7},{6,4},{7,5},{8,10},{9,11},{10,... | collective-permute-start | bytes 405512 | tf_op jit(solution)/shard_map/ppermute | solution.py:431
  23.7 0.0 collective-permute-done.8.refs_3_
  23.7 2.1 %collective-permute-start.4 = (bf16[2,264,128]{2,1,0:T(8,128)(2,1)S(1)}, bf16[2,264,128]{2,1,0:T(8,128)(2,1)S(1)}, u32[]{:S(2)}, u32[]{:S(2)}) collective-permute-start(bf16[2,264,128]{2,1,0:T(8,128)(2,1)S(1)} %pad_maximum_fusion.refs_0_), channel_id=1, source_target_pairs={{0,4},{1,5},{2,6},{3,7},{4,0},{5,1},{6,2},{7,3},{8,12},{9,13},{10,... | collective-permute-start | bytes 405512 | tf_op jit(solution)/shard_map/ppermute | solution.py:431
  25.8 0.0 collective-permute-done.9.refs_4_
  25.8 3.0 %collective-permute-start.5 = (bf16[2,264,128]{2,1,0:T(8,128)(2,1)S(1)}, bf16[2,264,128]{2,1,0:T(8,128)(2,1)S(1)}, u32[]{:S(2)}, u32[]{:S(2)}) collective-permute-start(bf16[2,264,128]{2,1,0:T(8,128)(2,1)S(1)} %pad_maximum_fusion.refs_0_), channel_id=1, source_target_pairs={{0,6},{1,7},{2,4},{3,5},{4,2},{5,3},{6,0},{7,1},{8,14},{9,15},{10,... | collective-permute-start | bytes 405512 | tf_op jit(solution)/shard_map/ppermute | solution.py:431
  28.8 0.0 collective-permute-done.query_far
  28.8 0.0 collective-permute-done.1.grad_far
  28.9 8.6 %attention.2 = (bf16[128,4096]{1,0:T(8,128)(2,1)}, bf16[128,4096]{1,0:T(8,128)(2,1)}, f32[32,128]{1,0:T(8,128)S(1)}, bf16[2,128,2048]{2,1,0:T(8,128)(2,1)S(1)}, ...) custom-call(s32[1]{0:T(128)} %bitcast.index_ref, ...), custom_call_target="tpu_custom_call" | custom-call | flops 3221225472 | bytes 2097152 | tf_op jit(solution)/shard_map/attention/pallas_call | solution.py:198
  37.5 0.0 collective-permute-done.3.refs_1_
  37.5 0.0 collective-permute-done.4.refs_2_
  37.5 0.0 collective-permute-done.5.refs_3_
  37.5 8.7 %attention.3 = (bf16[128,4096]{1,0:T(8,128)(2,1)}, bf16[128,4096]{1,0:T(8,128)(2,1)}, f32[32,128]{1,0:T(8,128)S(1)}, bf16[2,128,2048]{2,1,0:T(8,128)(2,1)S(1)}, ...) custom-call(s32[1]{0:T(128)} %bitcast.index_ref, ...), custom_call_target="tpu_custom_call", output_to_operand_aliasing={{0}: (10, {}), {1}: (11, {}), {2}: (12, {}), {3}: (13, {})} | custom-call | flops 3221225472 | bytes 2097152 | tf_op jit(solution)/shard_map/attention/pallas_call | solution.py:198
  46.2 0.0 collective-permute-start.13
  46.3 2.6 %collective-permute-start.14 = (bf16[2,256,128]{2,1,0:T(8,128)(2,1)S(1)}, bf16[2,256,128]{2,1,0:T(8,128)(2,1)S(1)}, u32[]{:S(2)}, u32[]{:S(2)}) collective-permute-start(bf16[2,256,128]{2,1,0:T(8,128)(2,1)S(1)} %get-tuple-element.48), channel_id=1, source_target_pairs={{0,2},{1,3},{2,0},{3,1},{4,6},{5,7},{6,4},{7,5},{8,10},{9,11},{10,... | collective-permute-start | bytes 393224 | tf_op jit(solution)/shard_map/ppermute | solution.py:453
  48.8 1.9 %collective-permute-start.15 = (bf16[2,256,128]{2,1,0:T(8,128)(2,1)S(1)}, bf16[2,256,128]{2,1,0:T(8,128)(2,1)S(1)}, u32[]{:S(2)}, u32[]{:S(2)}) collective-permute-start(bf16[2,256,128]{2,1,0:T(8,128)(2,1)S(1)} %get-tuple-element.49), channel_id=1, source_target_pairs={{0,4},{1,5},{2,6},{3,7},{4,0},{5,1},{6,2},{7,3},{8,12},{9,13},{10,... | collective-permute-start | bytes 393224 | tf_op jit(solution)/shard_map/ppermute | solution.py:453
  50.8 0.2 collective-permute-start.18
  51.0 1.5 %collective-permute-start.16 = (bf16[2,256,128]{2,1,0:T(8,128)(2,1)S(1)}, bf16[2,256,128]{2,1,0:T(8,128)(2,1)S(1)}, u32[]{:S(2)}, u32[]{:S(2)}) collective-permute-start(bf16[2,256,128]{2,1,0:T(8,128)(2,1)S(1)} %get-tuple-element.50), channel_id=1, source_target_pairs={{0,6},{1,7},{2,4},{3,5},{4,2},{5,3},{6,0},{7,1},{8,14},{9,15},{10,... | collective-permute-start | bytes 393224 | tf_op jit(solution)/shard_map/ppermute | solution.py:453
  52.4 0.0 collective-permute-done.18
  52.4 1.5 %collective-permute-start.19 = (f32[2,32,128]{2,1,0:T(8,128)S(1)}, f32[2,32,128]{2,1,0:T(8,128)S(1)}, u32[]{:S(2)}, u32[]{:S(2)}) collective-permute-start(f32[2,32,128]{2,1,0:T(8,128)S(1)} %pad_maximum_fusion.1), channel_id=1, source_target_pairs={{0,8},{8,0},{16,24},{24,16},{1,9},{9,1},{17,25},{25,17},{2,10},{10... | collective-permute-start | bytes 98312 | tf_op jit(solution)/shard_map/ppermute | solution.py:383
  53.9 1.9 %collective-permute-done.14.refs_1_ = bf16[2,256,128]{2,1,0:T(8,128)(2,1)S(1)} collective-permute-done((bf16[2,256,128]{2,1,0:T(8,128)(2,1)S(1)}, bf16[2,256,128]{2,1,0:T(8,128)(2,1)S(1)}, u32[]{:S(2)}, u32[]{:S(2)}) %collective-permute-start.14) | collective-permute-done | bytes 131104 | tf_op jit(solution)/shard_map/ppermute | solution.py:453
  55.8 1.5 %collective-permute-start.20 = (f32[2,32,128]{2,1,0:T(8,128)S(1)}, f32[2,32,128]{2,1,0:T(8,128)S(1)}, u32[]{:S(2)}, u32[]{:S(2)}) collective-permute-start(f32[2,32,128]{2,1,0:T(8,128)S(1)} %pad_maximum_fusion.1), channel_id=1, source_target_pairs={{0,16},{8,24},{16,0},{24,8},{1,17},{9,25},{17,1},{25,9},{2,18},{10... | collective-permute-start | bytes 98312 | tf_op jit(solution)/shard_map/ppermute | solution.py:383
  57.3 0.0 collective-permute-done.15.refs_2_
  57.3 1.4 %collective-permute-start.21 = (f32[2,32,128]{2,1,0:T(8,128)S(1)}, f32[2,32,128]{2,1,0:T(8,128)S(1)}, u32[]{:S(2)}, u32[]{:S(2)}) collective-permute-start(f32[2,32,128]{2,1,0:T(8,128)S(1)} %pad_maximum_fusion.1), channel_id=1, source_target_pairs={{0,24},{8,16},{16,8},{24,0},{1,25},{9,17},{17,9},{25,1},{2,26},{10... | collective-permute-start | bytes 98312 | tf_op jit(solution)/shard_map/ppermute | solution.py:383
  58.8 3.0 %collective-permute-done.16.refs_3_ = bf16[2,256,128]{2,1,0:T(8,128)(2,1)S(1)} collective-permute-done((bf16[2,256,128]{2,1,0:T(8,128)(2,1)S(1)}, bf16[2,256,128]{2,1,0:T(8,128)(2,1)S(1)}, u32[]{:S(2)}, u32[]{:S(2)}) %collective-permute-start.16) | collective-permute-done | bytes 131104 | tf_op jit(solution)/shard_map/ppermute | solution.py:453
  61.8 2.6 %collective-permute-start.25 = (bf16[2,256,128]{2,1,0:T(8,128)(2,1)S(1)}, bf16[2,256,128]{2,1,0:T(8,128)(2,1)S(1)}, u32[]{:S(2)}, u32[]{:S(2)}) collective-permute-start(bf16[2,256,128]{2,1,0:T(8,128)(2,1)S(1)} %get-tuple-element.60), channel_id=1, source_target_pairs={{0,2},{1,3},{2,0},{3,1},{4,6},{5,7},{6,4},{7,5},{8,10},{9,11},{10,... | collective-permute-start | bytes 393224 | tf_op jit(solution)/shard_map/ppermute | solution.py:453
  64.4 0.7 shard_map.101
  65.2 0.0 collective-permute-done.19
  65.2 3.4 %collective-permute-start.26 = (bf16[2,256,128]{2,1,0:T(8,128)(2,1)S(1)}, bf16[2,256,128]{2,1,0:T(8,128)(2,1)S(1)}, u32[]{:S(2)}, u32[]{:S(2)}) collective-permute-start(bf16[2,256,128]{2,1,0:T(8,128)(2,1)S(1)} %get-tuple-element.61), channel_id=1, source_target_pairs={{0,4},{1,5},{2,6},{3,7},{4,0},{5,1},{6,2},{7,3},{8,12},{9,13},{10,... | collective-permute-start | bytes 393224 | tf_op jit(solution)/shard_map/ppermute | solution.py:453
  68.5 0.0 collective-permute-done.20
  68.5 0.0 collective-permute-start.27
  68.5 0.0 collective-permute-done.21
  68.6 0.1 collective-permute-start.17
  68.7 0.0 collective-permute-done.25.refs_1_
  68.7 1.0 %collective-permute-start.22 = (f32[2,32,128]{2,1,0:T(8,128)S(1)}, f32[2,32,128]{2,1,0:T(8,128)S(1)}, u32[]{:S(2)}, u32[]{:S(2)}) collective-permute-start(f32[2,32,128]{2,1,0:T(8,128)S(1)} %add_add_fusion.1), channel_id=1, source_target_pairs={{0,2},{1,3},{2,0},{3,1},{4,6},{5,7},{6,4},{7,5},{8,10},{9,11},{10,... | collective-permute-start | bytes 98312 | tf_op jit(solution)/shard_map/ppermute | solution.py:383
  69.6 0.3 collective-permute-done.17.piece
  69.9 3.3 %collective-permute-start.23 = (f32[2,32,128]{2,1,0:T(8,128)S(1)}, f32[2,32,128]{2,1,0:T(8,128)S(1)}, u32[]{:S(2)}, u32[]{:S(2)}) collective-permute-start(f32[2,32,128]{2,1,0:T(8,128)S(1)} %add_add_fusion.1), channel_id=1, source_target_pairs={{0,4},{1,5},{2,6},{3,7},{4,0},{5,1},{6,2},{7,3},{8,12},{9,13},{10,... | collective-permute-start | bytes 98312 | tf_op jit(solution)/shard_map/ppermute | solution.py:383
  73.2 1.0 %collective-permute-start.24 = (f32[2,32,128]{2,1,0:T(8,128)S(1)}, f32[2,32,128]{2,1,0:T(8,128)S(1)}, u32[]{:S(2)}, u32[]{:S(2)}) collective-permute-start(f32[2,32,128]{2,1,0:T(8,128)S(1)} %add_add_fusion.1), channel_id=1, source_target_pairs={{0,6},{1,7},{2,4},{3,5},{4,2},{5,3},{6,0},{7,1},{8,14},{9,15},{10,... | collective-permute-start | bytes 98312 | tf_op jit(solution)/shard_map/ppermute | solution.py:383
  74.2 1.0 %place.1 = (bf16[128,4096]{1,0:T(8,128)(2,1)}, bf16[128,4096]{1,0:T(8,128)(2,1)}, bf16[128,512]{1,0:T(8,128)(2,1)}, bf16[128,512]{1,0:T(8,128)(2,1)}) custom-call(s32[1]{0:T(128)} %bitcast.index_ref, bf16[2,128,2048]{2,1,0:T(8,128)(2,1)S(1)} %collective-permute-done.13.far, ...), custom_call_target="tpu_custom_call", output_to_operand_aliasing={{0}: (3, {}), {1}: (4, {}), {2}: (5, {}), {3}: (6, {})} | custom-call | tf_op jit(solution)/shard_map/place/pallas_call | solution.py:271
  75.2 4.4 %collective-permute-done.26.refs_2_ = bf16[2,256,128]{2,1,0:T(8,128)(2,1)S(1)} collective-permute-done((bf16[2,256,128]{2,1,0:T(8,128)(2,1)S(1)}, bf16[2,256,128]{2,1,0:T(8,128)(2,1)S(1)}, u32[]{:S(2)}, u32[]{:S(2)}) %collective-permute-start.26) | collective-permute-done | bytes 131104 | tf_op jit(solution)/shard_map/ppermute | solution.py:453
  79.6 0.0 collective-permute-done.27.refs_3_
  79.6 0.7 shard_map.102
  80.3 0.0 collective-permute-start.28
  80.3 1.7 %collective-permute-done.23 = f32[2,32,128]{2,1,0:T(8,128)S(1)} collective-permute-done((f32[2,32,128]{2,1,0:T(8,128)S(1)}, f32[2,32,128]{2,1,0:T(8,128)S(1)}, u32[]{:S(2)}, u32[]{:S(2)}) %collective-permute-start.23) | collective-permute-done | bytes 32800 | tf_op jit(solution)/shard_map/ppermute | solution.py:383
  82.0 0.0 collective-permute-done.24
  82.1 0.7 last.1
  (14 shorter events, 0.1 us)
Async XLA Ops:
  0.6 28.2 %collective-permute-start = (bf16[128,4096]{1,0:T(8,128)(2,1)}, bf16[128,4096]{1,0:T(8,128)(2,1)S(1)}, u32[]{:S(2)}, u32[]{:S(2)}) collective-permute-start(bf16[128,4096]{1,0:T(8,128)(2,1)} %param.6), channel_id=1, source_target_pairs={{0,1},{1,0},{2,3},{3,2},{4,5},{5,4},{6,7},{7,6},{8,9},{9,8},{10,11... | collective-permute-start | bytes 3145736 | tf_op jit(solution)/shard_map/ppermute | solution.py:416
  1.2 27.7 %collective-permute-start.1 = (bf16[128,4096]{1,0:T(8,128)(2,1)}, bf16[128,4096]{1,0:T(8,128)(2,1)S(1)}, u32[]{:S(2)}, u32[]{:S(2)}) collective-permute-start(bf16[128,4096]{1,0:T(8,128)(2,1)} %param.9), channel_id=1, source_target_pairs={{0,1},{1,0},{2,3},{3,2},{4,5},{5,4},{6,7},{7,6},{8,9},{9,8},{10,11... | collective-permute-start | bytes 3145736 | tf_op jit(solution)/shard_map/ppermute | solution.py:417
  3.6 7.3 %collective-permute-start.10 = (bf16[264,128]{1,0:T(8,128)(2,1)}, bf16[264,128]{1,0:T(8,128)(2,1)S(1)}, u32[]{:S(2)}, u32[]{:S(2)}) collective-permute-start(bf16[264,128]{1,0:T(8,128)(2,1)} %get-tuple-element.41), channel_id=1, source_target_pairs={{0,5},{1,4},{2,7},{3,6},{4,1},{5,0},{6,3},{7,2},{8,13},{9,12},{10,... | collective-permute-start | bytes 202760 | tf_op jit(solution)/shard_map/ppermute | solution.py:435
  7.3 6.8 %collective-permute-start.11 = (bf16[264,128]{1,0:T(8,128)(2,1)}, bf16[264,128]{1,0:T(8,128)(2,1)S(1)}, u32[]{:S(2)}, u32[]{:S(2)}) collective-permute-start(bf16[264,128]{1,0:T(8,128)(2,1)} %get-tuple-element.40.refs_0_), channel_id=1, source_target_pairs={{0,6},{1,7},{2,4},{3,5},{4,2},{5,3},{6,0},{7,1},{8,14},{9,15},{10,... | collective-permute-start | bytes 202760 | tf_op jit(solution)/shard_map/ppermute | solution.py:435
  8.7 6.7 %collective-permute-start.12 = (bf16[264,128]{1,0:T(8,128)(2,1)}, bf16[264,128]{1,0:T(8,128)(2,1)S(1)}, u32[]{:S(2)}, u32[]{:S(2)}) collective-permute-start(bf16[264,128]{1,0:T(8,128)(2,1)} %get-tuple-element.41), channel_id=1, source_target_pairs={{0,7},{1,6},{2,5},{3,4},{4,3},{5,2},{6,1},{7,0},{8,15},{9,14},{10,... | collective-permute-start | bytes 202760 | tf_op jit(solution)/shard_map/ppermute | solution.py:435
  10.9 7.8 %collective-permute-start.6 = (bf16[264,128]{1,0:T(8,128)(2,1)}, bf16[264,128]{1,0:T(8,128)(2,1)S(1)}, u32[]{:S(2)}, u32[]{:S(2)}) collective-permute-start(bf16[264,128]{1,0:T(8,128)(2,1)} %get-tuple-element.41), channel_id=1, source_target_pairs={{0,1},{1,0},{2,3},{3,2},{4,5},{5,4},{6,7},{7,6},{8,9},{9,8},{10,11... | collective-permute-start | bytes 202760 | tf_op jit(solution)/shard_map/ppermute | solution.py:435
  14.1 1.3 %copy-start = (bf16[264,128]{1,0:T(8,128)(2,1)S(1)}, bf16[264,128]{1,0:T(8,128)(2,1)}, u32[]{:S(2)}) copy-start(bf16[264,128]{1,0:T(8,128)(2,1)} %get-tuple-element.40.refs_0_) | copy-start | bytes 202756
  14.1 4.6 %copy-start.3 = (bf16[264,128]{1,0:T(8,128)(2,1)S(1)}, bf16[264,128]{1,0:T(8,128)(2,1)}, u32[]{:S(2)}) copy-start(bf16[264,128]{1,0:T(8,128)(2,1)} %get-tuple-element.41) | copy-start | bytes 202756
  14.1 8.1 %copy-start.2 = (bf16[264,128]{1,0:T(8,128)(2,1)S(1)}, bf16[264,128]{1,0:T(8,128)(2,1)}, u32[]{:S(2)}) copy-start(bf16[264,128]{1,0:T(8,128)(2,1)} %get-tuple-element.38) | copy-start | bytes 202756
  14.1 4.7 %collective-permute-start.2 = (bf16[264,128]{1,0:T(8,128)(2,1)}, bf16[264,128]{1,0:T(8,128)(2,1)S(1)}, u32[]{:S(2)}, u32[]{:S(2)}) collective-permute-start(bf16[264,128]{1,0:T(8,128)(2,1)} %get-tuple-element.39), channel_id=1, source_target_pairs={{0,1},{1,0},{2,3},{3,2},{4,5},{5,4},{6,7},{7,6},{8,9},{9,8},{10,11... | collective-permute-start | bytes 202760 | tf_op jit(solution)/shard_map/ppermute | solution.py:427
  15.4 6.8 %collective-permute-start.7 = (bf16[264,128]{1,0:T(8,128)(2,1)S(1)}, bf16[264,128]{1,0:T(8,128)(2,1)S(1)}, u32[]{:S(2)}, u32[]{:S(2)}) collective-permute-start(bf16[264,128]{1,0:T(8,128)(2,1)S(1)} %copy-done), channel_id=1, source_target_pairs={{0,2},{1,3},{2,0},{3,1},{4,6},{5,7},{6,4},{7,5},{8,10},{9,11},{10,... | collective-permute-start | bytes 202760 | tf_op jit(solution)/shard_map/ppermute | solution.py:435
  18.7 5.0 %collective-permute-start.8 = (bf16[264,128]{1,0:T(8,128)(2,1)S(1)}, bf16[264,128]{1,0:T(8,128)(2,1)S(1)}, u32[]{:S(2)}, u32[]{:S(2)}) collective-permute-start(bf16[264,128]{1,0:T(8,128)(2,1)S(1)} %copy-done.3), channel_id=1, source_target_pairs={{0,3},{1,2},{2,1},{3,0},{4,7},{5,6},{6,5},{7,4},{8,11},{9,10},{10,... | collective-permute-start | bytes 202760 | tf_op jit(solution)/shard_map/ppermute | solution.py:435
  18.8 7.0 %collective-permute-start.9 = (bf16[264,128]{1,0:T(8,128)(2,1)S(1)}, bf16[264,128]{1,0:T(8,128)(2,1)S(1)}, u32[]{:S(2)}, u32[]{:S(2)}) collective-permute-start(bf16[264,128]{1,0:T(8,128)(2,1)S(1)} %copy-done), channel_id=1, source_target_pairs={{0,4},{1,5},{2,6},{3,7},{4,0},{5,1},{6,2},{7,3},{8,12},{9,13},{10,... | collective-permute-start | bytes 202760 | tf_op jit(solution)/shard_map/ppermute | solution.py:435
  22.3 6.6 %copy-start.1 = (s32[1,1024]{1,0:T(1,128)S(1)}, s32[1,1024]{1,0:T(1,128)}, u32[]{:S(2)}) copy-start(s32[1,1024]{1,0:T(1,128)} %param.10) | copy-start | bytes 12292
  22.3 15.2 %collective-permute-start.3 = (bf16[2,264,128]{2,1,0:T(8,128)(2,1)S(1)}, bf16[2,264,128]{2,1,0:T(8,128)(2,1)S(1)}, u32[]{:S(2)}, u32[]{:S(2)}) collective-permute-start(bf16[2,264,128]{2,1,0:T(8,128)(2,1)S(1)} %pad_maximum_fusion.refs_0_), channel_id=1, source_target_pairs={{0,2},{1,3},{2,0},{3,1},{4,6},{5,7},{6,4},{7,5},{8,10},{9,11},{10,... | collective-permute-start | bytes 405512 | tf_op jit(solution)/shard_map/ppermute | solution.py:431
  23.7 13.8 %collective-permute-start.4 = (bf16[2,264,128]{2,1,0:T(8,128)(2,1)S(1)}, bf16[2,264,128]{2,1,0:T(8,128)(2,1)S(1)}, u32[]{:S(2)}, u32[]{:S(2)}) collective-permute-start(bf16[2,264,128]{2,1,0:T(8,128)(2,1)S(1)} %pad_maximum_fusion.refs_0_), channel_id=1, source_target_pairs={{0,4},{1,5},{2,6},{3,7},{4,0},{5,1},{6,2},{7,3},{8,12},{9,13},{10,... | collective-permute-start | bytes 405512 | tf_op jit(solution)/shard_map/ppermute | solution.py:431
  25.8 11.7 %collective-permute-start.5 = (bf16[2,264,128]{2,1,0:T(8,128)(2,1)S(1)}, bf16[2,264,128]{2,1,0:T(8,128)(2,1)S(1)}, u32[]{:S(2)}, u32[]{:S(2)}) collective-permute-start(bf16[2,264,128]{2,1,0:T(8,128)(2,1)S(1)} %pad_maximum_fusion.refs_0_), channel_id=1, source_target_pairs={{0,6},{1,7},{2,4},{3,5},{4,2},{5,3},{6,0},{7,1},{8,14},{9,15},{10,... | collective-permute-start | bytes 405512 | tf_op jit(solution)/shard_map/ppermute | solution.py:431
  46.2 26.9 %collective-permute-start.13 = (bf16[2,128,2048]{2,1,0:T(8,128)(2,1)S(1)}, bf16[2,128,2048]{2,1,0:T(8,128)(2,1)S(1)}, u32[]{:S(2)}, u32[]{:S(2)}) collective-permute-start(bf16[2,128,2048]{2,1,0:T(8,128)(2,1)S(1)} %get-tuple-element.46), channel_id=1, source_target_pairs={{0,1},{1,0},{2,3},{3,2},{4,5},{5,4},{6,7},{7,6},{8,9},{9,8},{10,11... | collective-permute-start | bytes 3145736 | tf_op jit(solution)/shard_map/ppermute | solution.py:456
  46.3 9.5 %collective-permute-start.14 = (bf16[2,256,128]{2,1,0:T(8,128)(2,1)S(1)}, bf16[2,256,128]{2,1,0:T(8,128)(2,1)S(1)}, u32[]{:S(2)}, u32[]{:S(2)}) collective-permute-start(bf16[2,256,128]{2,1,0:T(8,128)(2,1)S(1)} %get-tuple-element.48), channel_id=1, source_target_pairs={{0,2},{1,3},{2,0},{3,1},{4,6},{5,7},{6,4},{7,5},{8,10},{9,11},{10,... | collective-permute-start | bytes 393224 | tf_op jit(solution)/shard_map/ppermute | solution.py:453
  48.8 8.5 %collective-permute-start.15 = (bf16[2,256,128]{2,1,0:T(8,128)(2,1)S(1)}, bf16[2,256,128]{2,1,0:T(8,128)(2,1)S(1)}, u32[]{:S(2)}, u32[]{:S(2)}) collective-permute-start(bf16[2,256,128]{2,1,0:T(8,128)(2,1)S(1)} %get-tuple-element.49), channel_id=1, source_target_pairs={{0,4},{1,5},{2,6},{3,7},{4,0},{5,1},{6,2},{7,3},{8,12},{9,13},{10,... | collective-permute-start | bytes 393224 | tf_op jit(solution)/shard_map/ppermute | solution.py:453
  50.8 1.7 %collective-permute-start.18 = (f32[32,128]{1,0:T(8,128)S(1)}, f32[32,128]{1,0:T(8,128)S(1)}, u32[]{:S(2)}, u32[]{:S(2)}) collective-permute-start(f32[32,128]{1,0:T(8,128)S(1)} %get-tuple-element.58), channel_id=1, source_target_pairs={{0,1},{1,0},{2,3},{3,2},{4,5},{5,4},{6,7},{7,6},{8,9},{9,8},{10,11... | collective-permute-start | bytes 49160 | tf_op jit(solution)/shard_map/ppermute | solution.py:457
  51.0 10.8 %collective-permute-start.16 = (bf16[2,256,128]{2,1,0:T(8,128)(2,1)S(1)}, bf16[2,256,128]{2,1,0:T(8,128)(2,1)S(1)}, u32[]{:S(2)}, u32[]{:S(2)}) collective-permute-start(bf16[2,256,128]{2,1,0:T(8,128)(2,1)S(1)} %get-tuple-element.50), channel_id=1, source_target_pairs={{0,6},{1,7},{2,4},{3,5},{4,2},{5,3},{6,0},{7,1},{8,14},{9,15},{10,... | collective-permute-start | bytes 393224 | tf_op jit(solution)/shard_map/ppermute | solution.py:453
  52.4 12.7 %collective-permute-start.19 = (f32[2,32,128]{2,1,0:T(8,128)S(1)}, f32[2,32,128]{2,1,0:T(8,128)S(1)}, u32[]{:S(2)}, u32[]{:S(2)}) collective-permute-start(f32[2,32,128]{2,1,0:T(8,128)S(1)} %pad_maximum_fusion.1), channel_id=1, source_target_pairs={{0,8},{8,0},{16,24},{24,16},{1,9},{9,1},{17,25},{25,17},{2,10},{10... | collective-permute-start | bytes 98312 | tf_op jit(solution)/shard_map/ppermute | solution.py:383
  55.8 12.7 %collective-permute-start.20 = (f32[2,32,128]{2,1,0:T(8,128)S(1)}, f32[2,32,128]{2,1,0:T(8,128)S(1)}, u32[]{:S(2)}, u32[]{:S(2)}) collective-permute-start(f32[2,32,128]{2,1,0:T(8,128)S(1)} %pad_maximum_fusion.1), channel_id=1, source_target_pairs={{0,16},{8,24},{16,0},{24,8},{1,17},{9,25},{17,1},{25,9},{2,18},{10... | collective-permute-start | bytes 98312 | tf_op jit(solution)/shard_map/ppermute | solution.py:383
  57.3 11.2 %collective-permute-start.21 = (f32[2,32,128]{2,1,0:T(8,128)S(1)}, f32[2,32,128]{2,1,0:T(8,128)S(1)}, u32[]{:S(2)}, u32[]{:S(2)}) collective-permute-start(f32[2,32,128]{2,1,0:T(8,128)S(1)} %pad_maximum_fusion.1), channel_id=1, source_target_pairs={{0,24},{8,16},{16,8},{24,0},{1,25},{9,17},{17,9},{25,1},{2,26},{10... | collective-permute-start | bytes 98312 | tf_op jit(solution)/shard_map/ppermute | solution.py:383
  61.8 6.9 %collective-permute-start.25 = (bf16[2,256,128]{2,1,0:T(8,128)(2,1)S(1)}, bf16[2,256,128]{2,1,0:T(8,128)(2,1)S(1)}, u32[]{:S(2)}, u32[]{:S(2)}) collective-permute-start(bf16[2,256,128]{2,1,0:T(8,128)(2,1)S(1)} %get-tuple-element.60), channel_id=1, source_target_pairs={{0,2},{1,3},{2,0},{3,1},{4,6},{5,7},{6,4},{7,5},{8,10},{9,11},{10,... | collective-permute-start | bytes 393224 | tf_op jit(solution)/shard_map/ppermute | solution.py:453
  65.2 14.4 %collective-permute-start.26 = (bf16[2,256,128]{2,1,0:T(8,128)(2,1)S(1)}, bf16[2,256,128]{2,1,0:T(8,128)(2,1)S(1)}, u32[]{:S(2)}, u32[]{:S(2)}) collective-permute-start(bf16[2,256,128]{2,1,0:T(8,128)(2,1)S(1)} %get-tuple-element.61), channel_id=1, source_target_pairs={{0,4},{1,5},{2,6},{3,7},{4,0},{5,1},{6,2},{7,3},{8,12},{9,13},{10,... | collective-permute-start | bytes 393224 | tf_op jit(solution)/shard_map/ppermute | solution.py:453
  68.5 11.0 %collective-permute-start.27 = (bf16[2,256,128]{2,1,0:T(8,128)(2,1)S(1)}, bf16[2,256,128]{2,1,0:T(8,128)(2,1)S(1)}, u32[]{:S(2)}, u32[]{:S(2)}) collective-permute-start(bf16[2,256,128]{2,1,0:T(8,128)(2,1)S(1)} %get-tuple-element.62), channel_id=1, source_target_pairs={{0,6},{1,7},{2,4},{3,5},{4,2},{5,3},{6,0},{7,1},{8,14},{9,15},{10,... | collective-permute-start | bytes 393224 | tf_op jit(solution)/shard_map/ppermute | solution.py:453
  68.6 1.3 %collective-permute-start.17 = (bf16[256,128]{1,0:T(8,128)(2,1)S(1)}, bf16[256,128]{1,0:T(8,128)(2,1)S(1)}, u32[]{:S(2)}, u32[]{:S(2)}) collective-permute-start(bf16[256,128]{1,0:T(8,128)(2,1)S(1)} %get-tuple-element.51), channel_id=1, source_target_pairs={{0,1},{1,0},{2,3},{3,2},{4,5},{5,4},{6,7},{7,6},{8,9},{9,8},{10,11... | collective-permute-start | bytes 196616 | tf_op jit(solution)/shard_map/ppermute | solution.py:464
  68.7 11.6 %collective-permute-start.22 = (f32[2,32,128]{2,1,0:T(8,128)S(1)}, f32[2,32,128]{2,1,0:T(8,128)S(1)}, u32[]{:S(2)}, u32[]{:S(2)}) collective-permute-start(f32[2,32,128]{2,1,0:T(8,128)S(1)} %add_add_fusion.1), channel_id=1, source_target_pairs={{0,2},{1,3},{2,0},{3,1},{4,6},{5,7},{6,4},{7,5},{8,10},{9,11},{10,... | collective-permute-start | bytes 98312 | tf_op jit(solution)/shard_map/ppermute | solution.py:383
  69.9 12.2 %collective-permute-start.23 = (f32[2,32,128]{2,1,0:T(8,128)S(1)}, f32[2,32,128]{2,1,0:T(8,128)S(1)}, u32[]{:S(2)}, u32[]{:S(2)}) collective-permute-start(f32[2,32,128]{2,1,0:T(8,128)S(1)} %add_add_fusion.1), channel_id=1, source_target_pairs={{0,4},{1,5},{2,6},{3,7},{4,0},{5,1},{6,2},{7,3},{8,12},{9,13},{10,... | collective-permute-start | bytes 98312 | tf_op jit(solution)/shard_map/ppermute | solution.py:383
  73.2 8.9 %collective-permute-start.24 = (f32[2,32,128]{2,1,0:T(8,128)S(1)}, f32[2,32,128]{2,1,0:T(8,128)S(1)}, u32[]{:S(2)}, u32[]{:S(2)}) collective-permute-start(f32[2,32,128]{2,1,0:T(8,128)S(1)} %add_add_fusion.1), channel_id=1, source_target_pairs={{0,6},{1,7},{2,4},{3,5},{4,2},{5,3},{6,0},{7,1},{8,14},{9,15},{10,... | collective-permute-start | bytes 98312 | tf_op jit(solution)/shard_map/ppermute | solution.py:383
  80.3 1.8 %collective-permute-start.28 = (bf16[256,128]{1,0:T(8,128)(2,1)S(1)}, bf16[256,128]{1,0:T(8,128)(2,1)S(1)}, u32[]{:S(2)}, u32[]{:S(2)}) collective-permute-start(bf16[256,128]{1,0:T(8,128)(2,1)S(1)} %get-tuple-element.65), channel_id=1, source_target_pairs={{0,1},{1,0},{2,3},{3,2},{4,5},{5,4},{6,7},{7,6},{8,9},{9,8},{10,11... | collective-permute-start | bytes 196616 | tf_op jit(solution)/shard_map/ppermute | solution.py:464

commit v5 on v4

--- a/solution.py
+++ b/solution.py
@@ -459,13 +459,15 @@
     both = summed(both, "ctx", powers(CORES, devices))
     factor = 1.0 / math.sqrt(length * devices * replicas)
     grads = None
+    crossed = []
     for hh in range(chunks):
         *grads, away = settle(index_arg, hh, chunks, returned[hh], key_rows.shape, grads)
-        away = lax.ppermute(away, "ctx", across)
-        if hh < chunks - 1:
-            attended, grad_query, *grads = place(
-                index_arg, hh, chunks, far_out, away, (attended, grad_query, *grads)
-            )
+        crossed.append(lax.ppermute(away, "ctx", across))
+    for hh in range(chunks - 1):
+        attended, grad_query, *grads = place(
+            index_arg, hh, chunks, far_out, crossed[hh], (attended, grad_query, *grads)
+        )
+    away = crossed[-1]
     *grads, bias_grad = last(index_arg, both, chunks - 1, chunks, away, grads, factor)
     return (attended, grad_query, *grads, bias_grad.reshape(-1))
 

time: 83 us -> 79.3 us (0.955)
  starting transfers between devices: 43.5 us -> 32.9 us
  waiting for transfers between devices: 14.2 us -> 21.2 us
    ppermute x7, starting transfers between devices: 14.4 us -> 10.3 us  [body(): pairs[r] = lax.ppermute(mine[r % CORES], 'ctx', xor(r))]
    ppermute x6, starting transfers between devices: 12 us -> 8.63 us  [body(): pieces[k] = lax.ppermute(parts[k], 'ctx', over(k))]
    ppermute x7, waiting for transfers between devices: 2.83 us -> 6.18 us  [body(): pairs[r] = lax.ppermute(mine[r % CORES], 'ctx', xor(r))]
    ppermute x6, waiting for transfers between devices: 9.3 us -> 11.5 us  [body(): pieces[k] = lax.ppermute(parts[k], 'ctx', over(k))]
    ppermute x3, starting transfers between devices: 6.56 us -> 4.39 us  [body(): pairs[k] = lax.ppermute(both, 'ctx', over(k))]
    ppermute x6, starting transfers between devices: 9.68 us -> 7.53 us  [summed(): moved = lax.ppermute(part, axis, [(i, i ^ mixed) for i in range(size)])]
  transfers between devices with their start and end apart: 29 -> 29, of which waited for: 6 -> 10; matrix products, arithmetic and copies ran while one was open for 2% -> 2% of each run, Pallas kernels for 15% -> 16%
where the time goes in v5:
time: 79.3 us; the launch traced here: 79.1 us
  starting transfers between devices  32.9 us (41%)
  Pallas kernels  22.3 us (28%)
  waiting for transfers between devices  21.2 us (27%)
  between operations  1.37 us (2%)
  local copies, waits for them, and re-layouts  1.28 us (2%)
    pallas_call x2, Pallas kernels, attention(): pl.pallas_call(functools.partial(attention_kernel, carried=carried is not...  17.4 us
    ppermute x6, waiting for transfers between devices, body(): pieces[k] = lax.ppermute(parts[k], 'ctx', over(k))  11.5 us
    ppermute x7, starting transfers between devices, body(): pairs[r] = lax.ppermute(mine[r % CORES], 'ctx', xor(r))  10.3 us
    ppermute x6, starting transfers between devices, body(): pieces[k] = lax.ppermute(parts[k], 'ctx', over(k))  8.63 us
    ppermute x6, starting transfers between devices, summed(): moved = lax.ppermute(part, axis, [(i, i ^ mixed) for i in range(size)])  7.53 us
    ppermute x7, waiting for transfers between devices, body(): pairs[r] = lax.ppermute(mine[r % CORES], 'ctx', xor(r))  6.18 us
    ppermute x3, starting transfers between devices, body(): pairs[k] = lax.ppermute(both, 'ctx', over(k))  4.39 us
    ppermute x6, waiting for transfers between devices, summed(): moved = lax.ppermute(part, axis, [(i, i ^ mixed) for i in range(size)])  2.29 us
  transfers between devices with their start and end apart: 29, of which 10 were waited for; matrix products, arithmetic and copies ran while one was open for 2% of the time, Pallas kernels for 16%

profile of v5, /device:TPU:0, one launch (start us, length us, event | category | flops | bytes accessed | tf_op | source)
XLA Modules:
  0.0 79.1 jit_solution(17251599884120359477)
XLA Ops:
  0.6 0.6 collective-permute-start
  1.2 0.1 collective-permute-start.1
  1.9 1.7 %payload.1 = (bf16[264,128]{1,0:T(8,128)(2,1)}, bf16[264,128]{1,0:T(8,128)(2,1)}, bf16[264,128]{1,0:T(8,128)(2,1)}, bf16[264,128]{1,0:T(8,128)(2,1)}) custom-call(s32[1]{0:T(128)} %bitcast.index_ref, s32[1,1]{1,0:T(1,128)S(6)} %copy.35.first_ref, bf16[128,512]{1,0:T(8,128)(2,1)} %keys.1, bf16[128,512]{1,0:T(8,128)(2,1)} %values.1), custom_call_target="tpu_custom_call" | custom-call | tf_op jit(solution)/shard_map/payload/pallas_call | solution.py:241
  3.6 0.4 collective-permute-start.2
  4.1 4.7 %collective-permute-start.11 = (bf16[264,128]{1,0:T(8,128)(2,1)}, bf16[264,128]{1,0:T(8,128)(2,1)S(1)}, u32[]{:S(2)}, u32[]{:S(2)}) collective-permute-start(bf16[264,128]{1,0:T(8,128)(2,1)} %get-tuple-element.40.refs_0_), channel_id=1, source_target_pairs={{0,6},{1,7},{2,4},{3,5},{4,2},{5,3},{6,0},{7,1},{8,14},{9,15},{10,... | collective-permute-start | bytes 202760 | tf_op jit(solution)/shard_map/ppermute | solution.py:435
  8.7 0.0 collective-permute-start.9
  8.7 0.0 collective-permute-done.2
  8.7 0.6 collective-permute-start.7
  9.3 2.6 %collective-permute-done.11.refs_6_ = bf16[264,128]{1,0:T(8,128)(2,1)S(1)} collective-permute-done((bf16[264,128]{1,0:T(8,128)(2,1)}, bf16[264,128]{1,0:T(8,128)(2,1)S(1)}, u32[]{:S(2)}, u32[]{:S(2)}) %collective-permute-start.11) | collective-permute-done | bytes 67616 | tf_op jit(solution)/shard_map/ppermute | solution.py:435
  11.9 2.5 %collective-permute-start.12 = (bf16[264,128]{1,0:T(8,128)(2,1)}, bf16[264,128]{1,0:T(8,128)(2,1)S(1)}, u32[]{:S(2)}, u32[]{:S(2)}) collective-permute-start(bf16[264,128]{1,0:T(8,128)(2,1)} %get-tuple-element.41), channel_id=1, source_target_pairs={{0,7},{1,6},{2,5},{3,4},{4,3},{5,2},{6,1},{7,0},{8,15},{9,14},{10,... | collective-permute-start | bytes 202760 | tf_op jit(solution)/shard_map/ppermute | solution.py:435
  14.4 1.3 %constant_dynamic-slice_fusion = (bf16[128,2048]{1,0:T(8,128)(2,1)S(1)}, bf16[128,2048]{1,0:T(8,128)(2,1)S(1)}) fusion(bf16[128,4096]{1,0:T(8,128)(2,1)} %param.9, s32[]{:T(128)S(6)} %select_n.12, bf16[128,4096]{1,0:T(8,128)(2,1)} %param.6), kind=kLoop, calls=%fused_computation.4 | loop fusion | bytes 2097156 | tf_op jit(solution)/shard_map/dynamic_slice | solution.py:420
  15.7 0.0 collective-permute-done.9.refs_4_
  15.7 1.6 %collective-permute-start.10 = (bf16[264,128]{1,0:T(8,128)(2,1)S(1)}, bf16[264,128]{1,0:T(8,128)(2,1)S(1)}, u32[]{:S(2)}, u32[]{:S(2)}) collective-permute-start(bf16[264,128]{1,0:T(8,128)(2,1)S(1)} %copy-done.3), channel_id=1, source_target_pairs={{0,5},{1,4},{2,7},{3,6},{4,1},{5,0},{6,3},{7,2},{8,13},{9,12},{10,... | collective-permute-start | bytes 202760 | tf_op jit(solution)/shard_map/ppermute | solution.py:435
  17.3 0.0 collective-permute-done.7.refs_2_
  17.3 0.6 collective-permute-start.8
  17.9 0.0 collective-permute-done.12.refs_7_
  17.9 0.3 collective-permute-start.6
  18.3 0.0 copy-start.1
  18.3 3.6 %collective-permute-done.10.refs_5_ = bf16[264,128]{1,0:T(8,128)(2,1)S(1)} collective-permute-done((bf16[264,128]{1,0:T(8,128)(2,1)S(1)}, bf16[264,128]{1,0:T(8,128)(2,1)S(1)}, u32[]{:S(2)}, u32[]{:S(2)}) %collective-permute-start.10) | collective-permute-done | bytes 67616 | tf_op jit(solution)/shard_map/ppermute | solution.py:435
  21.9 2.7 %collective-permute-start.5 = (bf16[2,264,128]{2,1,0:T(8,128)(2,1)S(1)}, bf16[2,264,128]{2,1,0:T(8,128)(2,1)S(1)}, u32[]{:S(2)}, u32[]{:S(2)}) collective-permute-start(bf16[2,264,128]{2,1,0:T(8,128)(2,1)S(1)} %pad_maximum_fusion.refs_0_), channel_id=1, source_target_pairs={{0,6},{1,7},{2,4},{3,5},{4,2},{5,3},{6,0},{7,1},{8,14},{9,15},{10,... | collective-permute-start | bytes 405512 | tf_op jit(solution)/shard_map/ppermute | solution.py:431
  24.6 0.0 collective-permute-done.8.refs_3_
  24.6 0.0 collective-permute-start.4
  24.6 0.0 collective-permute-done.6.refs_1_
  24.6 1.7 %collective-permute-start.3 = (bf16[2,264,128]{2,1,0:T(8,128)(2,1)S(1)}, bf16[2,264,128]{2,1,0:T(8,128)(2,1)S(1)}, u32[]{:S(2)}, u32[]{:S(2)}) collective-permute-start(bf16[2,264,128]{2,1,0:T(8,128)(2,1)S(1)} %pad_maximum_fusion.refs_0_), channel_id=1, source_target_pairs={{0,2},{1,3},{2,0},{3,1},{4,6},{5,7},{6,4},{7,5},{8,10},{9,11},{10,... | collective-permute-start | bytes 405512 | tf_op jit(solution)/shard_map/ppermute | solution.py:431
  26.3 0.0 collective-permute-done.query_far
  26.3 0.0 collective-permute-done.1.grad_far
  26.3 8.6 %attention.2 = (bf16[128,4096]{1,0:T(8,128)(2,1)}, bf16[128,4096]{1,0:T(8,128)(2,1)}, f32[32,128]{1,0:T(8,128)S(1)}, bf16[2,128,2048]{2,1,0:T(8,128)(2,1)S(1)}, ...) custom-call(s32[1]{0:T(128)} %bitcast.index_ref, ...), custom_call_target="tpu_custom_call" | custom-call | flops 3221225472 | bytes 2097152 | tf_op jit(solution)/shard_map/attention/pallas_call | solution.py:198
  34.9 0.0 collective-permute-done.5.refs_3_
  34.9 0.6 collective-permute-done.4.refs_2_
  35.5 0.0 collective-permute-done.3.refs_1_
  35.5 8.7 %attention.3 = (bf16[128,4096]{1,0:T(8,128)(2,1)}, bf16[128,4096]{1,0:T(8,128)(2,1)}, f32[32,128]{1,0:T(8,128)S(1)}, bf16[2,128,2048]{2,1,0:T(8,128)(2,1)S(1)}, ...) custom-call(s32[1]{0:T(128)} %bitcast.index_ref, ...), custom_call_target="tpu_custom_call", output_to_operand_aliasing={{0}: (10, {}), {1}: (11, {}), {2}: (12, {}), {3}: (13, {})} | custom-call | flops 3221225472 | bytes 2097152 | tf_op jit(solution)/shard_map/attention/pallas_call | solution.py:198
  44.3 0.0 collective-permute-start.13
  44.3 0.5 collective-permute-start.21
  44.8 0.4 collective-permute-start.18
  45.2 2.4 %collective-permute-start.19 = (bf16[2,256,128]{2,1,0:T(8,128)(2,1)S(1)}, bf16[2,256,128]{2,1,0:T(8,128)(2,1)S(1)}, u32[]{:S(2)}, u32[]{:S(2)}) collective-permute-start(bf16[2,256,128]{2,1,0:T(8,128)(2,1)S(1)} %get-tuple-element.56), channel_id=1, source_target_pairs={{0,4},{1,5},{2,6},{3,7},{4,0},{5,1},{6,2},{7,3},{8,12},{9,13},{10,... | collective-permute-start | bytes 393224 | tf_op jit(solution)/shard_map/ppermute | solution.py:453
  47.6 0.0 collective-permute-done.21
  47.6 1.5 %collective-permute-start.23 = (f32[2,32,128]{2,1,0:T(8,128)S(1)}, f32[2,32,128]{2,1,0:T(8,128)S(1)}, u32[]{:S(2)}, u32[]{:S(2)}) collective-permute-start(f32[2,32,128]{2,1,0:T(8,128)S(1)} %pad_maximum_fusion.1), channel_id=1, source_target_pairs={{0,16},{8,24},{16,0},{24,8},{1,17},{9,25},{17,1},{25,9},{2,18},{10... | collective-permute-start | bytes 98312 | tf_op jit(solution)/shard_map/ppermute | solution.py:383
  49.1 1.4 %collective-permute-start.24 = (f32[2,32,128]{2,1,0:T(8,128)S(1)}, f32[2,32,128]{2,1,0:T(8,128)S(1)}, u32[]{:S(2)}, u32[]{:S(2)}) collective-permute-start(f32[2,32,128]{2,1,0:T(8,128)S(1)} %pad_maximum_fusion.1), channel_id=1, source_target_pairs={{0,24},{8,16},{16,8},{24,0},{1,25},{9,17},{17,9},{25,1},{2,26},{10... | collective-permute-start | bytes 98312 | tf_op jit(solution)/shard_map/ppermute | solution.py:383
  50.5 1.0 %collective-permute-done.23 = f32[2,32,128]{2,1,0:T(8,128)S(1)} collective-permute-done((f32[2,32,128]{2,1,0:T(8,128)S(1)}, f32[2,32,128]{2,1,0:T(8,128)S(1)}, u32[]{:S(2)}, u32[]{:S(2)}) %collective-permute-start.23) | collective-permute-done | bytes 32800 | tf_op jit(solution)/shard_map/ppermute | solution.py:383
  51.5 1.5 %collective-permute-start.22 = (f32[2,32,128]{2,1,0:T(8,128)S(1)}, f32[2,32,128]{2,1,0:T(8,128)S(1)}, u32[]{:S(2)}, u32[]{:S(2)}) collective-permute-start(f32[2,32,128]{2,1,0:T(8,128)S(1)} %pad_maximum_fusion.1), channel_id=1, source_target_pairs={{0,8},{8,0},{16,24},{24,16},{1,9},{9,1},{17,25},{25,17},{2,10},{10... | collective-permute-start | bytes 98312 | tf_op jit(solution)/shard_map/ppermute | solution.py:383
  53.0 1.1 %collective-permute-done.24 = f32[2,32,128]{2,1,0:T(8,128)S(1)} collective-permute-done((f32[2,32,128]{2,1,0:T(8,128)S(1)}, f32[2,32,128]{2,1,0:T(8,128)S(1)}, u32[]{:S(2)}, u32[]{:S(2)}) %collective-permute-start.24) | collective-permute-done | bytes 32800 | tf_op jit(solution)/shard_map/ppermute | solution.py:383
  54.1 1.4 %collective-permute-start.20 = (bf16[2,256,128]{2,1,0:T(8,128)(2,1)S(1)}, bf16[2,256,128]{2,1,0:T(8,128)(2,1)S(1)}, u32[]{:S(2)}, u32[]{:S(2)}) collective-permute-start(bf16[2,256,128]{2,1,0:T(8,128)(2,1)S(1)} %get-tuple-element.57), channel_id=1, source_target_pairs={{0,6},{1,7},{2,4},{3,5},{4,2},{5,3},{6,0},{7,1},{8,14},{9,15},{10,... | collective-permute-start | bytes 393224 | tf_op jit(solution)/shard_map/ppermute | solution.py:453
  55.5 0.0 collective-permute-done.22
  55.5 0.0 collective-permute-start.14
  55.5 0.0 collective-permute-done.18.refs_1_
  55.5 2.9 %collective-permute-start.15 = (bf16[2,256,128]{2,1,0:T(8,128)(2,1)S(1)}, bf16[2,256,128]{2,1,0:T(8,128)(2,1)S(1)}, u32[]{:S(2)}, u32[]{:S(2)}) collective-permute-start(bf16[2,256,128]{2,1,0:T(8,128)(2,1)S(1)} %get-tuple-element.49), channel_id=1, source_target_pairs={{0,4},{1,5},{2,6},{3,7},{4,0},{5,1},{6,2},{7,3},{8,12},{9,13},{10,... | collective-permute-start | bytes 393224 | tf_op jit(solution)/shard_map/ppermute | solution.py:453
  58.5 0.0 collective-permute-done.19.refs_2_
  58.5 1.4 %collective-permute-start.16 = (bf16[2,256,128]{2,1,0:T(8,128)(2,1)S(1)}, bf16[2,256,128]{2,1,0:T(8,128)(2,1)S(1)}, u32[]{:S(2)}, u32[]{:S(2)}) collective-permute-start(bf16[2,256,128]{2,1,0:T(8,128)(2,1)S(1)} %get-tuple-element.50), channel_id=1, source_target_pairs={{0,6},{1,7},{2,4},{3,5},{4,2},{5,3},{6,0},{7,1},{8,14},{9,15},{10,... | collective-permute-start | bytes 393224 | tf_op jit(solution)/shard_map/ppermute | solution.py:453
  59.9 4.9 %collective-permute-done.14.refs_1_ = bf16[2,256,128]{2,1,0:T(8,128)(2,1)S(1)} collective-permute-done((bf16[2,256,128]{2,1,0:T(8,128)(2,1)S(1)}, bf16[2,256,128]{2,1,0:T(8,128)(2,1)S(1)}, u32[]{:S(2)}, u32[]{:S(2)}) %collective-permute-start.14) | collective-permute-done | bytes 131104 | tf_op jit(solution)/shard_map/ppermute | solution.py:453
  64.8 0.3 collective-permute-start.27
  65.2 6.6 %collective-permute-done.15.refs_2_ = bf16[2,256,128]{2,1,0:T(8,128)(2,1)S(1)} collective-permute-done((bf16[2,256,128]{2,1,0:T(8,128)(2,1)S(1)}, bf16[2,256,128]{2,1,0:T(8,128)(2,1)S(1)}, u32[]{:S(2)}, u32[]{:S(2)}) %collective-permute-start.15) | collective-permute-done | bytes 131104 | tf_op jit(solution)/shard_map/ppermute | solution.py:453
  71.7 0.0 collective-permute-start.26
  71.7 0.0 collective-permute-done.16.refs_3_
  71.7 2.8 %collective-permute-start.25 = (f32[2,32,128]{2,1,0:T(8,128)S(1)}, f32[2,32,128]{2,1,0:T(8,128)S(1)}, u32[]{:S(2)}, u32[]{:S(2)}) collective-permute-start(f32[2,32,128]{2,1,0:T(8,128)S(1)} %add_add_fusion.1), channel_id=1, source_target_pairs={{0,2},{1,3},{2,0},{3,1},{4,6},{5,7},{6,4},{7,5},{8,10},{9,11},{10,... | collective-permute-start | bytes 98312 | tf_op jit(solution)/shard_map/ppermute | solution.py:383
  74.5 0.7 shard_map.101
  75.2 0.7 shard_map.102
  76.0 0.5 collective-permute-start.17
  76.5 0.2 collective-permute-done.26
  76.7 0.1 collective-permute-done.25
  76.8 0.6 collective-permute-done.17.piece
  77.4 0.0 collective-permute-done.13.far
  77.4 1.0 %place.1 = (bf16[128,4096]{1,0:T(8,128)(2,1)}, bf16[128,4096]{1,0:T(8,128)(2,1)}, bf16[128,512]{1,0:T(8,128)(2,1)}, bf16[128,512]{1,0:T(8,128)(2,1)}) custom-call(s32[1]{0:T(128)} %bitcast.index_ref, bf16[2,128,2048]{2,1,0:T(8,128)(2,1)S(1)} %collective-permute-done.13.far, ...), custom_call_target="tpu_custom_call", output_to_operand_aliasing={{0}: (3, {}), {1}: (4, {}), {2}: (5, {}), {3}: (6, {})} | custom-call | tf_op jit(solution)/shard_map/place/pallas_call | solution.py:271
  78.4 0.0 collective-permute-done.28.piece
  78.4 0.7 last.1
  (14 shorter events, 0.1 us)
Async XLA Ops:
  0.6 25.6 %collective-permute-start = (bf16[128,4096]{1,0:T(8,128)(2,1)}, bf16[128,4096]{1,0:T(8,128)(2,1)S(1)}, u32[]{:S(2)}, u32[]{:S(2)}) collective-permute-start(bf16[128,4096]{1,0:T(8,128)(2,1)} %param.6), channel_id=1, source_target_pairs={{0,1},{1,0},{2,3},{3,2},{4,5},{5,4},{6,7},{7,6},{8,9},{9,8},{10,11... | collective-permute-start | bytes 3145736 | tf_op jit(solution)/shard_map/ppermute | solution.py:416
  1.2 25.1 %collective-permute-start.1 = (bf16[128,4096]{1,0:T(8,128)(2,1)}, bf16[128,4096]{1,0:T(8,128)(2,1)S(1)}, u32[]{:S(2)}, u32[]{:S(2)}) collective-permute-start(bf16[128,4096]{1,0:T(8,128)(2,1)} %param.9), channel_id=1, source_target_pairs={{0,1},{1,0},{2,3},{3,2},{4,5},{5,4},{6,7},{7,6},{8,9},{9,8},{10,11... | collective-permute-start | bytes 3145736 | tf_op jit(solution)/shard_map/ppermute | solution.py:417
  3.6 5.1 %collective-permute-start.2 = (bf16[264,128]{1,0:T(8,128)(2,1)}, bf16[264,128]{1,0:T(8,128)(2,1)S(1)}, u32[]{:S(2)}, u32[]{:S(2)}) collective-permute-start(bf16[264,128]{1,0:T(8,128)(2,1)} %get-tuple-element.39), channel_id=1, source_target_pairs={{0,1},{1,0},{2,3},{3,2},{4,5},{5,4},{6,7},{7,6},{8,9},{9,8},{10,11... | collective-permute-start | bytes 202760 | tf_op jit(solution)/shard_map/ppermute | solution.py:427
  4.1 7.8 %collective-permute-start.11 = (bf16[264,128]{1,0:T(8,128)(2,1)}, bf16[264,128]{1,0:T(8,128)(2,1)S(1)}, u32[]{:S(2)}, u32[]{:S(2)}) collective-permute-start(bf16[264,128]{1,0:T(8,128)(2,1)} %get-tuple-element.40.refs_0_), channel_id=1, source_target_pairs={{0,6},{1,7},{2,4},{3,5},{4,2},{5,3},{6,0},{7,1},{8,14},{9,15},{10,... | collective-permute-start | bytes 202760 | tf_op jit(solution)/shard_map/ppermute | solution.py:435
  8.7 6.9 %collective-permute-start.9 = (bf16[264,128]{1,0:T(8,128)(2,1)}, bf16[264,128]{1,0:T(8,128)(2,1)S(1)}, u32[]{:S(2)}, u32[]{:S(2)}) collective-permute-start(bf16[264,128]{1,0:T(8,128)(2,1)} %get-tuple-element.40.refs_0_), channel_id=1, source_target_pairs={{0,4},{1,5},{2,6},{3,7},{4,0},{5,1},{6,2},{7,3},{8,12},{9,13},{10,... | collective-permute-start | bytes 202760 | tf_op jit(solution)/shard_map/ppermute | solution.py:435
  8.7 8.6 %collective-permute-start.7 = (bf16[264,128]{1,0:T(8,128)(2,1)}, bf16[264,128]{1,0:T(8,128)(2,1)S(1)}, u32[]{:S(2)}, u32[]{:S(2)}) collective-permute-start(bf16[264,128]{1,0:T(8,128)(2,1)} %get-tuple-element.40.refs_0_), channel_id=1, source_target_pairs={{0,2},{1,3},{2,0},{3,1},{4,6},{5,7},{6,4},{7,5},{8,10},{9,11},{10,... | collective-permute-start | bytes 202760 | tf_op jit(solution)/shard_map/ppermute | solution.py:435
  11.9 3.8 %copy-start.3 = (bf16[264,128]{1,0:T(8,128)(2,1)S(1)}, bf16[264,128]{1,0:T(8,128)(2,1)}, u32[]{:S(2)}) copy-start(bf16[264,128]{1,0:T(8,128)(2,1)} %get-tuple-element.41) | copy-start | bytes 202756
  11.9 6.4 %copy-start.2 = (bf16[264,128]{1,0:T(8,128)(2,1)S(1)}, bf16[264,128]{1,0:T(8,128)(2,1)}, u32[]{:S(2)}) copy-start(bf16[264,128]{1,0:T(8,128)(2,1)} %get-tuple-element.38) | copy-start | bytes 202756
  11.9 6.0 %collective-permute-start.12 = (bf16[264,128]{1,0:T(8,128)(2,1)}, bf16[264,128]{1,0:T(8,128)(2,1)S(1)}, u32[]{:S(2)}, u32[]{:S(2)}) collective-permute-start(bf16[264,128]{1,0:T(8,128)(2,1)} %get-tuple-element.41), channel_id=1, source_target_pairs={{0,7},{1,6},{2,5},{3,4},{4,3},{5,2},{6,1},{7,0},{8,15},{9,14},{10,... | collective-permute-start | bytes 202760 | tf_op jit(solution)/shard_map/ppermute | solution.py:435
  15.7 6.2 %collective-permute-start.10 = (bf16[264,128]{1,0:T(8,128)(2,1)S(1)}, bf16[264,128]{1,0:T(8,128)(2,1)S(1)}, u32[]{:S(2)}, u32[]{:S(2)}) collective-permute-start(bf16[264,128]{1,0:T(8,128)(2,1)S(1)} %copy-done.3), channel_id=1, source_target_pairs={{0,5},{1,4},{2,7},{3,6},{4,1},{5,0},{6,3},{7,2},{8,13},{9,12},{10,... | collective-permute-start | bytes 202760 | tf_op jit(solution)/shard_map/ppermute | solution.py:435
  17.3 7.2 %collective-permute-start.8 = (bf16[264,128]{1,0:T(8,128)(2,1)S(1)}, bf16[264,128]{1,0:T(8,128)(2,1)S(1)}, u32[]{:S(2)}, u32[]{:S(2)}) collective-permute-start(bf16[264,128]{1,0:T(8,128)(2,1)S(1)} %copy-done.3), channel_id=1, source_target_pairs={{0,3},{1,2},{2,1},{3,0},{4,7},{5,6},{6,5},{7,4},{8,11},{9,10},{10,... | collective-permute-start | bytes 202760 | tf_op jit(solution)/shard_map/ppermute | solution.py:435
  17.9 6.6 %collective-permute-start.6 = (bf16[264,128]{1,0:T(8,128)(2,1)S(1)}, bf16[264,128]{1,0:T(8,128)(2,1)S(1)}, u32[]{:S(2)}, u32[]{:S(2)}) collective-permute-start(bf16[264,128]{1,0:T(8,128)(2,1)S(1)} %copy-done.3), channel_id=1, source_target_pairs={{0,1},{1,0},{2,3},{3,2},{4,5},{5,4},{6,7},{7,6},{8,9},{9,8},{10,11... | collective-permute-start | bytes 202760 | tf_op jit(solution)/shard_map/ppermute | solution.py:435
  18.3 8.0 %copy-start = (bf16[264,128]{1,0:T(8,128)(2,1)S(1)}, bf16[264,128]{1,0:T(8,128)(2,1)}, u32[]{:S(2)}) copy-start(bf16[264,128]{1,0:T(8,128)(2,1)} %get-tuple-element.40.refs_0_) | copy-start | bytes 202756
  18.3 8.0 %copy-start.1 = (s32[1,1024]{1,0:T(1,128)S(1)}, s32[1,1024]{1,0:T(1,128)}, u32[]{:S(2)}) copy-start(s32[1,1024]{1,0:T(1,128)} %param.10) | copy-start | bytes 12292
  21.9 13.1 %collective-permute-start.5 = (bf16[2,264,128]{2,1,0:T(8,128)(2,1)S(1)}, bf16[2,264,128]{2,1,0:T(8,128)(2,1)S(1)}, u32[]{:S(2)}, u32[]{:S(2)}) collective-permute-start(bf16[2,264,128]{2,1,0:T(8,128)(2,1)S(1)} %pad_maximum_fusion.refs_0_), channel_id=1, source_target_pairs={{0,6},{1,7},{2,4},{3,5},{4,2},{5,3},{6,0},{7,1},{8,14},{9,15},{10,... | collective-permute-start | bytes 405512 | tf_op jit(solution)/shard_map/ppermute | solution.py:431
  24.6 11.0 %collective-permute-start.4 = (bf16[2,264,128]{2,1,0:T(8,128)(2,1)S(1)}, bf16[2,264,128]{2,1,0:T(8,128)(2,1)S(1)}, u32[]{:S(2)}, u32[]{:S(2)}) collective-permute-start(bf16[2,264,128]{2,1,0:T(8,128)(2,1)S(1)} %pad_maximum_fusion.refs_0_), channel_id=1, source_target_pairs={{0,4},{1,5},{2,6},{3,7},{4,0},{5,1},{6,2},{7,3},{8,12},{9,13},{10,... | collective-permute-start | bytes 405512 | tf_op jit(solution)/shard_map/ppermute | solution.py:431
  24.6 11.0 %collective-permute-start.3 = (bf16[2,264,128]{2,1,0:T(8,128)(2,1)S(1)}, bf16[2,264,128]{2,1,0:T(8,128)(2,1)S(1)}, u32[]{:S(2)}, u32[]{:S(2)}) collective-permute-start(bf16[2,264,128]{2,1,0:T(8,128)(2,1)S(1)} %pad_maximum_fusion.refs_0_), channel_id=1, source_target_pairs={{0,2},{1,3},{2,0},{3,1},{4,6},{5,7},{6,4},{7,5},{8,10},{9,11},{10,... | collective-permute-start | bytes 405512 | tf_op jit(solution)/shard_map/ppermute | solution.py:431
  44.3 33.1 %collective-permute-start.13 = (bf16[2,128,2048]{2,1,0:T(8,128)(2,1)S(1)}, bf16[2,128,2048]{2,1,0:T(8,128)(2,1)S(1)}, u32[]{:S(2)}, u32[]{:S(2)}) collective-permute-start(bf16[2,128,2048]{2,1,0:T(8,128)(2,1)S(1)} %get-tuple-element.46), channel_id=1, source_target_pairs={{0,1},{1,0},{2,3},{3,2},{4,5},{5,4},{6,7},{7,6},{8,9},{9,8},{10,11... | collective-permute-start | bytes 3145736 | tf_op jit(solution)/shard_map/ppermute | solution.py:456
  44.3 3.3 %collective-permute-start.21 = (f32[32,128]{1,0:T(8,128)S(1)}, f32[32,128]{1,0:T(8,128)S(1)}, u32[]{:S(2)}, u32[]{:S(2)}) collective-permute-start(f32[32,128]{1,0:T(8,128)S(1)} %get-tuple-element.64), channel_id=1, source_target_pairs={{0,1},{1,0},{2,3},{3,2},{4,5},{5,4},{6,7},{7,6},{8,9},{9,8},{10,11... | collective-permute-start | bytes 49160 | tf_op jit(solution)/shard_map/ppermute | solution.py:457
  44.8 10.8 %collective-permute-start.18 = (bf16[2,256,128]{2,1,0:T(8,128)(2,1)S(1)}, bf16[2,256,128]{2,1,0:T(8,128)(2,1)S(1)}, u32[]{:S(2)}, u32[]{:S(2)}) collective-permute-start(bf16[2,256,128]{2,1,0:T(8,128)(2,1)S(1)} %get-tuple-element.55), channel_id=1, source_target_pairs={{0,2},{1,3},{2,0},{3,1},{4,6},{5,7},{6,4},{7,5},{8,10},{9,11},{10,... | collective-permute-start | bytes 393224 | tf_op jit(solution)/shard_map/ppermute | solution.py:453
  45.2 13.3 %collective-permute-start.19 = (bf16[2,256,128]{2,1,0:T(8,128)(2,1)S(1)}, bf16[2,256,128]{2,1,0:T(8,128)(2,1)S(1)}, u32[]{:S(2)}, u32[]{:S(2)}) collective-permute-start(bf16[2,256,128]{2,1,0:T(8,128)(2,1)S(1)} %get-tuple-element.56), channel_id=1, source_target_pairs={{0,4},{1,5},{2,6},{3,7},{4,0},{5,1},{6,2},{7,3},{8,12},{9,13},{10,... | collective-permute-start | bytes 393224 | tf_op jit(solution)/shard_map/ppermute | solution.py:453
  47.6 3.9 %collective-permute-start.23 = (f32[2,32,128]{2,1,0:T(8,128)S(1)}, f32[2,32,128]{2,1,0:T(8,128)S(1)}, u32[]{:S(2)}, u32[]{:S(2)}) collective-permute-start(f32[2,32,128]{2,1,0:T(8,128)S(1)} %pad_maximum_fusion.1), channel_id=1, source_target_pairs={{0,16},{8,24},{16,0},{24,8},{1,17},{9,25},{17,1},{25,9},{2,18},{10... | collective-permute-start | bytes 98312 | tf_op jit(solution)/shard_map/ppermute | solution.py:383
  49.1 5.0 %collective-permute-start.24 = (f32[2,32,128]{2,1,0:T(8,128)S(1)}, f32[2,32,128]{2,1,0:T(8,128)S(1)}, u32[]{:S(2)}, u32[]{:S(2)}) collective-permute-start(f32[2,32,128]{2,1,0:T(8,128)S(1)} %pad_maximum_fusion.1), channel_id=1, source_target_pairs={{0,24},{8,16},{16,8},{24,0},{1,25},{9,17},{17,9},{25,1},{2,26},{10... | collective-permute-start | bytes 98312 | tf_op jit(solution)/shard_map/ppermute | solution.py:383
  51.5 4.0 %collective-permute-start.22 = (f32[2,32,128]{2,1,0:T(8,128)S(1)}, f32[2,32,128]{2,1,0:T(8,128)S(1)}, u32[]{:S(2)}, u32[]{:S(2)}) collective-permute-start(f32[2,32,128]{2,1,0:T(8,128)S(1)} %pad_maximum_fusion.1), channel_id=1, source_target_pairs={{0,8},{8,0},{16,24},{24,16},{1,9},{9,1},{17,25},{25,17},{2,10},{10... | collective-permute-start | bytes 98312 | tf_op jit(solution)/shard_map/ppermute | solution.py:383
  54.1 21.2 %collective-permute-start.20 = (bf16[2,256,128]{2,1,0:T(8,128)(2,1)S(1)}, bf16[2,256,128]{2,1,0:T(8,128)(2,1)S(1)}, u32[]{:S(2)}, u32[]{:S(2)}) collective-permute-start(bf16[2,256,128]{2,1,0:T(8,128)(2,1)S(1)} %get-tuple-element.57), channel_id=1, source_target_pairs={{0,6},{1,7},{2,4},{3,5},{4,2},{5,3},{6,0},{7,1},{8,14},{9,15},{10,... | collective-permute-start | bytes 393224 | tf_op jit(solution)/shard_map/ppermute | solution.py:453
  55.5 9.3 %collective-permute-start.14 = (bf16[2,256,128]{2,1,0:T(8,128)(2,1)S(1)}, bf16[2,256,128]{2,1,0:T(8,128)(2,1)S(1)}, u32[]{:S(2)}, u32[]{:S(2)}) collective-permute-start(bf16[2,256,128]{2,1,0:T(8,128)(2,1)S(1)} %get-tuple-element.48), channel_id=1, source_target_pairs={{0,2},{1,3},{2,0},{3,1},{4,6},{5,7},{6,4},{7,5},{8,10},{9,11},{10,... | collective-permute-start | bytes 393224 | tf_op jit(solution)/shard_map/ppermute | solution.py:453
  55.5 16.2 %collective-permute-start.15 = (bf16[2,256,128]{2,1,0:T(8,128)(2,1)S(1)}, bf16[2,256,128]{2,1,0:T(8,128)(2,1)S(1)}, u32[]{:S(2)}, u32[]{:S(2)}) collective-permute-start(bf16[2,256,128]{2,1,0:T(8,128)(2,1)S(1)} %get-tuple-element.49), channel_id=1, source_target_pairs={{0,4},{1,5},{2,6},{3,7},{4,0},{5,1},{6,2},{7,3},{8,12},{9,13},{10,... | collective-permute-start | bytes 393224 | tf_op jit(solution)/shard_map/ppermute | solution.py:453
  58.5 13.3 %collective-permute-start.16 = (bf16[2,256,128]{2,1,0:T(8,128)(2,1)S(1)}, bf16[2,256,128]{2,1,0:T(8,128)(2,1)S(1)}, u32[]{:S(2)}, u32[]{:S(2)}) collective-permute-start(bf16[2,256,128]{2,1,0:T(8,128)(2,1)S(1)} %get-tuple-element.50), channel_id=1, source_target_pairs={{0,6},{1,7},{2,4},{3,5},{4,2},{5,3},{6,0},{7,1},{8,14},{9,15},{10,... | collective-permute-start | bytes 393224 | tf_op jit(solution)/shard_map/ppermute | solution.py:453
  64.8 11.2 %collective-permute-start.27 = (f32[2,32,128]{2,1,0:T(8,128)S(1)}, f32[2,32,128]{2,1,0:T(8,128)S(1)}, u32[]{:S(2)}, u32[]{:S(2)}) collective-permute-start(f32[2,32,128]{2,1,0:T(8,128)S(1)} %add_add_fusion.1), channel_id=1, source_target_pairs={{0,6},{1,7},{2,4},{3,5},{4,2},{5,3},{6,0},{7,1},{8,14},{9,15},{10,... | collective-permute-start | bytes 98312 | tf_op jit(solution)/shard_map/ppermute | solution.py:383
  71.7 4.9 %collective-permute-start.26 = (f32[2,32,128]{2,1,0:T(8,128)S(1)}, f32[2,32,128]{2,1,0:T(8,128)S(1)}, u32[]{:S(2)}, u32[]{:S(2)}) collective-permute-start(f32[2,32,128]{2,1,0:T(8,128)S(1)} %add_add_fusion.1), channel_id=1, source_target_pairs={{0,4},{1,5},{2,6},{3,7},{4,0},{5,1},{6,2},{7,3},{8,12},{9,13},{10,... | collective-permute-start | bytes 98312 | tf_op jit(solution)/shard_map/ppermute | solution.py:383
  71.7 5.0 %collective-permute-start.25 = (f32[2,32,128]{2,1,0:T(8,128)S(1)}, f32[2,32,128]{2,1,0:T(8,128)S(1)}, u32[]{:S(2)}, u32[]{:S(2)}) collective-permute-start(f32[2,32,128]{2,1,0:T(8,128)S(1)} %add_add_fusion.1), channel_id=1, source_target_pairs={{0,2},{1,3},{2,0},{3,1},{4,6},{5,7},{6,4},{7,5},{8,10},{9,11},{10,... | collective-permute-start | bytes 98312 | tf_op jit(solution)/shard_map/ppermute | solution.py:383
  76.0 2.4 %collective-permute-start.28 = (bf16[256,128]{1,0:T(8,128)(2,1)S(1)}, bf16[256,128]{1,0:T(8,128)(2,1)S(1)}, u32[]{:S(2)}, u32[]{:S(2)}) collective-permute-start(bf16[256,128]{1,0:T(8,128)(2,1)S(1)} %get-tuple-element.65), channel_id=1, source_target_pairs={{0,1},{1,0},{2,3},{3,2},{4,5},{5,4},{6,7},{7,6},{8,9},{9,8},{10,11... | collective-permute-start | bytes 196616 | tf_op jit(solution)/shard_map/ppermute | solution.py:465
  76.0 1.4 %collective-permute-start.17 = (bf16[256,128]{1,0:T(8,128)(2,1)S(1)}, bf16[256,128]{1,0:T(8,128)(2,1)S(1)}, u32[]{:S(2)}, u32[]{:S(2)}) collective-permute-start(bf16[256,128]{1,0:T(8,128)(2,1)S(1)} %get-tuple-element.51), channel_id=1, source_target_pairs={{0,1},{1,0},{2,3},{3,2},{4,5},{5,4},{6,7},{7,6},{8,9},{9,8},{10,11... | collective-permute-start | bytes 196616 | tf_op jit(solution)/shard_map/ppermute | solution.py:465
